TPU v7x, 32 devices: a whole 2x2x4 slice. The times are simulated.
32 devices in a mesh: tower: 2 (over x), dp: 4 (over y, core), mp: 4 (over z).
Axes of the slice: x: 2, y: 2, z: 4, core: 2. Of those that a mesh axis runs over, the one named last changes fastest.
Arguments:
- tower_in: bfloat16 [2, 4608, 768], P('tower', ('dp', 'mp')), may hold values from -6 to 6
- out_cot: bfloat16 [2, 4608, 768], P('tower', ('dp', 'mp')), may hold values from -6 to 6
- segment_ids: int32 [72, 64], P('dp'), may hold values from 0 to 3, never falling along the last dimension, each value on 1 to 32 neighbouring positions
- row_image: int32 [72], P('dp'), may hold values from 0 to 1
- attn_qkv: bfloat16 [2, 3, 768, 768], P('tower', None, None, 'mp'), may hold values from -0.21875 to 0.21875
- attn_out: bfloat16 [2, 768, 768], P('tower', 'mp'), may hold values from -0.625 to 0.625
- mlp_in: bfloat16 [2, 768, 3072], P('tower', None, 'mp'), may hold values from -0.21875 to 0.21875
- mlp_out: bfloat16 [2, 3072, 768], P('tower', 'mp'), may hold values from -0.109375 to 0.109375
- cross_proj: bfloat16 [2, 2, 768, 768], P('tower', None, None, 'mp'), may hold values from -0.3125 to 0.3125
- qv_bias: float32 [2, 2, 768], P('tower'), may hold values from -3 to 3
- out_bias: float32 [2, 768], P('tower'), may hold values from -1.75 to 1.75
- mlp_bias_in: float32 [2, 3072], P('tower'), may hold values from -3 to 3
- mlp_bias_out: float32 [2, 768], P('tower'), may hold values from -1.75 to 1.75
- norm_gain: float32 [2, 3, 768], P('tower'), may hold values from 0.25 to 1.75
- norm_bias: float32 [2, 3, 768], P('tower'), may hold values from -1.75 to 1.75
Outputs:
- tower_out: bfloat16 [2, 4608, 768], P('tower', ('dp', 'mp'))
- tower_in_grad: bfloat16 [2, 4608, 768], P('tower', ('dp', 'mp'))
- qkv_grad: float32 [2, 3, 768, 768], P('tower', None, 'dp', 'mp')
- attn_out_grad: float32 [2, 768, 768], P('tower', 'mp', 'dp')
- mlp_in_grad: float32 [2, 768, 3072], P('tower', 'dp', 'mp')
- mlp_out_grad: float32 [2, 3072, 768], P('tower', 'mp', 'dp')
- cross_grad: float32 [2, 2, 768, 768], P('tower', None, 'dp', 'mp')
- qv_bias_grad: float32 [2, 2, 768], P('tower')
- out_bias_grad: float32 [2, 768], P('tower')
- mlp_bias_in_grad: float32 [2, 3072], P('tower')
- mlp_bias_out_grad: float32 [2, 768], P('tower')
- norm_gain_grad: float32 [2, 3, 768], P('tower')
- norm_bias_grad: float32 [2, 3, 768], P('tower')
Inputs may be any that keep to these rules, and one draw needn't show every extreme that they name: `segment_ids`: within a caption row of 64 tokens the numbers never fall. Row r and image i belong to one group where r // 18 == i // 2; row_image counts images within the group.
All inputs are finite; a program needn't handle non-finite values.
Results may differ from a plain program's by a relative error of at most 0.03.
Values may be sent and summed in bfloat16 or wider, within the bound.
A program may use at most 192 MiB of HBM per device.

v0:
```python
import jax
import jax.numpy as jnp
from jax import lax
from jax.sharding import PartitionSpec as P

HDIM = 64
PATCH = 576
LTXT = 64


EPS = 1e-06
NEG = -1e30
HIGH = lax.Precision.HIGHEST


def passed_along(x, axis, by):
    devices = lax.axis_size(axis)
    pairs = [(i, i + by) for i in range(devices) if 0 <= i + by < devices]
    return lax.ppermute(x, axis, pairs)


def norm_rows(values, gain_vec, shift_vec):
    center = values - jnp.mean(values, axis=-1, keepdims=True)
    spread = jnp.mean(center * center, axis=-1, keepdims=True)
    return center * lax.rsqrt(spread + EPS) * gain_vec + shift_vec


def gelu_tanh(values):
    return jax.nn.gelu(values, approximate=True)


def norm_back(values, gain_vec, shift_vec, grad_normed):
    _, pullback = jax.vjp(norm_rows, values, gain_vec, shift_vec)
    return pullback(grad_normed)


def gated_run(active, compute, operands):

    def spare_run(inputs):
        return jax.tree.map(jnp.zeros_like, compute(inputs))

    return lax.cond(active, compute, spare_run, operands)


def widen_rows(rows_low):
    return lax.all_gather(rows_low, "mp", axis=0, tiled=True)


def combine(partial_rows):
    return lax.psum_scatter(
        partial_rows.astype(jnp.bfloat16), "mp", scatter_dimension=0, tiled=True
    ).astype(jnp.float32)


def masked_scores(queries, key_rows, allowed, scale_qk):
    scores = (
        jnp.einsum("bqhe,bkhe->bhqk", queries, key_rows, preferred_element_type=jnp.float32)
        * scale_qk
    )
    if allowed is None:
        return scores
    return jnp.where(allowed[:, None], scores, NEG)


def attend(queries, key_rows, value_rows, allowed, scale_qk):
    scores = masked_scores(queries, key_rows, allowed, scale_qk)
    row_top = jnp.max(scores, axis=-1, keepdims=True)
    log_total = row_top + jnp.log(jnp.sum(jnp.exp(scores - row_top), axis=-1, keepdims=True))
    weights_low = jnp.exp(scores - log_total).astype(jnp.bfloat16)
    mixed_rows = jnp.einsum(
        "bhqk,bkhe->bqhe", weights_low, value_rows, preferred_element_type=jnp.float32
    )
    return (mixed_rows.astype(jnp.bfloat16), log_total)


def attend_back(queries, key_rows, value_rows, allowed, log_total, grad_mixed, scale_qk):
    scores = masked_scores(queries, key_rows, allowed, scale_qk)
    weights_f = jnp.exp(scores - log_total)
    grad_weights = jnp.einsum(
        "bqhe,bkhe->bhqk", grad_mixed, value_rows, preferred_element_type=jnp.float32
    )
    row_dot = jnp.sum(weights_f * grad_weights, axis=-1, keepdims=True)
    grad_scores = (weights_f * (grad_weights - row_dot)).astype(jnp.bfloat16)
    grad_query = (
        jnp.einsum("bhqk,bkhe->bqhe", grad_scores, key_rows, preferred_element_type=jnp.float32)
        * scale_qk
    )
    grad_key = (
        jnp.einsum("bhqk,bqhe->bkhe", grad_scores, queries, preferred_element_type=jnp.float32)
        * scale_qk
    )
    grad_value = jnp.einsum(
        "bhqk,bqhe->bkhe",
        weights_f.astype(jnp.bfloat16),
        grad_mixed,
        preferred_element_type=jnp.float32,
    )
    return (grad_query, grad_key, grad_value)


def cross_attention(query_rows, image_keys, image_vals, row_picks, scale_qk):

    def one_block(block_items):
        q_blk, pick_blk = block_items
        key_pick = jnp.take(image_keys, pick_blk, axis=0)
        val_pick = jnp.take(image_vals, pick_blk, axis=0)
        return attend(q_blk, key_pick, val_pick, None, scale_qk)

    return lax.map(one_block, (query_rows, row_picks))


def cross_attention_back(
    query_rows, image_keys, image_vals, row_picks, log_total, grad_mixed, scale_qk
):
    images = image_keys.shape[0]

    def one_block(block_items):
        q_blk, pick_blk, total_blk, grad_blk = block_items
        key_pick = jnp.take(image_keys, pick_blk, axis=0)
        val_pick = jnp.take(image_vals, pick_blk, axis=0)
        grad_query, grad_key, grad_value = attend_back(
            q_blk, key_pick, val_pick, None, total_blk, grad_blk, scale_qk
        )
        chooser = (pick_blk[:, None] == jnp.arange(images, dtype=jnp.int32)[None, :]).astype(
            jnp.float32
        )
        key_sum = jnp.einsum("ri,rkhe->ikhe", chooser, grad_key, precision=HIGH)
        val_sum = jnp.einsum("ri,rkhe->ikhe", chooser, grad_value, precision=HIGH)
        return (grad_query, key_sum, val_sum)

    grad_query, key_sum, val_sum = lax.map(
        one_block, (query_rows, row_picks, log_total, grad_mixed)
    )
    return (grad_query, jnp.sum(key_sum, axis=0), jnp.sum(val_sum, axis=0))


def body(
    tower_in,
    out_cot,
    segment_ids,
    row_image,
    attn_qkv,
    attn_out,
    mlp_in,
    mlp_out,
    cross_proj,
    qv_bias,
    out_bias,
    mlp_bias_in,
    mlp_bias_out,
    norm_gain,
    norm_bias,
):
    is_enc = lax.axis_index("tower") == 0
    is_dec = jnp.logical_not(is_enc)
    mp_index = lax.axis_index("mp")
    weight_qkv = attn_qkv[0]
    weight_out = attn_out[0]
    weight_in = mlp_in[0]
    weight_mlp = mlp_out[0]
    weight_cross = cross_proj[0]
    width = tower_in.shape[2]
    head_cols = weight_qkv.shape[2]
    hidden_cols = weight_in.shape[1]
    heads_here = head_cols // HDIM
    scale_qk = HDIM ** (-0.5)
    bias_qv = lax.dynamic_slice_in_dim(qv_bias[0], mp_index * head_cols, head_cols, 1)
    bias_in = lax.dynamic_slice_in_dim(mlp_bias_in[0], mp_index * hidden_cols, hidden_cols, 0)
    bias_out = out_bias[0]
    bias_mlp = mlp_bias_out[0]
    gains = norm_gain[0]
    shifts = norm_bias[0]
    row_count = segment_ids.shape[0]
    blocks = row_count * LTXT // PATCH
    tokens = blocks * PATCH
    per_block = PATCH // LTXT

    def shaped(flat_rows):
        return flat_rows.reshape(blocks, PATCH, heads_here, HDIM)

    def row_shaped(flat_rows):
        return flat_rows.reshape(blocks, per_block, LTXT, heads_here, HDIM)

    places = jnp.arange(LTXT)
    earlier = places[None, :] <= places[:, None]
    seg_rows = segment_ids.reshape(blocks, per_block, LTXT)
    row_masks = jnp.logical_and(
        earlier[None, None], seg_rows[:, :, :, None] == seg_rows[:, :, None, :]
    )
    row_picks = row_image.reshape(blocks, per_block)

    def enc_self(items):
        q_all, k_all, v_all = items

        def one_block(block_items):
            q_blk, k_blk, v_blk = block_items
            mixed_blk, total_blk = attend(q_blk[None], k_blk[None], v_blk[None], None, scale_qk)
            return (mixed_blk[0], total_blk[0])

        mixed_rows, log_total = lax.map(one_block, (shaped(q_all), shaped(k_all), shaped(v_all)))
        return (mixed_rows.reshape(tokens, head_cols), log_total.reshape(blocks, -1))

    def dec_self(items):
        q_all, k_all, v_all = items

        def one_block(block_items):
            q_blk, k_blk, v_blk, mask_blk = block_items
            return attend(q_blk, k_blk, v_blk, mask_blk, scale_qk)

        mixed_rows, log_total = lax.map(
            one_block, (row_shaped(q_all), row_shaped(k_all), row_shaped(v_all), row_masks)
        )
        return (mixed_rows.reshape(tokens, head_cols), log_total.reshape(blocks, -1))

    def enc_self_back(items):
        q_all, k_all, v_all, total_all, grad_all = items

        def one_block(block_items):
            q_blk, k_blk, v_blk, total_blk, grad_blk = block_items
            grad_query, grad_key, grad_value = attend_back(
                q_blk[None],
                k_blk[None],
                v_blk[None],
                None,
                total_blk.reshape(1, heads_here, PATCH, 1),
                grad_blk[None],
                scale_qk,
            )
            return (grad_query[0], grad_key[0], grad_value[0])

        grads = lax.map(
            one_block, (shaped(q_all), shaped(k_all), shaped(v_all), total_all, shaped(grad_all))
        )
        return tuple((piece.reshape(tokens, head_cols) for piece in grads))

    def dec_self_back(items):
        q_all, k_all, v_all, total_all, grad_all = items

        def one_block(block_items):
            q_blk, k_blk, v_blk, mask_blk, total_blk, grad_blk = block_items
            return attend_back(
                q_blk,
                k_blk,
                v_blk,
                mask_blk,
                total_blk.reshape(per_block, heads_here, LTXT, 1),
                grad_blk,
                scale_qk,
            )

        grads = lax.map(
            one_block,
            (
                row_shaped(q_all),
                row_shaped(k_all),
                row_shaped(v_all),
                row_masks,
                total_all,
                row_shaped(grad_all),
            ),
        )
        return tuple((piece.reshape(tokens, head_cols) for piece in grads))

    stream = tower_in[0].astype(jnp.float32)
    act_one = widen_rows(norm_rows(stream, gains[0], shifts[0]).astype(jnp.bfloat16))
    projected = jnp.einsum("td,cdm->ctm", act_one, weight_qkv, preferred_element_type=jnp.float32)
    queries = (projected[0] + bias_qv[0]).astype(jnp.bfloat16)
    key_rows = projected[1].astype(jnp.bfloat16)
    value_rows = (projected[2] + bias_qv[1]).astype(jnp.bfloat16)
    flat_self, total_self = lax.cond(is_enc, enc_self, dec_self, (queries, key_rows, value_rows))
    stream_one = (
        stream
        + combine(jnp.dot(flat_self, weight_out, preferred_element_type=jnp.float32))
        + bias_out
    )

    def feed_forward(inputs):
        pre_act = jnp.dot(inputs, weight_in, preferred_element_type=jnp.float32) + bias_in
        hidden = gelu_tanh(pre_act).astype(jnp.bfloat16)
        return (jnp.dot(hidden, weight_mlp, preferred_element_type=jnp.float32), pre_act, hidden)

    act_enc = widen_rows(norm_rows(stream_one, gains[1], shifts[1]).astype(jnp.bfloat16))
    part_enc, pre_enc, hidden_enc = gated_run(is_enc, feed_forward, act_enc)
    out_enc = stream_one + combine(part_enc) + bias_mlp
    base_three = jnp.where(is_enc, out_enc, stream_one)
    act_three = widen_rows(norm_rows(base_three, gains[2], shifts[2]).astype(jnp.bfloat16))

    def image_side(inputs):
        return jnp.einsum(
            "td,cdm->ctm", inputs, weight_cross, preferred_element_type=jnp.float32
        ).astype(jnp.bfloat16)

    def text_side(inputs):
        return jnp.dot(inputs, weight_cross[0], preferred_element_type=jnp.float32).astype(
            jnp.bfloat16
        )

    image_pair = gated_run(is_enc, image_side, act_three)
    cross_query = gated_run(is_dec, text_side, act_three)
    image_recv = passed_along(image_pair, "tower", 1)
    image_keys = shaped(image_recv[0])
    image_vals = shaped(image_recv[1])

    def cross_forward(inputs):
        mixed_rows, log_total = cross_attention(
            row_shaped(inputs), image_keys, image_vals, row_picks, scale_qk
        )
        flat_mix = mixed_rows.reshape(tokens, head_cols)
        return (
            jnp.einsum("tm,dm->td", flat_mix, weight_cross[1], preferred_element_type=jnp.float32),
            flat_mix,
            log_total,
        )

    part_cross, flat_cross, total_cross = gated_run(is_dec, cross_forward, cross_query)
    stream_two = stream_one + combine(part_cross)
    act_dec = widen_rows(norm_rows(stream_two, gains[1], shifts[1]).astype(jnp.bfloat16))
    part_dec, pre_dec, hidden_dec = gated_run(is_dec, feed_forward, act_dec)
    out_dec = stream_two + combine(part_dec) + bias_mlp
    tower_out = jnp.where(is_enc, out_enc, out_dec).astype(jnp.bfloat16)

    def ffn_back(inputs):
        grad_wide, act_two, pre_act, hidden = inputs
        g_mlp = jnp.einsum("tf,td->fd", hidden, grad_wide, preferred_element_type=jnp.float32)
        grad_hidden = jnp.einsum(
            "td,fd->tf", grad_wide, weight_mlp, preferred_element_type=jnp.float32
        )
        _, pullback = jax.vjp(gelu_tanh, pre_act)
        grad_pre = pullback(grad_hidden)[0].astype(jnp.bfloat16)
        g_in = jnp.einsum("td,tf->df", act_two, grad_pre, preferred_element_type=jnp.float32)
        g_bias_in = jnp.sum(grad_pre, axis=0, dtype=jnp.float32)
        partial_rows = jnp.einsum(
            "tf,df->td", grad_pre, weight_in, preferred_element_type=jnp.float32
        )
        return (partial_rows, g_in, g_mlp, g_bias_in)

    grad_out = out_cot[0].astype(jnp.float32)
    grad_low = grad_out.astype(jnp.bfloat16)
    wide_dec = widen_rows(grad_low)
    part_a, g_in_dec, g_mlp_dec, g_bin_dec = gated_run(
        is_dec, ffn_back, (wide_dec, act_dec, pre_dec, hidden_dec)
    )
    back_a, gain_a, shift_a = norm_back(stream_two, gains[1], shifts[1], combine(part_a))
    grad_two = grad_out + back_a
    wide_cross = widen_rows(grad_two.astype(jnp.bfloat16))

    def cross_back(inputs):
        g_outw = jnp.einsum("td,tm->dm", inputs, flat_cross, preferred_element_type=jnp.float32)
        grad_mix = jnp.einsum(
            "td,dm->tm", inputs, weight_cross[1], preferred_element_type=jnp.float32
        ).astype(jnp.bfloat16)
        grad_query, key_sum, val_sum = cross_attention_back(
            row_shaped(cross_query),
            image_keys,
            image_vals,
            row_picks,
            total_cross,
            row_shaped(grad_mix),
            scale_qk,
        )
        grad_query = grad_query.reshape(tokens, head_cols).astype(jnp.bfloat16)
        pair_grad = jnp.stack(
            [key_sum.reshape(tokens, head_cols), val_sum.reshape(tokens, head_cols)]
        ).astype(jnp.bfloat16)
        g_query_w = jnp.einsum(
            "td,tm->dm", act_three, grad_query, preferred_element_type=jnp.float32
        )
        partial_rows = jnp.einsum(
            "tm,dm->td", grad_query, weight_cross[0], preferred_element_type=jnp.float32
        )
        return (pair_grad, jnp.stack([g_query_w, g_outw]), partial_rows)

    pair_grad, g_cross_dec, part_query = gated_run(is_dec, cross_back, wide_cross)
    pair_recv = passed_along(pair_grad, "tower", -1)

    def image_back(inputs):
        g_pair = jnp.einsum("td,ctm->cdm", act_three, inputs, preferred_element_type=jnp.float32)
        partial_rows = jnp.einsum(
            "ctm,cdm->td", inputs, weight_cross, preferred_element_type=jnp.float32
        )
        return (g_pair, partial_rows)

    g_cross_enc, part_pair = gated_run(is_enc, image_back, pair_recv)
    back_three, gain_three, shift_three = norm_back(
        base_three, gains[2], shifts[2], combine(part_query + part_pair)
    )
    grad_enc = grad_out + back_three
    grad_one_dec = grad_two + back_three
    grad_enc_low = grad_enc.astype(jnp.bfloat16)
    wide_enc = widen_rows(grad_enc_low)
    part_b, g_in_enc, g_mlp_enc, g_bin_enc = gated_run(
        is_enc, ffn_back, (wide_enc, act_enc, pre_enc, hidden_enc)
    )
    back_b, gain_b, shift_b = norm_back(stream_one, gains[1], shifts[1], combine(part_b))
    grad_one = jnp.where(is_enc, grad_enc + back_b, grad_one_dec)
    g_in_total = g_in_dec + g_in_enc
    g_mlp_total = g_mlp_dec + g_mlp_enc
    grad_one_low = grad_one.astype(jnp.bfloat16)
    wide_one = widen_rows(grad_one_low)
    g_out = jnp.einsum("tm,td->md", flat_self, wide_one, preferred_element_type=jnp.float32)
    grad_mix_self = jnp.einsum(
        "td,md->tm", wide_one, weight_out, preferred_element_type=jnp.float32
    ).astype(jnp.bfloat16)
    grad_q, grad_k, grad_v = lax.cond(
        is_enc,
        enc_self_back,
        dec_self_back,
        (queries, key_rows, value_rows, total_self, grad_mix_self),
    )
    grad_proj = jnp.stack([grad_q, grad_k, grad_v]).astype(jnp.bfloat16)
    g_qkv = jnp.einsum("td,ctm->cdm", act_one, grad_proj, preferred_element_type=jnp.float32)
    g_bias_q = jnp.sum(grad_proj[0], axis=0, dtype=jnp.float32)
    g_bias_v = jnp.sum(grad_proj[2], axis=0, dtype=jnp.float32)
    part_one = jnp.einsum("ctm,cdm->td", grad_proj, weight_qkv, preferred_element_type=jnp.float32)
    back_one, gain_one, shift_one = norm_back(stream, gains[0], shifts[0], combine(part_one))
    grad_in = (grad_one + back_one).astype(jnp.bfloat16)
    g_cross = g_cross_dec + g_cross_enc
    zero_index = mp_index * 0
    full_qv = lax.dynamic_update_slice(
        jnp.zeros((2, width), jnp.float32),
        jnp.stack([g_bias_q, g_bias_v]),
        (zero_index, mp_index * head_cols),
    )
    full_in = lax.dynamic_update_slice(
        jnp.zeros((mlp_bias_in.shape[1],), jnp.float32),
        g_bin_dec + g_bin_enc,
        (mp_index * hidden_cols,),
    )
    g_bias_out = jnp.sum(grad_one_low, axis=0, dtype=jnp.float32)
    g_bias_mlp = jnp.where(
        is_enc,
        jnp.sum(grad_enc_low, axis=0, dtype=jnp.float32),
        jnp.sum(grad_low, axis=0, dtype=jnp.float32),
    )
    g_gain = jnp.stack([gain_one, gain_a + gain_b, gain_three])
    g_shift = jnp.stack([shift_one, shift_a + shift_b, shift_three])
    smalls = lax.psum(
        (
            full_qv[None],
            g_bias_out[None],
            full_in[None],
            g_bias_mlp[None],
            g_gain[None],
            g_shift[None],
        ),
        ("dp", "mp"),
    )
    qkv_grad, attn_out_grad, mlp_in_grad, mlp_out_grad, cross_grad = (
        lax.psum_scatter(
            g_qkv[None].astype(jnp.bfloat16), "dp", scatter_dimension=2, tiled=True
        ).astype(jnp.float32),
        lax.psum_scatter(
            g_out[None].astype(jnp.bfloat16), "dp", scatter_dimension=2, tiled=True
        ).astype(jnp.float32),
        lax.psum_scatter(
            g_in_total[None].astype(jnp.bfloat16), "dp", scatter_dimension=1, tiled=True
        ).astype(jnp.float32),
        lax.psum_scatter(
            g_mlp_total[None].astype(jnp.bfloat16), "dp", scatter_dimension=2, tiled=True
        ).astype(jnp.float32),
        lax.psum_scatter(
            g_cross[None].astype(jnp.bfloat16), "dp", scatter_dimension=2, tiled=True
        ).astype(jnp.float32),
    )
    return (
        tower_out[None],
        grad_in[None],
        qkv_grad,
        attn_out_grad,
        mlp_in_grad,
        mlp_out_grad,
        cross_grad,
        smalls[0],
        smalls[1],
        smalls[2],
        smalls[3],
        smalls[4],
        smalls[5],
    )


def solution(mesh):
    return jax.shard_map(
        body,
        mesh=mesh,
        in_specs=(
            P("tower", ("dp", "mp"), None),
            P("tower", ("dp", "mp"), None),
            P("dp", None),
            P("dp"),
            P("tower", None, None, "mp"),
            P("tower", "mp", None),
            P("tower", None, "mp"),
            P("tower", "mp", None),
            P("tower", None, None, "mp"),
            P("tower", None, None),
            P("tower", None),
            P("tower", None),
            P("tower", None),
            P("tower", None, None),
            P("tower", None, None),
        ),
        out_specs=(
            P("tower", ("dp", "mp"), None),
            P("tower", ("dp", "mp"), None),
            P("tower", None, "dp", "mp"),
            P("tower", "mp", "dp"),
            P("tower", "dp", "mp"),
            P("tower", "mp", "dp"),
            P("tower", None, "dp", "mp"),
            P("tower", None, None),
            P("tower", None),
            P("tower", None),
            P("tower", None),
            P("tower", None, None),
            P("tower", None, None),
        ),
        check_vma=False,
    )
```

profile of v0, /device:TPU:11, one launch (start us, length us, event | category | flops | bytes accessed | tf_op | source)
XLA Modules:
  0.0 1240.0 jit_solution(6260435258188161629)
XLA Ops:
  16.3 37.7 %all-gather.10.cloned.1.call-done = bf16[1152,768]{1,0:T(8,128)(2,1)} async-done(((bf16[288,768]{1,0:T(8,128)(2,1)}), bf16[1152,768]{1,0:T(8,128)(2,1)}) %all-gather.10.cloned.1.call-update) | async-done | bytes 1769488 | tf_op jit(solution)/shard_map/all_gather | solution.py:46
  58.8 23.0 %conditional.11 = (bf16[1152,192]{1,0:T(8,128)(2,1)S(1)}, f32[2,1728]{1,0:T(2,128)S(1)}) conditional(s32[]{:T(128)} %convert_element_type.269, (bf16[1152,192]{0,1:T(8,128)(2,1)}, bf16[1152,192]{0,1:T(8,128)(2,1)}, bf16[1152,192]{0,1:T(8,128)(2,1)}, pred[2,9,64,64]{2,3,1,0:T(8,128)(4,1)}) %tuple.123, (bf16[1152,192]{0,1:T(8,128)(2,1)}, ...), branch_computations={%region_2.7_spmd, %region_7.12_spmd} | conditional | flops 262875456 | bytes 21433768 | solution.py:270
  71.3 6.3 while.74
  85.0 36.9 %reduce-scatter.20.cloned.1.call-done = bf16[288,768]{1,0:T(8,128)(2,1)} async-done(((bf16[1152,768]{1,0:T(8,128)(2,1)}), bf16[288,768]{1,0:T(8,128)(2,1)}) %reduce-scatter.20.cloned.1.call-update) | async-done | bytes 442384 | tf_op jit(solution)/shard_map/reduce_scatter | solution.py:50
  127.3 39.3 %all-gather.12.cloned.1.call-done = bf16[1152,768]{1,0:T(8,128)(2,1)} async-done(((bf16[288,768]{1,0:T(8,128)(2,1)}), bf16[1152,768]{1,0:T(8,128)(2,1)}) %all-gather.12.cloned.1.call-update) | async-done | bytes 1769488 | tf_op jit(solution)/shard_map/all_gather | solution.py:46
  175.7 42.4 %reduce-scatter.22.cloned.1.call-done = bf16[288,768]{1,0:T(8,128)(2,1)} async-done(((bf16[1152,768]{1,0:T(8,128)(2,1)}), bf16[288,768]{1,0:T(8,128)(2,1)}) %reduce-scatter.22.cloned.1.call-update) | async-done | bytes 442384 | tf_op jit(solution)/shard_map/reduce_scatter | solution.py:50
  221.5 40.0 %all-gather.14.cloned.1.call-done = bf16[1152,768]{1,0:T(8,128)(2,1)} async-done(((bf16[288,768]{1,0:T(8,128)(2,1)}), bf16[1152,768]{1,0:T(8,128)(2,1)}) %all-gather.14.cloned.1.call-update) | async-done | bytes 1769488 | tf_op jit(solution)/shard_map/all_gather | solution.py:46
  266.6 19.5 %collective-permute-done = bf16[2,1152,192]{1,2,0:T(8,128)(2,1)} collective-permute-done((bf16[2,1152,192]{1,2,0:T(8,128)(2,1)}, bf16[2,1152,192]{1,2,0:T(8,128)(2,1)}, u32[]{:S(2)}, u32[]{:S(2)}) %collective-permute-start) | collective-permute-done | bytes 884768 | tf_op jit(solution)/shard_map/ppermute | solution.py:19
  289.8 78.4 %conditional.15 = (bf16[1152,768]{1,0:T(8,128)(2,1)}, bf16[1152,192]{1,0:T(8,128)(2,1)}, f32[2,9,3,64,1]{3,2,1,4,0:T(4,128)}) conditional(s32[]{:T(128)} %convert_element_type.279, () %tuple.127, (bf16[1152,192]{0,1:T(8,128)(2,1)S(1)}, s32[2,9]{1,0:T(2,128)S(1)}, bf16[2,576,3,64]{1,0,3,2:T(2,128)(2,1)}, bf16[2,576,3,64]{1,0,3,2:T(2,128)(2,1)}, ...), branch_computations={%region_24.25_spmd, %region_25.31_spmd} | conditional | flops 604605824 | bytes 58426396 | solution.py:42
  291.0 3.7 copy.400
  294.8 3.7 copy.399
  304.2 56.7 %while.76 = (s32[]{:T(128)}, bf16[2,9,64,3,64]{2,4,3,1,0:T(8,128)(2,1)}, f32[2,9,3,64,1]{3,2,1,4,0:T(4,128)}, s32[2,9]{1,0:T(2,128)S(1)}, bf16[2,576,3,64]{3,2,1...) while((s32[]{:T(128)}, ...), condition=%wide.region_29.30_spmd, body=%wide.region_26.29_spmd.sunk | while | flops 264867200 | bytes 45204356 | solution.py:109
  304.3 7.2 gather_fusion.3
  311.4 7.2 gather_fusion.2
  318.6 7.8 broadcast_select_fusion.8
  332.6 7.2 gather_fusion.3
  339.8 7.2 gather_fusion.2
  347.0 7.8 broadcast_select_fusion.8
  368.4 38.3 %reduce-scatter.24.cloned.1.call-done = bf16[288,768]{1,0:T(8,128)(2,1)} async-done(((bf16[1152,768]{1,0:T(8,128)(2,1)}), bf16[288,768]{1,0:T(8,128)(2,1)}) %reduce-scatter.24.cloned.1.call-update) | async-done | bytes 442384 | tf_op jit(solution)/shard_map/reduce_scatter | solution.py:50
  410.3 39.2 %all-gather.16.cloned.1.call-done = bf16[1152,768]{1,0:T(8,128)(2,1)} async-done(((bf16[288,768]{1,0:T(8,128)(2,1)}), bf16[1152,768]{1,0:T(8,128)(2,1)}) %all-gather.16.cloned.1.call-update) | async-done | bytes 1769488 | tf_op jit(solution)/shard_map/all_gather | solution.py:46
  449.5 10.8 conditional.16
  449.5 6.0 fusion.45
  455.5 4.8 fusion.273
  460.3 30.1 %all-gather.24.cloned.1.call-done = bf16[1,1152,768]{2,1,0:T(8,128)(2,1)} async-done(((bf16[1,288,768]{2,1,0:T(8,128)(2,1)}), bf16[1,1152,768]{2,1,0:T(8,128)(2,1)}) %all-gather.24.cloned.1.call-update) | async-done | bytes 1769488 | tf_op jit(solution)/shard_map/all_gather | solution.py:46
  490.4 17.3 %conditional.17 = (bf16[1152,768]{1,0:T(8,128)(2,1)}, f32[768,768]{0,1:T(8,128)}, f32[768]{0:T(1024)S(1)}, f32[768,768]{0,1:T(8,128)}) conditional(s32[]{:T(128)} %convert_element_type.279, () %tuple.135, (bf16[1152,768]{1,0:T(8,128)(2,1)}, bf16[768,768]{1,0:T(8,128)(2,1)}, f32[1152,768]{1,0:T(8,128)}, bf16[768,768]{1,0:T(8,128)(2,1)S(1)}, ...), branch_computations={%region_36.38_spmd, %region_37.40_spmd} | conditional | flops 5455281152 | bytes 38931544 | solution.py:42
  490.6 6.3 convert_reduce_fusion
  496.9 4.8 fusion.275
  507.8 36.9 %reduce-scatter.28.cloned.1.call-done = bf16[288,768]{1,0:T(8,128)(2,1)} async-done(((bf16[1152,768]{1,0:T(8,128)(2,1)}), bf16[288,768]{1,0:T(8,128)(2,1)}) %reduce-scatter.28.cloned.1.call-update) | async-done | bytes 442384 | tf_op jit(solution)/shard_map/reduce_scatter | solution.py:50
  550.2 40.0 %all-gather.18.cloned.1.call-done = bf16[1152,768]{1,0:T(8,128)(2,1)} async-done(((bf16[288,768]{1,0:T(8,128)(2,1)}), bf16[1152,768]{1,0:T(8,128)(2,1)}) %all-gather.18.cloned.1.call-update) | async-done | bytes 1769488 | tf_op jit(solution)/shard_map/all_gather | solution.py:46
  590.2 157.7 %conditional.18 = (bf16[2,1152,192]{1,2,0:T(8,128)(2,1)}, f32[2,768,192]{1,2,0:T(8,128)S(1)}, f32[1152,768]{1,0:T(8,128)S(1)}) conditional(s32[]{:T(128)} %convert_element_type.279, () %tuple.134, (bf16[1152,192]{0,1:T(8,128)(2,1)}, bf16[2,768,192]{1,2,0:T(8,128)(2,1)S(1)}, bf16[1152,768]{1,0:T(8,128)(2,1)}, s32[2,9]{1,0:T(2,128)}, ...), branch_computations={%region_42.44_spmd, %region_43.50_spmd} | conditional | flops 2060180864 | bytes 178671584 | solution.py:42
  602.8 3.7 copy.404
  612.3 119.7 %while.77 = (s32[]{:T(128)}, bf16[2,9,64,3,64]{2,4,3,1,0:T(8,128)(2,1)}, f32[2,2,576,3,64]{2,1,4,3,0:T(2,128)}, f32[2,2,576,3,64]{2,1,4,3,0:T(2,128)}, s32[2,9]{...) while((s32[]{:T(128)}, ...), condition=%wide.region_46.47_spmd, body=%wide.region_44.46_spmd.sunk | while | flops 699825536 | bytes 133205432 | solution.py:131
  613.0 7.2 gather_fusion.1
  620.2 7.2 gather_fusion
  627.4 12.1 broadcast_select_fusion.7
  639.5 7.8 copy.534
  657.9 5.2 fusion.419
  665.5 5.3 fusion.417
  672.8 7.2 gather_fusion.1
  680.0 7.2 gather_fusion
  687.2 12.1 broadcast_select_fusion.7
  699.3 7.8 copy.534
  717.7 5.2 fusion.419
  725.2 5.2 fusion.417
  749.2 18.5 %collective-permute-done.1 = bf16[2,1152,192]{1,2,0:T(8,128)(2,1)S(1)} collective-permute-done((bf16[2,1152,192]{1,2,0:T(8,128)(2,1)}, bf16[2,1152,192]{1,2,0:T(8,128)(2,1)S(1)}, u32[]{:S(2)}, u32[]{:S(2)}) %collective-permute-start.1) | collective-permute-done | bytes 884768 | tf_op jit(solution)/shard_map/ppermute | solution.py:19
  770.9 4.8 add_convert_fusion
  775.8 42.2 %reduce-scatter.30.cloned.1.call-done = bf16[288,768]{1,0:T(8,128)(2,1)} async-done(((bf16[1152,768]{1,0:T(8,128)(2,1)}), bf16[288,768]{1,0:T(8,128)(2,1)}) %reduce-scatter.30.cloned.1.call-update) | async-done | bytes 442384 | tf_op jit(solution)/shard_map/reduce_scatter | solution.py:50
  823.1 40.0 %all-gather.20.cloned.1.call-done = bf16[1152,768]{1,0:T(8,128)(2,1)} async-done(((bf16[288,768]{1,0:T(8,128)(2,1)}), bf16[1152,768]{1,0:T(8,128)(2,1)}) %all-gather.20.cloned.1.call-update) | async-done | bytes 1769488 | tf_op jit(solution)/shard_map/all_gather | solution.py:46
  863.1 5.0 conditional.20
  871.8 45.0 %reduce-scatter.32.cloned.1.call-done = bf16[288,768]{1,0:T(8,128)(2,1)} async-done(((bf16[1152,768]{1,0:T(8,128)(2,1)}), bf16[288,768]{1,0:T(8,128)(2,1)}) %reduce-scatter.32.cloned.1.call-update) | async-done | bytes 442384 | tf_op jit(solution)/shard_map/reduce_scatter | solution.py:50
  923.0 33.5 %reduce-scatter.26.cloned.1.call-done = bf16[288,768]{1,0:T(8,128)(2,1)} async-done(((bf16[1152,768]{1,0:T(8,128)(2,1)}), bf16[288,768]{1,0:T(8,128)(2,1)}) %reduce-scatter.26.cloned.1.call-update) | async-done | bytes 442384 | tf_op jit(solution)/shard_map/reduce_scatter | solution.py:50
  956.5 4.4 convert_reduce_fusion.13
  964.7 3.7 fusion.210
  974.7 3.7 fusion.209
  978.4 22.5 %all-gather.22.cloned.1.call-done = bf16[1152,768]{1,0:T(8,128)(2,1)} async-done(((bf16[288,768]{1,0:T(8,128)(2,1)}), bf16[1152,768]{1,0:T(8,128)(2,1)}) %all-gather.22.cloned.1.call-update) | async-done | bytes 1769488 | tf_op jit(solution)/shard_map/all_gather | solution.py:46
  1006.2 50.2 %conditional.21 = (bf16[1,1152,192]{1,2,0:T(8,128)(2,1)}, f32[192]{0:T(256)S(1)}, bf16[1,1152,192]{1,2,0:T(8,128)(2,1)}, bf16[1,1152,192]{1,2,0:T(8,128)(2,1)}, f32[192]{0:T(256)S(1)}) conditional(s32[]{:T(128)} %convert_element_type.269, (bf16[1152,192]{0,1:T(8,128)(2,1)}, bf16[1152,192]{0,1:T(8,128)(2,1)}, ...), branch_computations={%region_60.65_spmd.clone, %region_64.69_spmd.clone} | conditional | flops 650057664 | bytes 65331464 | solution.py:404
  1023.9 17.1 %while.78 = (s32[]{:T(128)}, bf16[2,9,64,3,64]{4,2,3,1,0:T(8,128)(2,1)}, bf16[2,9,64,3,64]{4,2,3,1,0:T(8,128)(2,1)}, bf16[2,9,64,3,64]{2,4,3,1,0:T(8,128)(2,1)},...) while((s32[]{:T(128)}, ...), condition=%wide.region_63.64_spmd, body=%wide.region_61.63_spmd.sunk | while | flops 71993664 | bytes 21656128 | solution.py:251
  1059.7 3.7 fusion.206
  1068.6 4.1 fusion.200
  1077.1 5.8 reduce-scatter.36.cloned.1.call-done
  1085.1 21.3 %reduce-scatter.42.cloned.1.call-done = bf16[192,192]{1,0:T(8,128)(2,1)} async-done(((bf16[768,192]{1,0:T(8,128)(2,1)}), bf16[192,192]{1,0:T(8,128)(2,1)}) %reduce-scatter.42.cloned.1.call-update) | async-done | bytes 73744
  1108.3 25.3 %reduce-scatter.40.cloned.1.call-done = bf16[192,576]{1,0:T(8,128)(2,1)} async-done(((bf16[768,576]{1,0:T(8,128)(2,1)}), bf16[192,576]{1,0:T(8,128)(2,1)}) %reduce-scatter.40.cloned.1.call-update) | async-done | bytes 221200
  1135.9 36.5 %reduce-scatter.34.cloned.1.call-done = bf16[288,768]{1,0:T(8,128)(2,1)} async-done(((bf16[1152,768]{1,0:T(8,128)(2,1)}), bf16[288,768]{1,0:T(8,128)(2,1)}) %reduce-scatter.34.cloned.1.call-update) | async-done | bytes 442384 | tf_op jit(solution)/shard_map/reduce_scatter | solution.py:50
  1175.6 55.2 %all-reduce = (f32[1,2,768]{2,1,0:T(2,128)}, f32[1,768]{1,0:T(1,128)}, f32[1,3072]{1,0:T(1,128)}, f32[1,768]{1,0:T(1,128)}, f32[1,3,768]{2,0,1:T(1,128)}, /*index=5*/f32[1,3,768]{2,0,1:T(1,128)}) all-reduce(f32[1,2,768]{2,1,0:T(2,128)S(1)} %dynamic_update_slice.60, ...), channel_id=1, replica_groups=mesh['tower'=2,'dp'=4,'mp'=4] {'dp','mp'}, use_global_device_ids=true, to_apply=%region_78.80 | all-reduce | flops 10752 | bytes 86016 | tf_op jit(solution)/shard_map/psum | solution.py:437
  (556 shorter events, 292.1 us)
Async XLA Ops:
  7.2 46.9 %copy-start = (bf16[1,3,768,192]{2,3,1,0:T(8,128)(2,1)S(1)}, bf16[1,3,768,192]{2,3,1,0:T(8,128)(2,1)}, u32[]{:S(2)}) copy-start(bf16[1,3,768,192]{2,3,1,0:T(8,128)(2,1)} %param.55) | copy-start | bytes 2654212
  7.2 46.9 %all-gather.10.cloned.1.call-start = ((), (), s32[]{:S(2)}) async-start(), calls=%async_computation.13 | async-start | bytes 2211840 | tf_op jit(solution)/shard_map/all_gather | solution.py:46
  11.2 208.6 %copy-start.79 = (f32[768]{0:T(1024)}, f32[768]{0:T(1024)S(1)}, u32[]{:S(2)}) copy-start(f32[768]{0:T(1024)S(1)} %get-tuple-element.1220) | copy-start | bytes 9220
  11.2 535.5 %copy-start.70 = (f32[768]{0:T(1024)}, f32[768]{0:T(1024)S(1)}, u32[]{:S(2)}) copy-start(f32[768]{0:T(1024)S(1)} %get-tuple-element.1218) | copy-start | bytes 9220
  13.8 108.1 %reduce-scatter.20.cloned.1.call-start = ((), (), s32[]{:S(2)}) async-start(), calls=%async_computation.14 | async-start | bytes 2211840 | tf_op jit(solution)/shard_map/reduce_scatter | solution.py:50
  81.8 41.3 %copy-start.23 = (bf16[1152,192]{1,0:T(8,128)(2,1)}, bf16[1152,192]{1,0:T(8,128)(2,1)S(1)}, u32[]{:S(2)}) copy-start(bf16[1152,192]{1,0:T(8,128)(2,1)S(1)} %get-tuple-element.493) | copy-start | bytes 1327108
  81.8 41.3 %copy-start.59 = (f32[2,1728]{1,0:T(2,128)}, f32[2,1728]{1,0:T(2,128)S(1)}, u32[]{:S(2)}) copy-start(f32[2,1728]{1,0:T(2,128)S(1)} %get-tuple-element.508) | copy-start | bytes 41476
  84.9 81.7 %all-gather.12.cloned.1.call-start = ((), (), s32[]{:S(2)}) async-start(), calls=%async_computation.15 | async-start | bytes 2211840 | tf_op jit(solution)/shard_map/all_gather | solution.py:46
  85.0 321.6 %copy-start.67 = (f32[768]{0:T(1024)}, f32[768]{0:T(1024)S(1)}, u32[]{:S(2)}) copy-start(f32[768]{0:T(1024)S(1)} %reduce.14) | copy-start | bytes 9220
  123.2 43.5 %copy-start.77 = (f32[288]{0:T(512)}, f32[288]{0:T(512)S(1)}, u32[]{:S(2)}) copy-start(f32[288]{0:T(512)S(1)} %broadcast_multiply_fusion.2) | copy-start | bytes 3460
  124.5 42.1 %copy-start.96 = (f32[288]{0:T(512)}, f32[288]{0:T(512)S(1)}, u32[]{:S(2)}) copy-start(f32[288]{0:T(512)S(1)} %multiply_reduce_fusion.7) | copy-start | bytes 3460
  124.5 42.1 %copy-start.91 = (f32[288]{0:T(512)}, f32[288]{0:T(512)S(1)}, u32[]{:S(2)}) copy-start(f32[288]{0:T(512)S(1)} %fusion.257) | copy-start | bytes 3460
  126.6 91.5 %reduce-scatter.22.cloned.1.call-start = ((), (), s32[]{:S(2)}) async-start(), calls=%async_computation.16 | async-start | bytes 2211840 | tf_op jit(solution)/shard_map/reduce_scatter | solution.py:50
  172.1 46.0 %copy-start.10 = (bf16[288,768]{1,0:T(8,128)(2,1)S(1)}, bf16[288,768]{1,0:T(8,128)(2,1)}, u32[]{:S(2)}) copy-start(bf16[288,768]{1,0:T(8,128)(2,1)} %reduce-scatter.20.cloned.1.call-done) | copy-start | bytes 1327108
  175.6 85.9 %all-gather.14.cloned.1.call-start = ((), (), s32[]{:S(2)}) async-start(), calls=%async_computation.17 | async-start | bytes 2211840 | tf_op jit(solution)/shard_map/all_gather | solution.py:46
  175.7 43.8 %copy-start.83 = (f32[768]{0:T(1024)}, f32[768]{0:T(1024)S(1)}, u32[]{:S(2)}) copy-start(f32[768]{0:T(1024)S(1)} %reduce.18) | copy-start | bytes 9220
  175.7 85.8 %copy-start.25 = (bf16[1,2,768,192]{2,3,1,0:T(8,128)(2,1)S(1)}, bf16[1,2,768,192]{2,3,1,0:T(8,128)(2,1)}, u32[]{:S(2)}) copy-start(bf16[1,2,768,192]{2,3,1,0:T(8,128)(2,1)} %param.59) | copy-start | bytes 1769476
  219.5 42.0 %copy-start.81 = (f32[288]{0:T(512)}, f32[288]{0:T(512)S(1)}, u32[]{:S(2)}) copy-start(f32[288]{0:T(512)S(1)} %broadcast_multiply_fusion.1) | copy-start | bytes 3460
  219.8 41.7 %copy-start.97 = (f32[288]{0:T(512)}, f32[288]{0:T(512)S(1)}, u32[]{:S(2)}) copy-start(f32[288]{0:T(512)S(1)} %multiply_reduce_fusion.6) | copy-start | bytes 3460
  219.8 41.7 %copy-start.89 = (f32[288]{0:T(512)}, f32[288]{0:T(512)S(1)}, u32[]{:S(2)}) copy-start(f32[288]{0:T(512)S(1)} %fusion.258) | copy-start | bytes 3460
  221.4 185.2 %reduce-scatter.24.cloned.1.call-start = ((), (), s32[]{:S(2)}) async-start(), calls=%async_computation.18 | async-start | bytes 2211840 | tf_op jit(solution)/shard_map/reduce_scatter | solution.py:50
  262.7 23.4 %collective-permute-start = (bf16[2,1152,192]{1,2,0:T(8,128)(2,1)}, bf16[2,1152,192]{1,2,0:T(8,128)(2,1)}, u32[]{:S(2)}, u32[]{:S(2)}) collective-permute-start(bf16[2,1152,192]{1,2,0:T(8,128)(2,1)} %get-tuple-element.1797), channel_id=1, source_target_pairs={{0,16},{1,17},{2,18},{3,19},{4,20},{5,21},{6,22},{7,23},{8,24},{9,... | collective-permute-start | bytes 2654216 | tf_op jit(solution)/shard_map/ppermute | solution.py:19
  368.3 81.2 %copy-start.120 = (bf16[1,768,768]{2,1,0:T(8,128)(2,1)S(1)}, bf16[1,768,768]{2,1,0:T(8,128)(2,1)}, u32[]{:S(2)}) copy-start(bf16[1,768,768]{2,1,0:T(8,128)(2,1)} %param.57) | copy-start | bytes 3538948
  368.3 81.2 %all-gather.16.cloned.1.call-start = ((), (), s32[]{:S(2)}) async-start(), calls=%async_computation.19 | async-start | bytes 2211840 | tf_op jit(solution)/shard_map/all_gather | solution.py:46
  408.2 138.5 %copy-start.6 = (f32[288,768]{1,0:T(8,128)}, f32[288,768]{1,0:T(8,128)S(1)}, u32[]{:S(2)}) copy-start(f32[288,768]{1,0:T(8,128)S(1)} %get-tuple-element.1184) | copy-start | bytes 2654212
  409.5 80.9 %all-gather.24.cloned.1.call-start = ((), (), s32[]{:S(2)}) async-start(), calls=%async_computation.30 | async-start | bytes 2211840 | tf_op jit(solution)/shard_map/all_gather | solution.py:46
  410.2 134.5 %reduce-scatter.28.cloned.1.call-start = ((), (), s32[]{:S(2)}) async-start(), calls=%async_computation.21 | async-start | bytes 2211840 | tf_op jit(solution)/shard_map/reduce_scatter | solution.py:50
  507.7 40.5 %copy-start.110 = (f32[768]{0:T(1024)}, f32[768]{0:T(1024)S(1)}, u32[]{:S(2)}) copy-start(f32[768]{0:T(1024)S(1)} %get-tuple-element.518) | copy-start | bytes 9220
  507.7 41.5 %copy-start.16 = (bf16[1,288,768]{2,1,0:T(8,128)(2,1)S(1)}, bf16[1,288,768]{2,1,0:T(8,128)(2,1)}, u32[]{:S(2)}) copy-start(bf16[1,288,768]{2,1,0:T(8,128)(2,1)} %param.52) | copy-start | bytes 1327108
  507.7 82.5 %all-gather.18.cloned.1.call-start = ((), (), s32[]{:S(2)}) async-start(), calls=%async_computation.22 | async-start | bytes 2211840 | tf_op jit(solution)/shard_map/all_gather | solution.py:46
  546.7 43.5 %copy-start.26 = (bf16[1,2,768,192]{2,3,1,0:T(8,128)(2,1)S(1)}, bf16[1,2,768,192]{2,3,1,0:T(8,128)(2,1)}, u32[]{:S(2)}) copy-start(bf16[1,2,768,192]{2,3,1,0:T(8,128)(2,1)} %param.59) | copy-start | bytes 1769476
  546.7 43.5 %copy-start.29 = (bf16[2,576,3,64]{1,0,3,2:T(2,128)(2,1)S(1)}, bf16[2,576,3,64]{1,0,3,2:T(2,128)(2,1)}, u32[]{:S(2)}) copy-start(bf16[2,576,3,64]{1,0,3,2:T(2,128)(2,1)} %reshape_squeeze.6) | copy-start | bytes 1327108
  550.1 267.8 %reduce-scatter.30.cloned.1.call-start = ((), (), s32[]{:S(2)}) async-start(), calls=%async_computation.23 | async-start | bytes 2211840 | tf_op jit(solution)/shard_map/reduce_scatter | solution.py:50
  747.9 19.9 %collective-permute-start.1 = (bf16[2,1152,192]{1,2,0:T(8,128)(2,1)}, bf16[2,1152,192]{1,2,0:T(8,128)(2,1)S(1)}, u32[]{:S(2)}, u32[]{:S(2)}) collective-permute-start(bf16[2,1152,192]{1,2,0:T(8,128)(2,1)} %get-tuple-element.503), channel_id=1, source_target_pairs={{16,0},{17,1},{18,2},{19,3},{20,4},{21,5},{22,6},{23,7},{24,8},{25... | collective-permute-start | bytes 2654216 | tf_op jit(solution)/shard_map/ppermute | solution.py:19
  770.9 47.0 %copy-start.80 = (f32[768]{0:T(1024)S(1)}, f32[768]{0:T(1024)}, u32[]{:S(2)}) copy-start(f32[768]{0:T(1024)} %copy-done.79) | copy-start | bytes 9220
  770.9 47.0 %copy-start.82 = (f32[288]{0:T(512)S(1)}, f32[288]{0:T(512)}, u32[]{:S(2)}) copy-start(f32[288]{0:T(512)} %copy-done.81) | copy-start | bytes 3460
  770.9 47.0 %copy-start.90 = (f32[288]{0:T(512)S(1)}, f32[288]{0:T(512)}, u32[]{:S(2)}) copy-start(f32[288]{0:T(512)} %copy-done.89) | copy-start | bytes 3460
  775.7 42.2 %copy-start.13 = (f32[288,768]{1,0:T(8,128)S(1)}, f32[288,768]{1,0:T(8,128)}, u32[]{:S(2)}) copy-start(f32[288,768]{1,0:T(8,128)} %copy-done.12) | copy-start | bytes 2654212
  775.7 44.2 %copy-start.98 = (f32[288]{0:T(512)S(1)}, f32[288]{0:T(512)}, u32[]{:S(2)}) copy-start(f32[288]{0:T(512)} %copy-done.97) | copy-start | bytes 3460
  775.7 45.7 %copy-start.17 = (bf16[1,288,768]{2,1,0:T(8,128)(2,1)S(1)}, bf16[1,288,768]{2,1,0:T(8,128)(2,1)}, u32[]{:S(2)}) copy-start(bf16[1,288,768]{2,1,0:T(8,128)(2,1)} %param.52) | copy-start | bytes 1327108
  775.7 87.4 %all-gather.20.cloned.1.call-start = ((), (), s32[]{:S(2)}) async-start(), calls=%async_computation.24 | async-start | bytes 2211840 | tf_op jit(solution)/shard_map/all_gather | solution.py:46
  821.4 41.7 %copy-start.20 = (f32[288,768]{1,0:T(8,128)}, f32[288,768]{1,0:T(8,128)S(1)}, u32[]{:S(2)}) copy-start(f32[288,768]{1,0:T(8,128)S(1)} %get-tuple-element.1180) | copy-start | bytes 2654212
  821.4 41.7 %copy-start.101 = (f32[288]{0:T(512)}, f32[288]{0:T(512)S(1)}, u32[]{:S(2)}) copy-start(f32[288]{0:T(512)S(1)} %negate_multiply_fusion.2) | copy-start | bytes 3460
  823.1 93.7 %reduce-scatter.32.cloned.1.call-start = ((), (), s32[]{:S(2)}) async-start(), calls=%async_computation.25 | async-start | bytes 2211840 | tf_op jit(solution)/shard_map/reduce_scatter | solution.py:50
  868.1 88.4 %reduce-scatter.26.cloned.1.call-start = ((), (), s32[]{:S(2)}) async-start(), calls=%async_computation.20 | async-start | bytes 2211840 | tf_op jit(solution)/shard_map/reduce_scatter | solution.py:50
  868.2 48.6 %copy-start.4 = (bf16[1,288,768]{2,1,0:T(8,128)(2,1)S(1)}, bf16[1,288,768]{2,1,0:T(8,128)(2,1)}, u32[]{:S(2)}) copy-start(bf16[1,288,768]{2,1,0:T(8,128)(2,1)} %param.51) | copy-start | bytes 1327108
  868.2 48.6 %copy-start.11 = (bf16[288,768]{1,0:T(8,128)(2,1)S(1)}, bf16[288,768]{1,0:T(8,128)(2,1)}, u32[]{:S(2)}) copy-start(bf16[288,768]{1,0:T(8,128)(2,1)} %reduce-scatter.20.cloned.1.call-done) | copy-start | bytes 1327108
  868.2 48.6 %copy-start.68 = (f32[768]{0:T(1024)S(1)}, f32[768]{0:T(1024)}, u32[]{:S(2)}) copy-start(f32[768]{0:T(1024)} %copy-done.67) | copy-start | bytes 9220
  868.2 48.6 %copy-start.71 = (f32[768]{0:T(1024)S(1)}, f32[768]{0:T(1024)}, u32[]{:S(2)}) copy-start(f32[768]{0:T(1024)} %copy-done.70) | copy-start | bytes 9220
  868.2 48.6 %copy-start.78 = (f32[288]{0:T(512)S(1)}, f32[288]{0:T(512)}, u32[]{:S(2)}) copy-start(f32[288]{0:T(512)} %copy-done.77) | copy-start | bytes 3460
  871.7 84.8 %copy-start.7 = (f32[288,768]{1,0:T(8,128)S(1)}, f32[288,768]{1,0:T(8,128)}, u32[]{:S(2)}) copy-start(f32[288,768]{1,0:T(8,128)} %copy-done.6) | copy-start | bytes 2654212
  871.7 84.8 %copy-start.84 = (f32[768]{0:T(1024)S(1)}, f32[768]{0:T(1024)}, u32[]{:S(2)}) copy-start(f32[768]{0:T(1024)} %copy-done.83) | copy-start | bytes 9220
  871.8 129.2 %all-gather.22.cloned.1.call-start = ((), (), s32[]{:S(2)}) async-start(), calls=%async_computation.26 | async-start | bytes 2211840 | tf_op jit(solution)/shard_map/all_gather | solution.py:46
  960.9 112.0 %reduce-scatter.44.cloned.1.call-start = ((), (), s32[]{:S(2)}) async-start(), calls=%async_computation.33 | async-start | bytes 737280
  964.6 110.6 %reduce-scatter.38.cloned.1.call-start = ((), (), s32[]{:S(2)}) async-start(), calls=%async_computation.29 | async-start | bytes 1474560 | tf_op jit(solution)/shard_map/reduce_scatter | solution.py:458
  968.4 114.5 %reduce-scatter.36.cloned.1.call-start = ((), (), s32[]{:S(2)}) async-start(), calls=%async_computation.28 | async-start | bytes 1474560 | tf_op jit(solution)/shard_map/reduce_scatter | solution.py:455
  978.4 128.0 %reduce-scatter.42.cloned.1.call-start = ((), (), s32[]{:S(2)}) async-start(), calls=%async_computation.32 | async-start | bytes 491520
  1057.5 76.1 %reduce-scatter.40.cloned.1.call-start = ((), (), s32[]{:S(2)}) async-start(), calls=%async_computation.31 | async-start | bytes 1228800
  1068.3 104.2 %reduce-scatter.34.cloned.1.call-start = ((), (), s32[]{:S(2)}) async-start(), calls=%async_computation.27 | async-start | bytes 2211840 | tf_op jit(solution)/shard_map/reduce_scatter | solution.py:50
  1075.2 97.3 %copy-start.74 = (f32[768]{0:T(1024)S(1)}, f32[768]{0:T(1024)}, u32[]{:S(2)}) copy-start(f32[768]{0:T(1024)} %copy-done.73) | copy-start | bytes 9220
  1075.2 97.3 %copy-start.76 = (f32[288]{0:T(512)S(1)}, f32[288]{0:T(512)}, u32[]{:S(2)}) copy-start(f32[288]{0:T(512)} %copy-done.75) | copy-start | bytes 3460
  1077.1 96.8 %copy-start.95 = (f32[288]{0:T(512)S(1)}, f32[288]{0:T(512)}, u32[]{:S(2)}) copy-start(f32[288]{0:T(512)} %copy-done.94) | copy-start | bytes 3460
  1077.1 96.9 %copy-start.88 = (f32[288]{0:T(512)S(1)}, f32[288]{0:T(512)}, u32[]{:S(2)}) copy-start(f32[288]{0:T(512)} %copy-done.87) | copy-start | bytes 3460
  1107.4 123.4 %copy-start.37 = (f32[288,768]{1,0:T(8,128)S(1)}, f32[288,768]{1,0:T(8,128)}, u32[]{:S(2)}) copy-start(f32[288,768]{1,0:T(8,128)} %get-tuple-element.1178) | copy-start | bytes 2654212
  (93 other events, 457.7 us)
Sparse Core Ops, SparseCore 0:
  13.9 40.0 all-gather.9
  85.1 36.7 reduce-scatter.19
  126.7 39.8 all-gather.11
  175.7 42.3 reduce-scatter.21
  221.6 39.8 all-gather.13
  368.4 38.1 reduce-scatter.23
  409.6 39.8 all-gather.15
  451.2 39.1 all-gather.23
  507.9 36.7 reduce-scatter.27
  550.3 39.8 all-gather.17
  775.9 42.0 reduce-scatter.29
  823.2 39.8 all-gather.19
  868.3 48.4 reduce-scatter.31
  919.0 37.4 reduce-scatter.25
  961.1 39.8 all-gather.21
  1004.1 22.2 reduce-scatter.43
  1029.0 25.7 reduce-scatter.37
  1057.2 25.6 reduce-scatter.35
  1085.5 20.8 reduce-scatter.41
  1109.0 24.4 reduce-scatter.39
  1135.9 36.5 reduce-scatter.33
where the time goes:
time: 1260 us; the launch traced here: 1240 us
  waiting for transfers between devices  692 us (55%)
  local copies, waits for them, and re-layouts  239 us (19%)
  other arithmetic  120 us (10%)
  matrix products  111 us (9%)
  blocking collectives  55.2 us (4%)
  between operations  15.6 us (1%)
    reduce_scatter x8, waiting for transfers between devices, combine(): lax.psum_scatter(partial_rows.astype(jnp.bfloat16), 'mp', scatter_dimensi...  312 us
    all_gather x8, waiting for transfers between devices, widen_rows(): return lax.all_gather(rows_low, 'mp', axis=0, tiled=True)  289 us
    psum x1, blocking collectives, body(): lax.psum((full_qv[None], g_bias_out[None], full_in[None], g_bias_mlp[None...  55.2 us
    unnamed x24, waiting for transfers between devices  47.7 us
    select_n x4, other arithmetic, one_block(): val_pick = jnp.take(image_vals, pick_blk, axis=0)  39.8 us
    ppermute x2, waiting for transfers between devices, passed_along(): return lax.ppermute(x, axis, pairs)  38.1 us
    gather x4, local copies, waits for them, and re-layouts, one_block(): key_pick = jnp.take(image_keys, pick_blk, axis=0)  28.7 us
    gather x4, local copies, waits for them, and re-layouts, one_block(): val_pick = jnp.take(image_vals, pick_blk, axis=0)  28.7 us
  transfers between devices with their start and end apart: 23, of which 21 were waited for; matrix products, arithmetic and copies ran while one was open for 10% of the time, Pallas kernels for 0%

commit v1 on v0

v1 whole, which is shorter than its diff:
```python
import functools

import jax
import jax.numpy as jnp
from jax import lax
from jax.experimental import pallas as pl
from jax.experimental.pallas import tpu as pltpu
from jax.sharding import PartitionSpec as P

HDIM = 64
PATCH = 576
LTXT = 64
EPS = 1e-06
NEG = -1e30
LANES = 128
MESH = pl.DeviceIdType.MESH
F32 = jnp.float32
BF16 = jnp.bfloat16
VMEM_LIMIT = 60 * 1024 * 1024


def norm_parts(values):
    center = values - jnp.mean(values, axis=-1, keepdims=True)
    spread = jnp.mean(center * center, axis=-1, keepdims=True)
    scale = lax.rsqrt(spread + EPS)
    return (center * scale, scale)


def norm_rows(values, gain_vec, shift_vec):
    unit, _ = norm_parts(values)
    return unit * gain_vec + shift_vec


def norm_back(values, gain_vec, grad_normed):
    unit, scale = norm_parts(values)
    inner = grad_normed * gain_vec
    mean_one = jnp.mean(inner, axis=-1, keepdims=True)
    mean_two = jnp.mean(inner * unit, axis=-1, keepdims=True)
    back = (inner - mean_one - unit * mean_two) * scale
    return (back, jnp.sum(grad_normed * unit, axis=0), jnp.sum(grad_normed, axis=0))


def gelu_tanh(values):
    return jax.nn.gelu(values, approximate=True)


def dot_rows(left, right):
    return lax.dot_general(left, right, (((1,), (1,)), ((), ())), preferred_element_type=F32)


def dot_first(left, right):
    return lax.dot_general(left, right, (((0,), (0,)), ((), ())), preferred_element_type=F32)


def dot_plain(left, right):
    return lax.dot_general(left, right, (((1,), (0,)), ((), ())), preferred_element_type=F32)


def stack_heads(block, low_lanes):
    wide = block.astype(F32)
    return jnp.concatenate([jnp.where(low_lanes, wide, 0.0), jnp.where(low_lanes, 0.0, wide)], axis=0)


def merge_heads(pair, low_lanes):
    return jnp.where(low_lanes, pair[:LTXT], pair[LTXT:])


def low_half():
    return lax.broadcasted_iota(jnp.int32, (LTXT, LANES), 1) < HDIM


def causal_mask(seg_col, seg_row):
    key_at = lax.broadcasted_iota(jnp.int32, (LTXT, LANES), 0)
    query_at = lax.broadcasted_iota(jnp.int32, (LTXT, LANES), 1) % LTXT
    return jnp.logical_and(key_at <= query_at, seg_col == seg_row)


def key_block(mode, ref, r, picks):
    if mode == "image":
        return ref[...]
    if mode == "text":
        return ref[pl.ds(pl.multiple_of(r * LTXT, LTXT), LTXT), :]
    return ref[picks[r]]


def attend_kernel(mode, rows, scale, *refs):
    if mode == "cross":
        picks, q_ref, k_ref, v_ref, o_ref, l_ref = refs
    elif mode == "text":
        picks = None
        q_ref, k_ref, v_ref, segc_ref, segr_ref, o_ref, l_ref = refs
    else:
        picks = None
        q_ref, k_ref, v_ref, o_ref, l_ref = refs
    low = low_half()

    def step(r, carry):
        at = pl.ds(pl.multiple_of(r * LTXT, LTXT), LTXT)
        queries = (stack_heads(q_ref[at, :], low) * scale).astype(BF16)
        keys = key_block(mode, k_ref, r, picks)
        vals = key_block(mode, v_ref, r, picks)
        scores = dot_rows(keys, queries)
        if mode == "text":
            scores = jnp.where(causal_mask(segc_ref[at, :], segr_ref[pl.ds(r, 1), :]), scores, NEG)
        top = jnp.max(scores, axis=0, keepdims=True)
        grown = jnp.exp(scores - top)
        total = jnp.sum(grown, axis=0, keepdims=True)
        weights = (grown * (1.0 / total)).astype(BF16)
        mixed = dot_first(weights, vals)
        o_ref[at, :] = merge_heads(mixed, low).astype(BF16)
        l_ref[0, pl.ds(r, 1), :] = top + jnp.log(total)
        return carry

    lax.fori_loop(0, rows, step, 0, unroll=3)


def attend_back_kernel(mode, rows, scale, pairs, *refs):
    if mode == "cross":
        picks, q_ref, k_ref, v_ref, g_ref, l_ref, dq_ref, dk_ref, dv_ref, dk_acc, dv_acc = refs
    elif mode == "text":
        picks = None
        q_ref, k_ref, v_ref, g_ref, l_ref, segc_ref, segr_ref, d_ref, dk_acc, dv_acc = refs
    else:
        picks = None
        q_ref, k_ref, v_ref, g_ref, l_ref, d_ref, dk_acc, dv_acc = refs
    low = low_half()
    pair = pl.program_id(0)
    if mode != "text":
        dk_acc[...] = jnp.zeros_like(dk_acc)
        dv_acc[...] = jnp.zeros_like(dv_acc)

    def lanes(part):
        return pl.ds(pl.multiple_of((part * pairs + pair) * LANES, LANES), LANES)

    def step(r, carry):
        at = pl.ds(pl.multiple_of(r * LTXT, LTXT), LTXT)
        queries = (stack_heads(q_ref[at, :], low) * scale).astype(BF16)
        grads = stack_heads(g_ref[at, :], low).astype(BF16)
        keys = key_block(mode, k_ref, r, picks)
        vals = key_block(mode, v_ref, r, picks)
        scores = dot_rows(keys, queries)
        if mode == "text":
            scores = jnp.where(causal_mask(segc_ref[at, :], segr_ref[pl.ds(r, 1), :]), scores, NEG)
        weights = jnp.exp(scores - l_ref[0, pl.ds(r, 1), :])
        grad_w = dot_rows(vals, grads)
        row_dot = jnp.sum(weights * grad_w, axis=0, keepdims=True)
        grad_s = (weights * (grad_w - row_dot)).astype(BF16)
        grad_q = merge_heads(dot_first(grad_s, keys), low) * scale
        grad_k = dot_plain(grad_s, queries)
        grad_v = dot_plain(weights.astype(BF16), grads)
        if mode == "cross":
            dq_ref[at, :] = grad_q.astype(BF16)
            dk_acc[picks[r]] += grad_k
            dv_acc[picks[r]] += grad_v
        elif mode == "text":
            d_ref[at, lanes(0)] = grad_q.astype(BF16)
            d_ref[at, lanes(1)] = grad_k.astype(BF16)
            d_ref[at, lanes(2)] = grad_v.astype(BF16)
        else:
            d_ref[at, lanes(0)] = grad_q.astype(BF16)
            dk_acc[...] += grad_k
            dv_acc[...] += grad_v
        return carry

    lax.fori_loop(0, rows, step, 0)
    if mode == "cross":
        dk_ref[...] = dk_acc[...].astype(BF16)
        dv_ref[...] = dv_acc[...].astype(BF16)
    elif mode == "image":
        d_ref[:, lanes(1)] = dk_acc[...].astype(BF16)
        d_ref[:, lanes(2)] = dv_acc[...].astype(BF16)


def column(part, pairs, rows):
    return pl.BlockSpec((rows, LANES), lambda i, *_: (0, part * pairs + i))


def whole(shape):
    return pl.BlockSpec(shape, lambda i, *_: (0,) * len(shape))


def tops_spec():
    return pl.BlockSpec((1, 16, LANES), lambda i, *_: (i, 0, 0))


def self_cost(tokens, heads, products, mode):
    keys = PATCH if mode != "text" else LTXT
    return pl.CostEstimate(
        flops=2 * products * 2 * tokens * keys * HDIM * heads,
        bytes_accessed=8 * tokens * heads * HDIM,
        transcendentals=tokens * keys * heads,
    )


def kernel_params():
    return pltpu.CompilerParams(vmem_limit_bytes=VMEM_LIMIT)


def self_attend(mode, packed, seg_col, seg_row, scale):
    tokens = packed.shape[0]
    pairs = packed.shape[1] // (3 * LANES)
    rows = tokens // LTXT
    specs = [column(part, pairs, tokens) for part in range(3)]
    extra = ()
    if mode == "text":
        specs += [whole(seg_col.shape), whole(seg_row.shape)]
        extra = (seg_col, seg_row)
    return pl.pallas_call(
        functools.partial(attend_kernel, mode, rows, scale),
        grid=(pairs,),
        in_specs=specs,
        out_specs=[column(0, pairs, tokens), tops_spec()],
        out_shape=[
            jax.ShapeDtypeStruct((tokens, pairs * LANES), BF16),
            jax.ShapeDtypeStruct((pairs, 16, LANES), F32),
        ],
        compiler_params=kernel_params(),
        cost_estimate=self_cost(tokens, 2 * pairs, 2, mode),
        name="attend_" + mode,
    )(packed, packed, packed, *extra)


def self_attend_back(mode, packed, grads, tops, seg_col, seg_row, scale):
    tokens = packed.shape[0]
    pairs = packed.shape[1] // (3 * LANES)
    rows = tokens // LTXT
    specs = [column(part, pairs, tokens) for part in range(3)] + [column(0, pairs, tokens), tops_spec()]
    extra = ()
    if mode == "text":
        specs += [whole(seg_col.shape), whole(seg_row.shape)]
        extra = (seg_col, seg_row)
    return pl.pallas_call(
        functools.partial(attend_back_kernel, mode, rows, scale, pairs),
        grid=(pairs,),
        in_specs=specs,
        out_specs=whole(packed.shape),
        out_shape=jax.ShapeDtypeStruct(packed.shape, BF16),
        scratch_shapes=[pltpu.VMEM((tokens, LANES), F32), pltpu.VMEM((tokens, LANES), F32)],
        compiler_params=kernel_params(),
        cost_estimate=self_cost(tokens, 2 * pairs, 5, mode),
        name="attend_back_" + mode,
    )(packed, packed, packed, grads, tops, *extra)


def image_block(images, keys):
    return pl.BlockSpec((images, keys, LANES), lambda i, *_: (0, 0, i))


def cross_attend(queries, keys, vals, picks, scale):
    tokens, wide = queries.shape
    pairs = wide // LANES
    images, key_rows, _ = keys.shape
    grid = pltpu.PrefetchScalarGridSpec(
        num_scalar_prefetch=1,
        grid=(pairs,),
        in_specs=[column(0, pairs, tokens), image_block(images, key_rows), image_block(images, key_rows)],
        out_specs=[column(0, pairs, tokens), tops_spec()],
    )
    return pl.pallas_call(
        functools.partial(attend_kernel, "cross", tokens // LTXT, scale),
        grid_spec=grid,
        out_shape=[
            jax.ShapeDtypeStruct((tokens, wide), BF16),
            jax.ShapeDtypeStruct((pairs, 16, LANES), F32),
        ],
        compiler_params=kernel_params(),
        cost_estimate=self_cost(tokens, 2 * pairs, 2, "cross"),
        name="attend_cross",
    )(picks, queries, keys, vals)


def cross_attend_back(queries, keys, vals, grads, tops, picks, scale):
    tokens, wide = queries.shape
    pairs = wide // LANES
    images, key_rows, _ = keys.shape
    grid = pltpu.PrefetchScalarGridSpec(
        num_scalar_prefetch=1,
        grid=(pairs,),
        in_specs=[
            column(0, pairs, tokens),
            image_block(images, key_rows),
            image_block(images, key_rows),
            column(0, pairs, tokens),
            tops_spec(),
        ],
        out_specs=[column(0, pairs, tokens), image_block(images, key_rows), image_block(images, key_rows)],
        scratch_shapes=[pltpu.VMEM((images, key_rows, LANES), F32)] * 2,
    )
    return pl.pallas_call(
        functools.partial(attend_back_kernel, "cross", tokens // LTXT, scale, pairs),
        grid_spec=grid,
        out_shape=[
            jax.ShapeDtypeStruct((tokens, wide), BF16),
            jax.ShapeDtypeStruct(keys.shape, BF16),
            jax.ShapeDtypeStruct(keys.shape, BF16),
        ],
        compiler_params=kernel_params(),
        cost_estimate=self_cost(tokens, 2 * pairs, 5, "cross"),
        name="attend_back_cross",
    )(picks, queries, keys, vals, grads, tops)


def gather_kernel(pieces, n_src, *refs):
    srcs = refs[:n_src]
    outs = refs[n_src : 2 * n_src]
    stages = refs[2 * n_src : 3 * n_src]
    send_sem, recv_sem, local_sem, twin_send, twin_recv, = refs[3 * n_src :]
    tower = lax.axis_index("tower")
    dp = lax.axis_index("dp")
    z = lax.axis_index("mp")
    core = lax.rem(dp, 2)
    line = dp // 2
    place = z + core * (3 - 2 * z)
    ahead = z + 1 - 2 * core
    behind = z - 1 + 2 * core
    other = dp + 2 - 4 * line
    slot_of = (core, 1 - core)
    is_text = tower == 1
    cross = n_src - 1

    barrier = pltpu.get_barrier_semaphore()

    @pl.when(z > 0)
    def _():
        pl.semaphore_signal(barrier, inc=1, device_id={"mp": z - 1}, device_id_type=MESH)

    @pl.when(z < 3)
    def _():
        pl.semaphore_signal(barrier, inc=1, device_id={"mp": z + 1}, device_id_type=MESH)

    pl.semaphore_signal(barrier, inc=1, device_id={"dp": other}, device_id_type=MESH)
    pl.semaphore_signal(barrier, inc=1, device_id={"tower": 1 - tower}, device_id_type=MESH)

    @pl.when(jnp.logical_or(z == 0, z == 3))
    def _():
        pl.semaphore_wait(barrier, 3)

    @pl.when(jnp.logical_and(z > 0, z < 3))
    def _():
        pl.semaphore_wait(barrier, 4)

    def spot(piece, slot, half):
        which, first, start, size, far = piece
        part = size // 2
        count = srcs[which].shape[0]
        return outs[which].at[pl.ds(first, count), slot, pl.ds(start + half * part, part), :]

    def own(piece):
        which, first, start, size, far = piece
        part = size // 2
        if far:
            return outs[which].at[pl.ds(first, srcs[which].shape[0]), lax.rem(z, 2), pl.ds(start + line * part, part), :]
        return srcs[which].at[:, pl.ds(start + line * part, part), :]

    def move(k, source, slot, half, kind, arrive, target):
        return pltpu.make_async_remote_copy(
            src_ref=source,
            dst_ref=spot(pieces[k], slot, half),
            send_sem=send_sem.at[k, kind],
            recv_sem=recv_sem.at[k, arrive],
            device_id=target,
            device_id_type=MESH,
        )

    def twin_copy():
        slot = lax.rem(z, 2)
        return pltpu.make_async_remote_copy(
            src_ref=srcs[cross],
            dst_ref=outs[cross].at[pl.ds(0, srcs[cross].shape[0]), slot],
            send_sem=twin_send,
            recv_sem=twin_recv,
            device_id={"tower": 1 - tower},
            device_id_type=MESH,
        )

    holder = place <= 1

    @pl.when(jnp.logical_and(holder, tower == 0))
    def _():
        twin_copy().start()

    def local_in(i):
        return pltpu.make_async_copy(srcs[i], stages[i], local_sem.at[i, 0])

    def local_out(i):
        first = outs[i].shape[0] - srcs[i].shape[0]
        return pltpu.make_async_copy(stages[i], outs[i].at[pl.ds(first, srcs[i].shape[0]), lax.rem(z, 2)], local_sem.at[i, 1])

    def gate(piece, cond):
        which = piece[0]
        return jnp.logical_and(cond, is_text) if which == cross else cond

    def send_own(k):
        piece = pieces[k]

        @pl.when(gate(piece, place == 0))
        def _():
            move(k, own(piece), slot_of[0], line, 0, 0, {"mp": ahead}).start()

        @pl.when(gate(piece, place == 1))
        def _():
            move(k, own(piece), slot_of[1], line, 1, 1, {"mp": ahead}).start()
            move(k, own(piece), slot_of[1], line, 2, 1, {"mp": behind}).start()

    for k, piece in enumerate(pieces):
        if not piece[4]:
            send_own(k)

    @pl.when(holder)
    def _():
        for i in range(n_src):
            local_in(i).start()
        for i in range(n_src):
            local_in(i).wait()
            local_out(i).start()

    def pass_on(k):
        piece = pieces[k]
        if piece[4]:

            @pl.when(jnp.logical_and(holder, is_text))
            def _():
                twin_copy().wait_recv()

            send_own(k)

        @pl.when(gate(piece, place >= 1))
        def _():
            here = spot(piece, slot_of[0], line)
            move(k, here, slot_of[0], line, 0, 0, {"mp": z}).wait_recv()
            move(k, here, slot_of[0], line, 3, 2, {"dp": other}).start()

        @pl.when(gate(piece, jnp.logical_and(place >= 1, place <= 2)))
        def _():
            here = spot(piece, slot_of[0], line)
            move(k, here, slot_of[0], line, 0, 0, {"mp": ahead}).start()

        @pl.when(gate(piece, place != 1))
        def _():
            here = spot(piece, slot_of[1], line)
            move(k, here, slot_of[1], line, 1, 1, {"mp": z}).wait_recv()
            move(k, here, slot_of[1], line, 4, 3, {"dp": other}).start()

        @pl.when(gate(piece, place == 2))
        def _():
            here = spot(piece, slot_of[1], line)
            move(k, here, slot_of[1], line, 1, 1, {"mp": ahead}).start()

    for k in range(len(pieces)):
        pass_on(k)

    def finish(k):
        piece = pieces[k]

        @pl.when(gate(piece, place <= 2))
        def _():
            move(k, spot(piece, slot_of[0], line), slot_of[0], line, 0, 0, {"mp": z}).wait_send()

        @pl.when(gate(piece, jnp.logical_and(place >= 1, place <= 2)))
        def _():
            move(k, spot(piece, slot_of[1], line), slot_of[1], line, 1, 1, {"mp": z}).wait_send()

        @pl.when(gate(piece, place == 1))
        def _():
            move(k, spot(piece, slot_of[1], line), slot_of[1], line, 2, 1, {"mp": z}).wait_send()

        @pl.when(gate(piece, place >= 1))
        def _():
            made = move(k, spot(piece, slot_of[0], 1 - line), slot_of[0], 1 - line, 3, 2, {"dp": dp})
            made.wait_send()
            made.wait_recv()

        @pl.when(gate(piece, place != 1))
        def _():
            made = move(k, spot(piece, slot_of[1], 1 - line), slot_of[1], 1 - line, 4, 3, {"dp": dp})
            made.wait_send()
            made.wait_recv()

    for k in range(len(pieces)):
        finish(k)

    @pl.when(holder)
    def _():
        for i in range(n_src):
            local_out(i).wait()

    @pl.when(jnp.logical_and(holder, tower == 0))
    def _():
        twin_copy().wait_send()


def gather_weights(shards):
    n_src = len(shards)
    outs = [
        jax.ShapeDtypeStruct(((2 if i == n_src - 1 else 1) * s.shape[0], 2) + s.shape[1:], BF16)
        for i, s in enumerate(shards)
    ]
    pieces = []
    for i, s in enumerate(shards):
        rows = s.shape[1]
        if i == n_src - 1:
            pieces.append((i, s.shape[0], 0, rows, False))
            pieces.insert(2, (i, 0, 0, rows, True))
        else:
            cut = rows if rows <= 192 else rows // 2
            pieces += [(i, 0, at, cut, False) for at in range(0, rows, cut)]
    n = len(pieces)
    any_spec = pl.BlockSpec(memory_space=pl.ANY)
    return pl.pallas_call(
        functools.partial(gather_kernel, tuple(pieces), n_src),
        in_specs=[any_spec] * n_src,
        out_specs=[any_spec] * n_src,
        out_shape=outs,
        scratch_shapes=[pltpu.VMEM(s.shape, BF16) for s in shards]
        + [
            pltpu.SemaphoreType.DMA((n, 5)),
            pltpu.SemaphoreType.DMA((n, 4)),
            pltpu.SemaphoreType.DMA((n_src, 2)),
            pltpu.SemaphoreType.DMA,
            pltpu.SemaphoreType.DMA,
        ],
        compiler_params=pltpu.CompilerParams(
            collective_id=0, has_side_effects=True, vmem_limit_bytes=VMEM_LIMIT
        ),
        name="gather_weights",
    )(*shards)


TILE = 32


def reduce_kernel(pieces, flags, n_src, with_smalls, *refs):
    it = iter(refs)
    srcs = [next(it) for _ in range(n_src)]
    small_in = next(it) if with_smalls else None
    outs = [next(it) for _ in range(n_src)]
    small_out = next(it) if with_smalls else None
    mine = [next(it) for _ in range(n_src)]
    near = [next(it) for _ in range(n_src)]
    far = [next(it) for _ in range(n_src)]
    if with_smalls:
        small_near, small_all = next(it), next(it)
        small_sem = next(it)
    local_sem, y_send, y_recv, z_send, z_recv, c_send, c_recv = it
    tower = lax.axis_index("tower")
    dp = lax.axis_index("dp")
    z = lax.axis_index("mp")
    core = lax.rem(dp, 2)
    line = dp // 2
    other = dp + 2 - 4 * line
    partner = dp + 1 - 2 * core
    holder = z // 2 == core
    slot = lax.rem(z, 2)
    half = srcs[0].shape[3] // 2

    barrier = pltpu.get_barrier_semaphore()
    pl.semaphore_signal(barrier, inc=1, device_id={"dp": other}, device_id_type=MESH)
    pl.semaphore_signal(barrier, inc=1, device_id={"dp": partner}, device_id_type=MESH)
    for away in range(1, 4):
        pl.semaphore_signal(barrier, inc=1, device_id={"mp": lax.rem(z + away, 4)}, device_id_type=MESH)
    pl.semaphore_wait(barrier, 5)

    def gate(piece, cond=None):
        flag = flags[piece[0]]
        if flag is None:
            return cond
        here = tower == flag
        return here if cond is None else jnp.logical_and(cond, here)

    def guarded(cond, run):
        if cond is None:
            run()
        else:
            pl.when(cond)(run)

    def rows_of(piece):
        return pl.ds(piece[1], piece[2])

    def to_line(k):
        which = pieces[k][0]
        rows = rows_of(pieces[k])
        return pltpu.make_async_remote_copy(
            src_ref=srcs[which].at[:, :, rows, pl.ds(pl.multiple_of((1 - line) * half, LANES), half)],
            dst_ref=near[which].at[:, :, rows, :],
            send_sem=y_send.at[k],
            recv_sem=y_recv.at[k],
            device_id={"dp": other},
            device_id_type=MESH,
        )

    def to_mine(k):
        which = pieces[k][0]
        rows = rows_of(pieces[k])
        return pltpu.make_async_copy(
            srcs[which].at[:, :, rows, pl.ds(pl.multiple_of(line * half, LANES), half)],
            mine[which].at[:, :, rows, :],
            local_sem.at[k],
        )

    def to_chip(k, shard, seat):
        which = pieces[k][0]
        rows = rows_of(pieces[k])
        target = 2 * core + shard
        return pltpu.make_async_remote_copy(
            src_ref=mine[which].at[:, shard, rows, :],
            dst_ref=far[which].at[seat, :, rows, :],
            send_sem=z_send.at[k, shard],
            recv_sem=z_recv.at[k, seat],
            device_id={"mp": target},
            device_id_type=MESH,
        )

    def to_core(k):
        which = pieces[k][0]
        rows = rows_of(pieces[k])
        return pltpu.make_async_remote_copy(
            src_ref=outs[which].at[:, rows, :],
            dst_ref=outs[which].at[:, rows, :],
            send_sem=c_send.at[k],
            recv_sem=c_recv.at[k],
            device_id={"dp": partner},
            device_id_type=MESH,
        )

    def seat_of(shard):
        return lax.rem(z - (2 * core + shard) + 4, 4) - 1

    for k, piece in enumerate(pieces):

        def begin(k=k):
            to_line(k).start()
            to_mine(k).start()

        guarded(gate(piece), begin)

    if with_smalls:
        small_line = pltpu.make_async_remote_copy(
            src_ref=small_in,
            dst_ref=small_near,
            send_sem=small_sem.at[0],
            recv_sem=small_sem.at[1],
            device_id={"dp": other},
            device_id_type=MESH,
        )
        small_line.start()

        def small_move(away):
            return pltpu.make_async_remote_copy(
                src_ref=small_all.at[z],
                dst_ref=small_all.at[z],
                send_sem=small_sem.at[1 + away],
                recv_sem=small_sem.at[4 + away],
                device_id={"mp": lax.rem(z + away, 4)},
                device_id_type=MESH,
            )

        def small_got(away):
            sender = lax.rem(z + 4 - away, 4)
            return pltpu.make_async_remote_copy(
                src_ref=small_all.at[sender],
                dst_ref=small_all.at[sender],
                send_sem=small_sem.at[1 + away],
                recv_sem=small_sem.at[4 + away],
                device_id={"mp": lax.rem(z + away, 4)},
                device_id_type=MESH,
            )

        def small_core(which):
            return pltpu.make_async_remote_copy(
                src_ref=small_out.at[which],
                dst_ref=small_out.at[which],
                send_sem=small_sem.at[8],
                recv_sem=small_sem.at[9],
                device_id={"dp": partner},
                device_id_type=MESH,
            )

        small_line.wait()
        small_all[z] = small_in[...] + small_near[...]

    for k, piece in enumerate(pieces):
        which, start, size = piece
        count = srcs[which].shape[0]

        def add_near(k=k, which=which, start=start, size=size, count=count):
            to_mine(k).wait()
            to_line(k).wait_recv()

            @pl.loop(0, size // TILE)
            def _(i):
                rows = pl.ds(pl.multiple_of(start + i * TILE, TILE), TILE)
                for a in range(count):
                    for b in range(2):
                        total = mine[which][a, b, rows, :].astype(F32) + near[which][a, b, rows, :].astype(F32)
                        mine[which][a, b, rows, :] = total.astype(BF16)

            for shard in range(2):

                @pl.when(z != 2 * core + shard)
                def _(shard=shard):
                    to_chip(k, shard, seat_of(shard)).start()

        guarded(gate(piece), add_near)
        if with_smalls and k == 0:
            for away in range(1, 4):
                small_move(away).start()

    for k, piece in enumerate(pieces):
        which, start, size = piece
        count = srcs[which].shape[0]

        def add_far(k=k, which=which, start=start, size=size, count=count):
            for seat in range(3):
                to_chip(k, 0, seat).wait_recv()

            @pl.loop(0, size // TILE)
            def _(i):
                rows = pl.ds(pl.multiple_of(start + i * TILE, TILE), TILE)
                for a in range(count):
                    total = mine[which][a, slot, rows, :].astype(F32)
                    for seat in range(3):
                        total = total + far[which][seat, a, rows, :].astype(F32)
                    outs[which][a, rows, :] = total.astype(BF16)

            to_core(k).start()

        guarded(gate(piece, holder), add_far)

    if with_smalls:
        for away in range(1, 4):
            small_got(away).wait_recv()
        small_out[core] = ((small_all[0] + small_all[1]) + small_all[2]) + small_all[3]
        small_core(core).start()

    for k, piece in enumerate(pieces):

        def ended(k=k):
            to_line(k).wait_send()
            for shard in range(2):

                @pl.when(z != 2 * core + shard)
                def _(shard=shard):
                    to_chip(k, shard, 0).wait_send()

            @pl.when(holder)
            def _():
                to_core(k).wait_send()

            @pl.when(jnp.logical_not(holder))
            def _():
                to_core(k).wait_recv()

        guarded(gate(piece), ended)

    if with_smalls:
        for away in range(1, 4):
            small_move(away).wait_send()
        small_core(core).wait_send()
        small_core(1 - core).wait_recv()


def reduce_grads(grads, flags, smalls, collective_id):
    n_src = len(grads)
    pieces = []
    for i, g in enumerate(grads):
        rows = g.shape[2]
        cut = rows if rows <= 192 else rows // 2
        pieces += [(i, at, cut) for at in range(0, rows, cut)]
    n = len(pieces)
    half = grads[0].shape[3] // 2
    any_spec = pl.BlockSpec(memory_space=pl.ANY)
    vmem_spec = pl.BlockSpec(memory_space=pltpu.VMEM)
    in_specs = [any_spec] * n_src
    out_shape = [jax.ShapeDtypeStruct((g.shape[0], g.shape[2], half), BF16) for g in grads]
    out_specs = [vmem_spec] * n_src
    args = list(grads)
    with_smalls = smalls is not None
    scratch = (
        [pltpu.VMEM(g.shape[:3] + (half,), BF16) for g in grads] * 2
        + [pltpu.VMEM((3, g.shape[0], g.shape[2], half), BF16) for g in grads]
    )
    if with_smalls:
        in_specs.append(vmem_spec)
        out_specs.append(vmem_spec)
        out_shape.append(jax.ShapeDtypeStruct((2,) + smalls.shape, F32))
        args.append(smalls)
        scratch += [
            pltpu.VMEM(smalls.shape, F32),
            pltpu.VMEM((4,) + smalls.shape, F32),
            pltpu.SemaphoreType.DMA((10,)),
        ]
    scratch += [
        pltpu.SemaphoreType.DMA((n,)),
        pltpu.SemaphoreType.DMA((n,)),
        pltpu.SemaphoreType.DMA((n,)),
        pltpu.SemaphoreType.DMA((n, 2)),
        pltpu.SemaphoreType.DMA((n, 3)),
        pltpu.SemaphoreType.DMA((n,)),
        pltpu.SemaphoreType.DMA((n,)),
    ]
    return pl.pallas_call(
        functools.partial(reduce_kernel, tuple(pieces), tuple(flags), n_src, with_smalls),
        in_specs=in_specs,
        out_specs=out_specs,
        out_shape=out_shape,
        scratch_shapes=scratch,
        compiler_params=pltpu.CompilerParams(
            collective_id=collective_id, has_side_effects=True, vmem_limit_bytes=VMEM_LIMIT
        ),
        name="reduce_grads_%d" % collective_id,
    )(*args)


def gather_plain(shards):
    core = lax.rem(lax.axis_index("dp"), 2)
    outs = []
    for i, s in enumerate(shards):
        if i == len(shards) - 1:
            s = jnp.concatenate([lax.ppermute(s, "tower", [(0, 1)]), s], axis=0)
        full = lax.all_gather(s, "mp", axis=1, tiled=False)
        outs.append(lax.dynamic_slice_in_dim(full, 2 * core, 2, 1))
    return outs


def reduce_plain(grads, smalls):
    dp = lax.axis_index("dp")
    core = lax.rem(dp, 2)
    outs = []
    for g in grads:
        n, _, rows, wide = g.shape
        full = jnp.zeros((n, 4, rows, wide), BF16)
        full = lax.dynamic_update_slice(full, g, (0, 2 * core, 0, 0))
        part = lax.psum_scatter(full, "mp", scatter_dimension=1, tiled=False)
        part = lax.psum_scatter(part, "dp", scatter_dimension=2, tiled=True)
        outs.append(part)
    if smalls is None:
        return outs
    both = jnp.zeros((2,) + smalls.shape, F32)
    both = lax.dynamic_update_slice(both, smalls[None], (core, 0, 0))
    return outs + [lax.psum(both, ("dp", "mp"))]


def body(
    tower_in,
    out_cot,
    segment_ids,
    row_image,
    attn_qkv,
    attn_out,
    mlp_in,
    mlp_out,
    cross_proj,
    qv_bias,
    out_bias,
    mlp_bias_in,
    mlp_bias_out,
    norm_gain,
    norm_bias,
):
    lines = lax.axis_size("dp") // 2
    depth = lax.axis_size("mp")
    devices = lax.axis_size("dp")
    is_enc = lax.axis_index("tower") == 0
    dp = lax.axis_index("dp")
    z = lax.axis_index("mp")
    core = lax.rem(dp, 2)
    side = lax.rem(z, 2)
    group = z // 2
    direct = lines == 2
    assert depth == 4
    quarter = tower_in.shape[1]
    tokens = 2 * quarter
    assert tokens == PATCH
    width = tower_in.shape[2]
    head_cols = 2 * attn_qkv.shape[3]
    hidden = 2 * mlp_in.shape[2]
    scale_qk = HDIM ** (-0.5)

    out_moves, back_moves = [], []
    for d in range(devices):
        for place in range(depth):
            here = d * depth + place
            there = (d - d % 2 + place % 2) * depth + 2 * (d % 2) + place // 2
            out_moves.append((here, there))
            back_moves.append((there, here))

    def swap_cores(x):
        return lax.ppermute(x, "dp", [(i, i ^ 1) for i in range(devices)])

    def both_cores(own):
        other = swap_cores(own)
        return jnp.where(core == 0, jnp.concatenate([own, other], -2), jnp.concatenate([other, own], -2))

    def own_rows(full):
        return lax.dynamic_slice_in_dim(full, core * quarter, quarter, full.ndim - 2)

    def add_cores(part):
        low = lax.reduce_precision(part, 8, 7).astype(BF16)
        return low.astype(F32) + swap_cores(low).astype(F32)

    shards = [
        jnp.swapaxes(attn_qkv[0], 1, 2),
        attn_out,
        mlp_in,
        mlp_out,
        jnp.swapaxes(cross_proj[0], 1, 2),
    ]
    gathered = gather_weights(shards) if direct else gather_plain(shards)
    w_qkv = gathered[0].reshape(3 * head_cols, width)
    w_out = gathered[1].reshape(head_cols, width)
    w_in = gathered[2][0]
    w_mlp = gathered[3].reshape(hidden, width)
    w_cross = gathered[4].reshape(4, head_cols, width)
    bias_qv = lax.dynamic_slice_in_dim(qv_bias[0], core * head_cols, head_cols, 1)
    bias_packed = jnp.concatenate([bias_qv[0], jnp.zeros_like(bias_qv[0]), bias_qv[1]])
    bias_in = lax.dynamic_slice_in_dim(mlp_bias_in[0], core * hidden, hidden, 0)
    gains = norm_gain[0]
    shifts = norm_bias[0]

    stream_low = both_cores(lax.ppermute(tower_in[0], ("dp", "mp"), out_moves))
    cot_low = both_cores(lax.ppermute(out_cot[0], ("dp", "mp"), out_moves))
    stream = stream_low.astype(F32)
    rows_dev = segment_ids.shape[0]
    rows = rows_dev // 2
    segs = jnp.where(core == group, segment_ids, swap_cores(segment_ids))
    segs = lax.dynamic_slice_in_dim(segs, rows * side, rows, 0)
    picks = jnp.where(core == group, row_image, swap_cores(row_image))
    picks = lax.dynamic_slice_in_dim(picks, rows * side, rows, 0)
    seg_row = jnp.pad(jnp.concatenate([segs, segs], axis=1), ((0, 16 - rows), (0, 0)))
    seg_col = jnp.broadcast_to(segs.reshape(rows * LTXT, 1), (rows * LTXT, LANES))

    act_one = norm_rows(stream, gains[0], shifts[0]).astype(BF16)
    packed = (dot_rows(act_one, w_qkv) + bias_packed).astype(BF16)
    mixed, tops = lax.cond(
        is_enc,
        lambda p: tuple(self_attend("image", p, seg_col, seg_row, scale_qk)),
        lambda p: tuple(self_attend("text", p, seg_col, seg_row, scale_qk)),
        packed,
    )
    stream_one = stream + add_cores(dot_plain(mixed, w_out)) + out_bias[0]

    def feed_in(values):
        act = norm_rows(values, gains[1], shifts[1]).astype(BF16)
        pre = jnp.concatenate([dot_plain(act, w_in[0]), dot_plain(act, w_in[1])], axis=1) + bias_in
        return (act, pre, gelu_tanh(pre).astype(BF16))

    def feed_out(hid):
        return add_cores(dot_plain(hid, w_mlp)) + mlp_bias_out[0]

    act_enc, pre_enc, hid_enc = feed_in(stream_one)
    out_enc = stream_one + feed_out(hid_enc)
    base_three = jnp.where(is_enc, out_enc, stream_one)
    act_three = norm_rows(base_three, gains[2], shifts[2]).astype(BF16)

    near_half = lax.ppermute(own_rows(act_three), "tower", [(0, 1)])
    far_half = lax.ppermute(near_half, "mp", [(i, i ^ 1) for i in range(depth)])
    halves = jnp.where(side == 0, jnp.stack([near_half, far_half]), jnp.stack([far_half, near_half]))
    images = both_cores(halves)

    cross_q = dot_rows(act_three, w_cross[2]).astype(BF16)
    flat_images = images.reshape(2 * tokens, width)
    cross_k = dot_rows(flat_images, w_cross[0]).astype(BF16).reshape(2, tokens, head_cols)
    cross_v = dot_rows(flat_images, w_cross[1]).astype(BF16).reshape(2, tokens, head_cols)
    cross_mix, cross_tops = cross_attend(cross_q, cross_k, cross_v, picks, scale_qk)
    stream_two = stream_one + add_cores(dot_plain(cross_mix, w_cross[3]))

    act_dec, pre_dec, hid_dec = feed_in(stream_two)
    out_dec = stream_two + feed_out(hid_dec)
    tower_out = own_rows(jnp.where(is_enc, out_enc, out_dec).astype(BF16))
    tower_out = lax.ppermute(tower_out, ("dp", "mp"), back_moves)

    def feed_back(grad_low, pre):
        grad_hid = dot_rows(grad_low, w_mlp)
        _, pullback = jax.vjp(gelu_tanh, pre)
        grad_pre = pullback(grad_hid)[0].astype(BF16)
        cols = hidden // 2
        part = dot_rows(grad_pre[:, :cols], w_in[0]) + dot_rows(grad_pre[:, cols:], w_in[1])
        return (grad_pre, add_cores(part))

    def feed_grads(grad_low, act, grad_pre, hid):
        g_in = dot_first(grad_pre, act).astype(BF16)
        g_mlp = dot_first(hid, grad_low).astype(BF16)
        return (
            g_in.reshape(1, 2, hidden // 2, width),
            g_mlp.reshape(1, 2, hidden // 2, width),
        )

    cot = cot_low.astype(F32)
    grad_pre_dec, back_in = feed_back(cot_low, pre_dec)
    back_a, gain_a, shift_a = norm_back(stream_two, gains[1], back_in)
    grad_two = cot + back_a
    grad_two_low = grad_two.astype(BF16)

    grad_mix = dot_rows(grad_two_low, w_cross[3]).astype(BF16)
    grad_q, grad_k, grad_v = cross_attend_back(
        cross_q, cross_k, cross_v, grad_mix, cross_tops, picks, scale_qk
    )
    flat_k = grad_k.reshape(2 * tokens, head_cols)
    flat_v = grad_v.reshape(2 * tokens, head_cols)
    part_images = dot_plain(flat_k, w_cross[0]) + dot_plain(flat_v, w_cross[1])
    part_low = part_images.astype(BF16).reshape(2, 2, quarter, width)
    give = lax.dynamic_index_in_dim(part_low, 1 - core, 1, keepdims=False)
    keep = lax.dynamic_index_in_dim(part_low, core, 1, keepdims=False)
    pair_sum = (keep.astype(F32) + swap_cores(give).astype(F32)).astype(BF16)
    give = lax.dynamic_index_in_dim(pair_sum, 1 - side, 0, keepdims=False)
    keep = lax.dynamic_index_in_dim(pair_sum, side, 0, keepdims=False)
    got = lax.ppermute(give, "mp", [(i, i ^ 1) for i in range(depth)])
    image_sum = (keep.astype(F32) + got.astype(F32)).astype(BF16)
    image_back = both_cores(lax.ppermute(image_sum, "tower", [(1, 0)])).astype(F32)
    query_back = add_cores(dot_plain(grad_q, w_cross[2]))

    g_cross = jnp.concatenate(
        [
            dot_first(flat_k, flat_images).astype(BF16),
            dot_first(flat_v, flat_images).astype(BF16),
            dot_first(grad_q, act_three).astype(BF16),
            dot_first(cross_mix, grad_two_low).astype(BF16),
        ],
        axis=0,
    ).reshape(4, 2, head_cols // 2, width)

    back_three, gain_three, shift_three = norm_back(
        base_three, gains[2], jnp.where(is_enc, image_back, query_back)
    )
    grad_enc = cot + back_three
    grad_enc_low = grad_enc.astype(BF16)
    grad_pre_enc, back_in = feed_back(grad_enc_low, pre_enc)
    back_b, gain_b, shift_b = norm_back(stream_one, gains[1], back_in)
    grad_one = jnp.where(is_enc, grad_enc + back_b, grad_two + back_three)
    grad_one_low = grad_one.astype(BF16)

    feed_low = jnp.where(is_enc, grad_enc_low, cot_low)
    feed_pre = jnp.where(is_enc, grad_pre_enc, grad_pre_dec)
    g_in, g_mlp = feed_grads(
        feed_low,
        jnp.where(is_enc, act_enc, act_dec),
        feed_pre,
        jnp.where(is_enc, hid_enc, hid_dec),
    )

    g_out = dot_first(mixed, grad_one_low).astype(BF16).reshape(1, 2, head_cols // 2, width)
    grad_mixed = dot_rows(grad_one_low, w_out).astype(BF16)
    grad_packed = lax.cond(
        is_enc,
        lambda p, g, t: self_attend_back("image", p, g, t, seg_col, seg_row, scale_qk),
        lambda p, g, t: self_attend_back("text", p, g, t, seg_col, seg_row, scale_qk),
        packed,
        grad_mixed,
        tops,
    )
    g_qkv = dot_first(grad_packed, act_one).astype(BF16).reshape(3, 2, head_cols // 2, width)
    back_in = add_cores(dot_plain(grad_packed, w_qkv))
    back_one, gain_one, shift_one = norm_back(stream, gains[0], back_in)
    grad_in = own_rows((grad_one + back_one).astype(BF16))
    grad_in = lax.ppermute(grad_in, ("dp", "mp"), back_moves)

    packed_sum = jnp.sum(grad_packed, axis=0, dtype=F32)
    shared = [
        jnp.sum(grad_one_low, axis=0, dtype=F32),
        jnp.sum(feed_low, axis=0, dtype=F32),
        gain_one,
        jnp.where(is_enc, gain_b, gain_a),
        gain_three,
        shift_one,
        jnp.where(is_enc, shift_b, shift_a),
        shift_three,
    ]
    by_core = [
        packed_sum[:head_cols],
        packed_sum[2 * head_cols :],
        jnp.sum(feed_pre, axis=0, dtype=F32),
    ]
    smalls = jnp.concatenate(shared + by_core)
    used = smalls.shape[0]
    lines_of = -(-used // (8 * LANES)) * 8
    smalls = jnp.pad(smalls, (0, lines_of * LANES - used)).reshape(lines_of, LANES)

    grads = [g_qkv, g_out, g_in, g_mlp, g_cross]
    flags = [None, None, None, None, 1]
    if direct:
        sums = reduce_grads(grads, flags, smalls, 1)

        def own_cols(x):
            cut = x.shape[2] // 2
            return jnp.where(core == 0, x[:, :, :cut], x[:, :, cut:])

        *sums, total = sums
        sums = [own_cols(s) for s in sums]
    else:
        *sums, total = reduce_plain(grads, smalls)
    s_qkv, s_out, s_in, s_mlp, s_cross = sums
    from_text = lax.ppermute(s_cross[:2], "tower", [(1, 0)])
    s_cross = jnp.where(is_enc, from_text, s_cross[2:])

    def turned(x):
        return jnp.swapaxes(x, 1, 2).astype(F32)

    cross_pair = jnp.stack(
        [
            s_cross[0].T,
            s_cross[1].T,
        ]
    ).astype(F32)
    total = total.reshape(2, lines_of * LANES)
    first = total[0]
    pieces = [first[i * width : (i + 1) * width] for i in range(8)]
    at = 8 * width
    parts = total[:, at:]
    qv_total = jnp.stack(
        [
            parts[:, :head_cols].reshape(-1),
            parts[:, head_cols : 2 * head_cols].reshape(-1),
        ]
    )
    in_total = parts[:, 2 * head_cols : 2 * head_cols + hidden].reshape(-1)
    return (
        tower_out[None],
        grad_in[None],
        turned(s_qkv)[None],
        s_out.astype(F32),
        turned(s_in),
        s_mlp.astype(F32),
        cross_pair[None],
        qv_total[None],
        pieces[0][None],
        in_total[None],
        pieces[1][None],
        jnp.stack(pieces[2:5])[None],
        jnp.stack(pieces[5:8])[None],
    )


def solution(mesh):
    return jax.shard_map(
        body,
        mesh=mesh,
        in_specs=(
            P("tower", ("dp", "mp"), None),
            P("tower", ("dp", "mp"), None),
            P("dp", None),
            P("dp"),
            P("tower", None, None, "mp"),
            P("tower", "mp", None),
            P("tower", None, "mp"),
            P("tower", "mp", None),
            P("tower", None, None, "mp"),
            P("tower", None, None),
            P("tower", None),
            P("tower", None),
            P("tower", None),
            P("tower", None, None),
            P("tower", None, None),
        ),
        out_specs=(
            P("tower", ("dp", "mp"), None),
            P("tower", ("dp", "mp"), None),
            P("tower", None, "dp", "mp"),
            P("tower", "mp", "dp"),
            P("tower", "dp", "mp"),
            P("tower", "mp", "dp"),
            P("tower", None, "dp", "mp"),
            P("tower", None, None),
            P("tower", None),
            P("tower", None),
            P("tower", None),
            P("tower", None, None),
            P("tower", None, None),
        ),
        check_vma=False,
    )
```

time: 1260 us -> 613 us (0.49)
  waiting for transfers between devices: 692 us -> 66.5 us
  Pallas kernels: 0 us -> 371 us
  local copies, waits for them, and re-layouts: 239 us -> 36 us
  other arithmetic: 120 us -> 38.6 us
  blocking collectives: 55.2 us -> 0 us
  matrix products: 111 us -> 61.8 us
  starting transfers between devices: 3.72 us -> 26.8 us
  between operations: 15.6 us -> 2.6 us
    pallas_call x0 -> x6, Pallas kernels: none -> 371 us  [the longest x1 217 us: reduce_grads(): pl.pallas_call(functools.partial(reduce_kernel, tuple(pieces), tuple(flag...]
    reduce_scatter x10 -> x0, waiting for transfers between devices: 317 us -> none  [the longest x8 312 us: combine(): lax.psum_scatter(partial_rows.astype(jnp.bfloat16), 'mp', scatter_dimensi...]
    all_gather x8 -> x0, waiting for transfers between devices: 289 us -> none  [widen_rows(): return lax.all_gather(rows_low, 'mp', axis=0, tiled=True)]
    gather x8 -> x0, local copies, waits for them, and re-layouts: 57.4 us -> none  [the longest x4 28.7 us: one_block(): key_pick = jnp.take(image_keys, pick_blk, axis=0)]
    psum x1 -> x0, blocking collectives: 55.2 us -> none  [body(): lax.psum((full_qv[None], g_bias_out[None], full_in[None], g_bias_mlp[None...]
    unnamed x24 -> x0, waiting for transfers between devices: 47.7 us -> none
    while x108 -> x0, local copies, waits for them, and re-layouts: 43.4 us -> none
    dot_general x48 -> x32, matrix products: 103 us -> 61.8 us  [the longest x12 23.5 us: dot_rows(): lax.dot_general(left, right, (((1,), (1,)), ((), ())), preferred_element_...]
  transfers between devices with their start and end apart: 23 -> 24, of which waited for: 21 -> 11; matrix products, arithmetic and copies ran while one was open for 10% -> 7% of each run, Pallas kernels for 0% -> 17%
where the time goes in v1:
time: 613 us; the launch traced here: 603 us
  Pallas kernels  371 us (61%)
  waiting for transfers between devices  66.5 us (11%)
  matrix products  61.8 us (10%)
  other arithmetic  38.6 us (6%)
  local copies, waits for them, and re-layouts  36 us (6%)
  starting transfers between devices  26.8 us (4%)
    pallas_call x1, Pallas kernels, reduce_grads(): pl.pallas_call(functools.partial(reduce_kernel, tuple(pieces), tuple(flag...  217 us
    pallas_call x1, Pallas kernels, gather_weights(): pl.pallas_call(functools.partial(gather_kernel, tuple(pieces), n_src), in...  102 us
    unnamed x239, local copies, waits for them, and re-layouts  24.5 us
    dot_general x12, matrix products, dot_rows(): lax.dot_general(left, right, (((1,), (1,)), ((), ())), preferred_element_...  23.5 us
    dot_general x12, matrix products, dot_plain(): lax.dot_general(left, right, (((1,), (0,)), ((), ())), preferred_element_...  20 us
    pallas_call x1, Pallas kernels, cross_attend_back(): pl.pallas_call(functools.partial(attend_back_kernel, 'cross', tokens // L...  19.4 us
    dot_general x8, matrix products, dot_first(): lax.dot_general(left, right, (((0,), (0,)), ((), ())), preferred_element_...  18.3 us
    pallas_call x1, Pallas kernels, self_attend_back(): pl.pallas_call(functools.partial(attend_back_kernel, mode, rows, scale, p...  12.5 us
  transfers between devices with their start and end apart: 24, of which 11 were waited for; matrix products, arithmetic and copies ran while one was open for 7% of the time, Pallas kernels for 17%

profile of v1, /device:TPU:11, one launch (start us, length us, event | category | flops | bytes accessed | tf_op | source)
XLA Modules:
  0.0 603.4 jit_solution(17087662391373780927)
XLA Ops:
  0.7 3.2 collective-permute-start
  6.1 8.0 %collective-permute-done = bf16[288,768]{1,0:T(8,128)(2,1)S(1)} collective-permute-done((bf16[288,768]{1,0:T(8,128)(2,1)}, bf16[288,768]{1,0:T(8,128)(2,1)S(1)}, u32[]{:S(2)}, u32[]{:S(2)}) %collective-permute-start) | collective-permute-done | bytes 442400 | tf_op jit(solution)/shard_map/ppermute | solution.py:920
  14.2 2.3 collective-permute-start.1
  16.5 1.3 slice_reduce_fusion
  17.9 102.2 %gather_weights.1 = (bf16[3,2,192,768]{3,2,1,0:T(8,128)(2,1)}, bf16[1,2,192,768]{3,2,1,0:T(8,128)(2,1)}, bf16[1,2,768,768]{3,2,1,0:T(8,128)(2,1)}, bf16[1,2,768,...) custom-call(bf16[3,192,768]{2,1,0:T(8,128)(2,1)} %bitcast.197, bf16[1,192,768]{2,1,0:T(8,128)(2,1)} %refs_1_.2, ...), custom_call_target="tpu_custom_call" | custom-call | tf_op jit(solution)/shard_map/gather_weights/pallas_call | solution.py:509
  121.8 1.6 fusion.15
  124.3 9.9 %conditional.2 = ((bf16[576,384]{1,0:T(8,128)(2,1)}, f32[3,16,128]{2,1,0:T(8,128)})) conditional(s32[]{:T(128)} %convert_element_type.243, (bf16[576,1152]{1,0:T(8,128)(2,1)S(1)}, s32[576,128]{1,0:T(8,128)}, s32[16,128]{1,0:T(8,128)S(1)}) %tuple.28, bf16[576,1152]{1,0:T(8,128)(2,1)S(1)} %fusion.15), branch_computations={%region_2.3_spmd, %region_3.4_spmd} | conditional | flops 1019215872 | bytes 1769480 | solution.py:934
  124.3 9.9 %attend_text.1 = (bf16[576,384]{1,0:T(8,128)(2,1)}, f32[3,16,128]{2,1,0:T(8,128)}) custom-call(bf16[576,1152]{1,0:T(8,128)(2,1)S(1)} %get-tuple-element.33.refs_0_.refs_1_.refs_2_, bf16[576,1152]{1,0:T(8,128)(2,1)S(1)} %get-tuple-element.33.refs_0_.refs_1_.refs_2_, bf16[576,1152]{1,0:T(8,128)(2,1)S(1)} %get-tuple-element.33.refs_0_.refs_1_.refs_2_, ...), custom_call_target="tpu_custom_call" | custom-call | flops 113246208 | bytes 1769472 | tf_op jit(solution)/shard_map/cond/branch_0_fun/attend_text/pallas_call | solution.py:208
  134.2 1.6 reduce-precision_convert_fusion.7
  136.8 1.7 collective-permute-done.3
  138.5 2.3 fusion.85
  145.0 1.8 copy-done.92
  146.7 3.3 reduce-precision_convert_fusion.6
  150.2 2.6 collective-permute-done.4
  152.8 2.8 fusion.84
  157.8 1.7 collective-permute-start.6
  159.6 11.9 %collective-permute-done.6 = bf16[288,768]{1,0:T(8,128)(2,1)} collective-permute-done((bf16[288,768]{1,0:T(8,128)(2,1)S(1)}, bf16[288,768]{1,0:T(8,128)(2,1)}, u32[]{:S(2)}, u32[]{:S(2)}) %collective-permute-start.6) | collective-permute-done | bytes 442400 | tf_op jit(solution)/shard_map/ppermute | solution.py:955
  171.7 10.7 %collective-permute-done.7 = bf16[288,768]{1,0:T(8,128)(2,1)} collective-permute-done((bf16[288,768]{1,0:T(8,128)(2,1)}, bf16[288,768]{1,0:T(8,128)(2,1)}, u32[]{:S(2)}, u32[]{:S(2)}) %collective-permute-start.7) | collective-permute-done | bytes 442400 | tf_op jit(solution)/shard_map/ppermute | solution.py:956
  182.5 1.7 maximum_select_fusion.2
  184.2 1.9 collective-permute-start.8
  186.2 2.6 fusion.89
  189.6 1.4 convolution_convert_fusion.10.refs_1_
  191.8 2.0 convolution_convert_fusion.3
  193.9 2.0 convolution_convert_fusion.4
  195.9 9.5 %attend_cross.1 = (bf16[576,384]{1,0:T(8,128)(2,1)}, f32[3,16,128]{2,1,0:T(8,128)}) custom-call(s32[9]{0:T(128)} %dynamic_slice.38.refs_0_, bf16[576,384]{1,0:T(8,128)(2,1)} %convolution_convert_fusion.10.refs_1_, bf16[2,576,384]{2,1,0:T(8,128)(2,1)} %bitcast.221, bf16[2,576,384]{2,1,0:T(8,128)(2,1)} %bitcast.219), custom_call_target="tpu_custom_call" | custom-call | flops 1019215872 | bytes 1769472 | tf_op jit(solution)/shard_map/attend_cross/pallas_call | solution.py:259
  205.4 1.9 reduce-precision_convert_fusion.5
  207.8 1.9 collective-permute-start.12
  209.7 10.0 %collective-permute-done.12 = bf16[288,768]{1,0:T(8,128)(2,1)S(1)} collective-permute-done((bf16[288,768]{1,0:T(8,128)(2,1)S(1)}, bf16[288,768]{1,0:T(8,128)(2,1)S(1)}, u32[]{:S(2)}, u32[]{:S(2)}) %collective-permute-start.12) | collective-permute-done | bytes 442400 | tf_op jit(solution)/shard_map/ppermute | solution.py:921
  219.7 3.1 collective-permute-start.13
  227.7 1.8 copy-done.93
  229.5 4.4 fusion.13
  235.2 1.8 reduce-precision_convert_fusion.3
  238.4 1.4 collective-permute-done.14
  239.8 3.6 multiply_reduce_fusion.1
  243.4 2.8 convert_add_fusion.2
  247.5 1.4 convolution_convert_fusion.9.refs_4_
  248.9 19.4 %attend_back_cross.1 = (bf16[576,384]{1,0:T(8,128)(2,1)}, bf16[2,576,384]{2,1,0:T(8,128)(2,1)}, bf16[2,576,384]{2,1,0:T(8,128)(2,1)}) custom-call(s32[9]{0:T(128)} %dynamic_slice.38.refs_0_, bf16[576,384]{1,0:T(8,128)(2,1)} %convolution_convert_fusion.10.refs_1_, bf16[2,576,384]{2,1,0:T(8,128)(2,1)} %bitcast.222, bf16[2,576,384]{2,1,0:T(8,128)(2,1)} %bitcast.220, ...), custom_call_target="tpu_custom_call" | custom-call | flops 2548039680 | bytes 1769472 | tf_op jit(solution)/shard_map/attend_back_cross/pallas_call | solution.py:289
  268.4 2.5 fusion.90
  273.7 2.3 reduce-precision_convert_fusion.4
  280.1 8.5 %collective-permute-done.16 = bf16[288,768]{1,0:T(8,128)(2,1)S(1)} collective-permute-done((bf16[288,768]{1,0:T(8,128)(2,1)S(1)}, bf16[288,768]{1,0:T(8,128)(2,1)S(1)}, u32[]{:S(2)}, u32[]{:S(2)}) %collective-permute-start.16) | collective-permute-done | bytes 442400 | tf_op jit(solution)/shard_map/ppermute | solution.py:1007
  290.4 2.2 collective-permute-start.11
  293.5 5.0 collective-permute-done.17
  298.5 1.9 collective-permute-start.18
  301.1 1.6 pad_maximum_fusion
  303.8 1.8 multiply_reduce_fusion
  305.6 2.4 convert_reduce_fusion.4
  308.1 5.5 convert_reduce_fusion.2
  313.6 3.6 convolution_convert_fusion.1
  319.1 5.6 convolution_convert_fusion
  324.6 1.5 multiply_reduce_fusion.2
  326.1 2.5 convert_reduce_fusion.5
  329.9 14.1 %conditional.3 = (bf16[576,1152]{1,0:T(8,128)(2,1)}, f32[384]{0:T(512)S(1)}, f32[384]{0:T(512)S(1)}) conditional(s32[]{:T(128)} %convert_element_type.243, (bf16[576,1152]{1,0:T(8,128)(2,1)S(1)}, bf16[576,384]{1,0:T(8,128)(2,1)S(1)}, f32[3,16,128]{2,1,0:T(8,128)S(1)}, s32[576,128]{1,0:T(8,128)}, s32[16,128]{1,0:T(8,128)S(1)}) %tuple.93, ...), branch_computations={%region_16.18_spmd, %region_18.20_spmd} | conditional | flops 2549365760 | bytes 3107352 | solution.py:1043
  329.9 12.5 %attend_back_text.2 = bf16[576,1152]{1,0:T(8,128)(2,1)} custom-call(bf16[576,1152]{1,0:T(8,128)(2,1)S(1)} %get-tuple-element.36.refs_0_.refs_1_.refs_2_, bf16[576,1152]{1,0:T(8,128)(2,1)S(1)} %get-tuple-element.36.refs_0_.refs_1_.refs_2_, bf16[576,1152]{1,0:T(8,128)(2,1)S(1)} %get-tuple-element.36.refs_0_.refs_1_.refs_2_, ...), custom_call_target="tpu_custom_call" | custom-call | flops 283115520 | bytes 1769472 | tf_op jit(solution)/shard_map/cond/branch_0_fun/attend_back_text/pallas_call | solution.py:232
  342.4 1.5 convert_reduce_fusion
  344.0 3.3 reduce-precision_convert_fusion
  348.0 1.5 convolution_convert_fusion.7
  349.5 4.4 convolution_convert_fusion.2
  353.9 2.8 fusion.27
  357.6 217.5 %reduce_grads_1.1 = (bf16[3,192,384]{2,1,0:T(8,128)(2,1)}, bf16[1,192,384]{2,1,0:T(8,128)(2,1)}, bf16[1,768,384]{2,1,0:T(8,128)(2,1)}, bf16[1,768,384]{2,1,0:T(8...) custom-call(bf16[3,2,192,768]{3,2,1,0:T(8,128)(2,1)} %bitcast.196, bf16[1,2,192,768]{3,2,1,0:T(8,128)(2,1)} %bitcast.193, ...), custom_call_target="tpu_custom_call" | custom-call | tf_op jit(solution)/shard_map/reduce_grads_1/pallas_call | solution.py:801
  582.1 2.0 collective-permute-start.23
  585.3 2.2 copy.34
  587.5 1.7 fusion.48
  589.2 2.5 collective-permute-start.22
  595.7 5.7 collective-permute-done.22
  (347 shorter events, 52.7 us)
Async XLA Ops:
  0.6 136.1 %copy-start = (f32[1,3072]{1,0:T(1,128)S(1)}, f32[1,3072]{1,0:T(1,128)}, u32[]{:S(2)}) copy-start(f32[1,3072]{1,0:T(1,128)} %param.30) | copy-start | bytes 36868
  0.7 13.5 %collective-permute-start = (bf16[288,768]{1,0:T(8,128)(2,1)}, bf16[288,768]{1,0:T(8,128)(2,1)S(1)}, u32[]{:S(2)}, u32[]{:S(2)}) collective-permute-start(bf16[288,768]{1,0:T(8,128)(2,1)} %bitcast.217), channel_id=1, source_target_pairs={{0,0},{1,4},{2,1},{3,5},{4,2},{5,6},{6,3},{7,7},{8,8},{9,12},{10,9... | collective-permute-start | bytes 1327112 | tf_op jit(solution)/shard_map/ppermute | solution.py:920
  3.9 116.2 %collective-permute-start.2 = (s32[18,64]{1,0:T(8,128)}, s32[18,64]{1,0:T(8,128)S(1)}, u32[]{:S(2)}, u32[]{:S(2)}) collective-permute-start(s32[18,64]{1,0:T(8,128)} %param.21), channel_id=1, source_target_pairs={{0,4},{4,0},{8,12},{12,8},{1,5},{5,1},{9,13},{13,9},{2,6},{6,2},{1... | collective-permute-start | bytes 13832 | tf_op jit(solution)/shard_map/ppermute | solution.py:888
  6.1 115.0 %copy-start.76 = (f32[768]{0:T(1024)}, f32[768]{0:T(1024)S(1)}, u32[]{:S(2)}) copy-start(f32[768]{0:T(1024)S(1)} %get-tuple-element.142) | copy-start | bytes 9220
  14.2 106.1 %collective-permute-start.1 = (bf16[288,768]{1,0:T(8,128)(2,1)S(1)}, bf16[288,768]{1,0:T(8,128)(2,1)S(1)}, u32[]{:S(2)}, u32[]{:S(2)}) collective-permute-start(bf16[288,768]{1,0:T(8,128)(2,1)S(1)} %collective-permute-done), channel_id=1, source_target_pairs={{0,4},{4,0},{8,12},{12,8},{1,5},{5,1},{9,13},{13,9},{2,6},{6,2},{1... | collective-permute-start | bytes 1327112 | tf_op jit(solution)/shard_map/ppermute | solution.py:888
  17.8 103.3 %copy-start.84 = (f32[768]{0:T(1024)}, f32[768]{0:T(1024)S(1)}, u32[]{:S(2)}) copy-start(f32[768]{0:T(1024)S(1)} %get-tuple-element.145) | copy-start | bytes 9220
  17.9 102.2 %copy-start.83 = (s32[18,64]{1,0:T(8,128)S(1)}, s32[18,64]{1,0:T(8,128)}, u32[]{:S(2)}) copy-start(s32[18,64]{1,0:T(8,128)} %param.21) | copy-start | bytes 13828
  120.3 4.0 copy-start.47
  124.3 9.9 %copy-start.40 = (bf16[1,2,192,768]{3,2,1,0:T(8,128)(2,1)S(1)}, bf16[1,2,192,768]{3,2,1,0:T(8,128)(2,1)}, u32[]{:S(2)}) copy-start(bf16[1,2,192,768]{3,2,1,0:T(8,128)(2,1)} %get-tuple-element.80) | copy-start | bytes 1769476
  135.9 2.6 collective-permute-start.3
  136.8 7.9 %copy-start.78 = (f32[1536]{0:T(1024)}, f32[1536]{0:T(1024)S(1)}, u32[]{:S(2)}) copy-start(f32[1536]{0:T(1024)S(1)} %dynamic-slice_reduce_fusion) | copy-start | bytes 18436
  144.7 5.3 copy-start.102
  150.0 2.8 collective-permute-start.4
  150.1 5.4 copy-start.59
  157.8 13.6 %collective-permute-start.6 = (bf16[288,768]{1,0:T(8,128)(2,1)S(1)}, bf16[288,768]{1,0:T(8,128)(2,1)}, u32[]{:S(2)}, u32[]{:S(2)}) collective-permute-start(bf16[288,768]{1,0:T(8,128)(2,1)S(1)} %constant_dynamic-slice_fusion.1), channel_id=1, source_target_pairs={{0,16},{1,17},{2,18},{3,19},{4,20},{5,21},{6,22},{7,23},{8,24},{9,... | collective-permute-start | bytes 1327112 | tf_op jit(solution)/shard_map/ppermute | solution.py:955
  171.4 11.0 %collective-permute-start.7 = (bf16[288,768]{1,0:T(8,128)(2,1)}, bf16[288,768]{1,0:T(8,128)(2,1)}, u32[]{:S(2)}, u32[]{:S(2)}) collective-permute-start(bf16[288,768]{1,0:T(8,128)(2,1)} %collective-permute-done.6), channel_id=1, source_target_pairs={{0,1},{1,0},{2,3},{3,2},{4,5},{5,4},{6,7},{7,6},{8,9},{9,8},{10,11... | collective-permute-start | bytes 1327112 | tf_op jit(solution)/shard_map/ppermute | solution.py:956
  184.2 6.9 %collective-permute-start.8 = (bf16[2,288,768]{2,1,0:T(8,128)(2,1)S(1)}, bf16[2,288,768]{2,1,0:T(8,128)(2,1)S(1)}, u32[]{:S(2)}, u32[]{:S(2)}) collective-permute-start(bf16[2,288,768]{2,1,0:T(8,128)(2,1)S(1)} %maximum_select_fusion.2), channel_id=1, source_target_pairs={{0,4},{4,0},{8,12},{12,8},{1,5},{5,1},{9,13},{13,9},{2,6},{6,2},{1... | collective-permute-start | bytes 2654216 | tf_op jit(solution)/shard_map/ppermute | solution.py:888
  186.1 2.7 collective-permute-start.5
  186.2 3.4 copy-start.28
  188.8 5.0 copy-start.24
  207.3 15.5 %collective-permute-start.9 = (bf16[576,768]{1,0:T(8,128)(2,1)S(1)}, bf16[576,768]{1,0:T(8,128)(2,1)S(1)}, u32[]{:S(2)}, u32[]{:S(2)}) collective-permute-start(bf16[576,768]{1,0:T(8,128)(2,1)S(1)} %reduce-precision_convert_fusion.5), channel_id=1, source_target_pairs={{0,4},{4,0},{8,12},{12,8},{1,5},{5,1},{9,13},{13,9},{2,6},{6,2},{1... | collective-permute-start | bytes 2654216 | tf_op jit(solution)/shard_map/ppermute | solution.py:888
  207.8 11.9 %collective-permute-start.12 = (bf16[288,768]{1,0:T(8,128)(2,1)S(1)}, bf16[288,768]{1,0:T(8,128)(2,1)S(1)}, u32[]{:S(2)}, u32[]{:S(2)}) collective-permute-start(bf16[288,768]{1,0:T(8,128)(2,1)S(1)} %bitcast.218), channel_id=1, source_target_pairs={{0,0},{1,4},{2,1},{3,5},{4,2},{5,6},{6,3},{7,7},{8,8},{9,12},{10,9... | collective-permute-start | bytes 1327112 | tf_op jit(solution)/shard_map/ppermute | solution.py:921
  219.7 7.7 %copy-start.16 = (bf16[288,768]{1,0:T(8,128)(2,1)}, bf16[288,768]{1,0:T(8,128)(2,1)S(1)}, u32[]{:S(2)}) copy-start(bf16[288,768]{1,0:T(8,128)(2,1)S(1)} %collective-permute-done.12) | copy-start | bytes 1327108
  219.7 7.7 %collective-permute-start.13 = (bf16[288,768]{1,0:T(8,128)(2,1)S(1)}, bf16[288,768]{1,0:T(8,128)(2,1)S(1)}, u32[]{:S(2)}, u32[]{:S(2)}) collective-permute-start(bf16[288,768]{1,0:T(8,128)(2,1)S(1)} %collective-permute-done.12), channel_id=1, source_target_pairs={{0,4},{4,0},{8,12},{12,8},{1,5},{5,1},{9,13},{13,9},{2,6},{6,2},{1... | collective-permute-start | bytes 1327112 | tf_op jit(solution)/shard_map/ppermute | solution.py:888
  227.4 6.5 %copy-start.106 = (f32[576,768]{1,0:T(8,128)}, f32[576,768]{1,0:T(8,128)S(1)}, u32[]{:S(2)}) copy-start(f32[576,768]{1,0:T(8,128)S(1)} %fusion.44) | copy-start | bytes 5308420
  229.5 4.5 copy-start.18
  237.0 2.8 collective-permute-start.14
  238.4 5.0 copy-start.3
  238.4 5.0 copy-start.17
  238.4 5.0 copy-start.19
  238.4 5.0 copy-start.56
  243.4 4.1 copy-start.25
  272.1 4.0 copy-start.8
  272.1 4.0 copy-start.44
  272.1 4.7 collective-permute-start.15
  276.0 14.1 %collective-permute-start.10 = (bf16[576,768]{1,0:T(8,128)(2,1)S(1)}, bf16[576,768]{1,0:T(8,128)(2,1)S(1)}, u32[]{:S(2)}, u32[]{:S(2)}) collective-permute-start(bf16[576,768]{1,0:T(8,128)(2,1)S(1)} %reduce-precision_convert_fusion.4), channel_id=1, source_target_pairs={{0,4},{4,0},{8,12},{12,8},{1,5},{5,1},{9,13},{13,9},{2,6},{6,2},{1... | collective-permute-start | bytes 2654216 | tf_op jit(solution)/shard_map/ppermute | solution.py:888
  277.2 11.4 %collective-permute-start.16 = (bf16[288,768]{1,0:T(8,128)(2,1)S(1)}, bf16[288,768]{1,0:T(8,128)(2,1)S(1)}, u32[]{:S(2)}, u32[]{:S(2)}) collective-permute-start(bf16[288,768]{1,0:T(8,128)(2,1)S(1)} %dynamic-slice_bitcast_fusion.1), channel_id=1, source_target_pairs={{0,1},{1,0},{2,3},{3,2},{4,5},{5,4},{6,7},{7,6},{8,9},{9,8},{10,11... | collective-permute-start | bytes 1327112 | tf_op jit(solution)/shard_map/ppermute | solution.py:1007
  278.7 11.4 %copy-start.4 = (f32[576,768]{1,0:T(8,128)S(1)}, f32[576,768]{1,0:T(8,128)}, u32[]{:S(2)}) copy-start(f32[576,768]{1,0:T(8,128)} %copy-done.2) | copy-start | bytes 5308420
  278.7 11.4 %copy-start.26 = (bf16[576,768]{1,0:T(8,128)(2,1)S(1)}, bf16[576,768]{1,0:T(8,128)(2,1)}, u32[]{:S(2)}) copy-start(bf16[576,768]{1,0:T(8,128)(2,1)} %get-tuple-element.159) | copy-start | bytes 2654212
  278.7 11.4 %copy-start.60 = (f32[768]{0:T(1024)S(1)}, f32[768]{0:T(1024)}, u32[]{:S(2)}) copy-start(f32[768]{0:T(1024)} %copy-done.59) | copy-start | bytes 9220
  278.7 25.0 %collective-permute-start.19 = (bf16[576,768]{1,0:T(8,128)(2,1)S(1)}, bf16[576,768]{1,0:T(8,128)(2,1)S(1)}, u32[]{:S(2)}, u32[]{:S(2)}) collective-permute-start(bf16[576,768]{1,0:T(8,128)(2,1)S(1)} %reduce-precision_convert_fusion.2), channel_id=1, source_target_pairs={{0,4},{4,0},{8,12},{12,8},{1,5},{5,1},{9,13},{13,9},{2,6},{6,2},{1... | collective-permute-start | bytes 2654216 | tf_op jit(solution)/shard_map/ppermute | solution.py:888
  288.7 9.8 %collective-permute-start.17 = (bf16[288,768]{1,0:T(8,128)(2,1)S(1)}, bf16[288,768]{1,0:T(8,128)(2,1)S(1)}, u32[]{:S(2)}, u32[]{:S(2)}) collective-permute-start(bf16[288,768]{1,0:T(8,128)(2,1)S(1)} %fusion.56), channel_id=1, source_target_pairs={{16,0},{17,1},{18,2},{19,3},{20,4},{21,5},{22,6},{23,7},{24,8},{25... | collective-permute-start | bytes 1327112 | tf_op jit(solution)/shard_map/ppermute | solution.py:1009
  290.4 10.0 %copy-start.29 = (bf16[576,768]{1,0:T(8,128)(2,1)S(1)}, bf16[576,768]{1,0:T(8,128)(2,1)}, u32[]{:S(2)}) copy-start(bf16[576,768]{1,0:T(8,128)(2,1)} %copy-done.27) | copy-start | bytes 2654212
  290.4 13.4 %collective-permute-start.11 = (bf16[288,768]{1,0:T(8,128)(2,1)S(1)}, bf16[288,768]{1,0:T(8,128)(2,1)S(1)}, u32[]{:S(2)}, u32[]{:S(2)}) collective-permute-start(bf16[288,768]{1,0:T(8,128)(2,1)S(1)} %fusion.55), channel_id=1, source_target_pairs={{0,0},{4,1},{1,2},{5,3},{2,4},{6,5},{3,6},{7,7},{8,8},{12,9},{9,10... | collective-permute-start | bytes 1327112 | tf_op jit(solution)/shard_map/ppermute | solution.py:970
  298.5 5.2 collective-permute-start.18
  308.1 5.5 copy-start.35
  308.1 5.5 copy-start.37
  313.6 3.6 copy-start.91
  319.0 5.7 copy-start.50
  319.0 5.6 collective-permute-start.20
  343.9 4.0 copy-start.61
  343.9 4.0 copy-start.68
  343.9 4.0 copy-start.67
  344.0 4.0 copy-start.10
  344.0 4.0 copy-start.45
  347.4 6.6 %collective-permute-start.21 = (bf16[576,768]{1,0:T(8,128)(2,1)S(1)}, bf16[576,768]{1,0:T(8,128)(2,1)S(1)}, u32[]{:S(2)}, u32[]{:S(2)}) collective-permute-start(bf16[576,768]{1,0:T(8,128)(2,1)S(1)} %reduce-precision_convert_fusion), channel_id=1, source_target_pairs={{0,4},{4,0},{8,12},{12,8},{1,5},{5,1},{9,13},{13,9},{2,6},{6,2},{1... | collective-permute-start | bytes 2654216 | tf_op jit(solution)/shard_map/ppermute | solution.py:888
  575.1 5.4 copy-start.46
  575.1 6.1 %copy-start.30 = (bf16[4,192,384]{2,1,0:T(8,128)(2,1)S(1)}, bf16[4,192,384]{2,1,0:T(8,128)(2,1)}, u32[]{:S(2)}) copy-start(bf16[4,192,384]{2,1,0:T(8,128)(2,1)} %get-tuple-element.97) | copy-start | bytes 1769476
  580.5 3.6 copy-start.31
  580.5 3.6 copy-start.32
  582.1 12.5 %collective-permute-start.23 = (bf16[2,192,192]{2,1,0:T(8,128)(2,1)}, bf16[2,192,192]{2,1,0:T(8,128)(2,1)}, u32[]{:S(2)}, u32[]{:S(2)}) collective-permute-start(bf16[2,192,192]{2,1,0:T(8,128)(2,1)} %slice.250), channel_id=1, source_target_pairs={{16,0},{17,1},{18,2},{19,3},{20,4},{21,5},{22,6},{23,7},{24,8},{25... | collective-permute-start | bytes 442376 | tf_op jit(solution)/shard_map/ppermute | solution.py:1092
  589.2 12.2 %collective-permute-start.22 = (bf16[288,768]{1,0:T(8,128)(2,1)S(1)}, bf16[288,768]{1,0:T(8,128)(2,1)S(1)}, u32[]{:S(2)}, u32[]{:S(2)}) collective-permute-start(bf16[288,768]{1,0:T(8,128)(2,1)S(1)} %fusion.48), channel_id=1, source_target_pairs={{0,0},{4,1},{1,2},{5,3},{2,4},{6,5},{3,6},{7,7},{8,8},{12,9},{9,10... | collective-permute-start | bytes 1327112 | tf_op jit(solution)/shard_map/ppermute | solution.py:1055
  593.0 8.5 %copy-start.43 = (bf16[288,768]{1,0:T(8,128)(2,1)S(1)}, bf16[288,768]{1,0:T(8,128)(2,1)}, u32[]{:S(2)}) copy-start(bf16[288,768]{1,0:T(8,128)(2,1)} %copy-done.42) | copy-start | bytes 1327108
  594.7 8.3 %copy-start.1 = (f32[1,3072]{1,0:T(1,128)S(1)}, f32[1,3072]{1,0:T(1,128)}, u32[]{:S(2)}) copy-start(f32[1,3072]{1,0:T(1,128)} %param.30) | copy-start | bytes 36868
  (68 other events, 137.1 us)

commit v2 on v1

--- a/solution.py
+++ b/solution.py
@@ -300,56 +300,39 @@
     )(picks, queries, keys, vals, grads, tops)
 
 
-def gather_kernel(pieces, n_src, *refs):
-    srcs = refs[:n_src]
-    outs = refs[n_src : 2 * n_src]
-    stages = refs[2 * n_src : 3 * n_src]
-    send_sem, recv_sem, local_sem, twin_send, twin_recv, = refs[3 * n_src :]
+def spots():
     tower = lax.axis_index("tower")
     dp = lax.axis_index("dp")
     z = lax.axis_index("mp")
     core = lax.rem(dp, 2)
     line = dp // 2
+    return tower, dp, z, core, line, dp + 2 - 4 * line, dp + 1 - 2 * core
+
+
+def greet(target):
+    pl.semaphore_signal(pltpu.get_barrier_semaphore(), inc=1, device_id=target, device_id_type=MESH)
+
+
+def weight_steps(pieces, srcs, outs, stages, sems):
+    send_sem, recv_sem, local_sem, twin_send, twin_recv = sems
+    tower, dp, z, core, line, other, partner = spots()
     place = z + core * (3 - 2 * z)
     ahead = z + 1 - 2 * core
     behind = z - 1 + 2 * core
-    other = dp + 2 - 4 * line
     slot_of = (core, 1 - core)
-    is_text = tower == 1
-    cross = n_src - 1
-
-    barrier = pltpu.get_barrier_semaphore()
-
-    @pl.when(z > 0)
-    def _():
-        pl.semaphore_signal(barrier, inc=1, device_id={"mp": z - 1}, device_id_type=MESH)
-
-    @pl.when(z < 3)
-    def _():
-        pl.semaphore_signal(barrier, inc=1, device_id={"mp": z + 1}, device_id_type=MESH)
-
-    pl.semaphore_signal(barrier, inc=1, device_id={"dp": other}, device_id_type=MESH)
-    pl.semaphore_signal(barrier, inc=1, device_id={"tower": 1 - tower}, device_id_type=MESH)
-
-    @pl.when(jnp.logical_or(z == 0, z == 3))
-    def _():
-        pl.semaphore_wait(barrier, 3)
-
-    @pl.when(jnp.logical_and(z > 0, z < 3))
-    def _():
-        pl.semaphore_wait(barrier, 4)
+    holder = place <= 1
+    far_src = [p[0] for p in pieces if p[5]]
 
     def spot(piece, slot, half):
-        which, first, start, size, far = piece
+        which, first, start, size, _, _ = piece
         part = size // 2
-        count = srcs[which].shape[0]
-        return outs[which].at[pl.ds(first, count), slot, pl.ds(start + half * part, part), :]
+        return outs[which].at[pl.ds(first, srcs[which].shape[0]), slot, pl.ds(start + half * part, part), :]
 
     def own(piece):
-        which, first, start, size, far = piece
+        which, first, start, size, _, far = piece
         part = size // 2
         if far:
-            return outs[which].at[pl.ds(first, srcs[which].shape[0]), lax.rem(z, 2), pl.ds(start + line * part, part), :]
+            return spot(piece, lax.rem(z, 2), line)
         return srcs[which].at[:, pl.ds(start + line * part, part), :]
 
     def move(k, source, slot, half, kind, arrive, target):
@@ -363,32 +346,27 @@
         )
 
     def twin_copy():
-        slot = lax.rem(z, 2)
+        which = far_src[0]
         return pltpu.make_async_remote_copy(
-            src_ref=srcs[cross],
-            dst_ref=outs[cross].at[pl.ds(0, srcs[cross].shape[0]), slot],
+            src_ref=srcs[which],
+            dst_ref=outs[which].at[pl.ds(0, srcs[which].shape[0]), lax.rem(z, 2)],
             send_sem=twin_send,
             recv_sem=twin_recv,
             device_id={"tower": 1 - tower},
             device_id_type=MESH,
         )
 
-    holder = place <= 1
-
-    @pl.when(jnp.logical_and(holder, tower == 0))
-    def _():
-        twin_copy().start()
-
     def local_in(i):
         return pltpu.make_async_copy(srcs[i], stages[i], local_sem.at[i, 0])
 
     def local_out(i):
         first = outs[i].shape[0] - srcs[i].shape[0]
-        return pltpu.make_async_copy(stages[i], outs[i].at[pl.ds(first, srcs[i].shape[0]), lax.rem(z, 2)], local_sem.at[i, 1])
+        return pltpu.make_async_copy(
+            stages[i], outs[i].at[pl.ds(first, srcs[i].shape[0]), lax.rem(z, 2)], local_sem.at[i, 1]
+        )
 
     def gate(piece, cond):
-        which = piece[0]
-        return jnp.logical_and(cond, is_text) if which == cross else cond
+        return cond if piece[4] is None else jnp.logical_and(cond, tower == piece[4])
 
     def send_own(k):
         piece = pieces[k]
@@ -402,23 +380,40 @@
             move(k, own(piece), slot_of[1], line, 1, 1, {"mp": ahead}).start()
             move(k, own(piece), slot_of[1], line, 2, 1, {"mp": behind}).start()
 
-    for k, piece in enumerate(pieces):
-        if not piece[4]:
-            send_own(k)
-
-    @pl.when(holder)
-    def _():
-        for i in range(n_src):
-            local_in(i).start()
-        for i in range(n_src):
-            local_in(i).wait()
-            local_out(i).start()
+    def begin():
+        if far_src:
+
+            @pl.when(jnp.logical_and(holder, tower == 0))
+            def _():
+                twin_copy().start()
+
+        for k, piece in enumerate(pieces):
+            if not piece[5]:
+                send_own(k)
+
+    def begin_local():
+        for i in range(len(srcs)):
+            flag = next(p[4] for p in pieces if p[0] == i)
+            keep = holder if flag is None else jnp.logical_and(holder, tower == flag)
+
+            @pl.when(keep)
+            def _(i=i):
+                local_in(i).start()
+
+        for i in range(len(srcs)):
+            flag = next(p[4] for p in pieces if p[0] == i)
+            keep = holder if flag is None else jnp.logical_and(holder, tower == flag)
+
+            @pl.when(keep)
+            def _(i=i):
+                local_in(i).wait()
+                local_out(i).start()
 
     def pass_on(k):
         piece = pieces[k]
-        if piece[4]:
-
-            @pl.when(jnp.logical_and(holder, is_text))
+        if piece[5]:
+
+            @pl.when(jnp.logical_and(holder, tower == 1))
             def _():
                 twin_copy().wait_recv()
 
@@ -446,90 +441,320 @@
             here = spot(piece, slot_of[1], line)
             move(k, here, slot_of[1], line, 1, 1, {"mp": ahead}).start()
 
+    def arrived(k):
+        piece = pieces[k]
+
+        @pl.when(gate(piece, place >= 1))
+        def _():
+            move(k, spot(piece, slot_of[0], 1 - line), slot_of[0], 1 - line, 3, 2, {"dp": dp}).wait_recv()
+
+        @pl.when(gate(piece, place != 1))
+        def _():
+            move(k, spot(piece, slot_of[1], 1 - line), slot_of[1], 1 - line, 4, 3, {"dp": dp}).wait_recv()
+
+    def sent(k):
+        piece = pieces[k]
+
+        @pl.when(gate(piece, place <= 2))
+        def _():
+            move(k, spot(piece, slot_of[0], line), slot_of[0], line, 0, 0, {"mp": z}).wait_send()
+
+        @pl.when(gate(piece, jnp.logical_and(place >= 1, place <= 2)))
+        def _():
+            move(k, spot(piece, slot_of[1], line), slot_of[1], line, 1, 1, {"mp": z}).wait_send()
+
+        @pl.when(gate(piece, place == 1))
+        def _():
+            move(k, spot(piece, slot_of[1], line), slot_of[1], line, 2, 1, {"mp": z}).wait_send()
+
+        @pl.when(gate(piece, place >= 1))
+        def _():
+            move(k, spot(piece, slot_of[0], line), slot_of[0], line, 3, 2, {"dp": dp}).wait_send()
+
+        @pl.when(gate(piece, place != 1))
+        def _():
+            move(k, spot(piece, slot_of[1], line), slot_of[1], line, 4, 3, {"dp": dp}).wait_send()
+
+    def end_local():
+        for i in range(len(srcs)):
+            flag = next(p[4] for p in pieces if p[0] == i)
+            keep = holder if flag is None else jnp.logical_and(holder, tower == flag)
+
+            @pl.when(keep)
+            def _(i=i):
+                local_out(i).wait()
+
+        if far_src:
+
+            @pl.when(jnp.logical_and(holder, tower == 0))
+            def _():
+                twin_copy().wait_send()
+
+    return begin, begin_local, pass_on, arrived, sent, end_local
+
+
+def token_steps(blocks, outs, stage, sems):
+    send_sem, recv_sem, local_sem = sems
+    tower, dp, z, core, line, other, partner = spots()
+    stays = z == 3 * core
+    size = blocks[0].shape[0]
+
+    def rows(which_core):
+        return pl.ds(pl.multiple_of(which_core * size, 16), size)
+
+    def away(i):
+        target = {"dp": 2 * line + lax.rem(z, 2), "mp": 2 * core + z // 2}
+        return pltpu.make_async_remote_copy(
+            src_ref=blocks[i],
+            dst_ref=outs[i].at[rows(lax.rem(z, 2)), :],
+            send_sem=send_sem.at[i, 0],
+            recv_sem=recv_sem.at[i, 0],
+            device_id=target,
+            device_id_type=MESH,
+        )
+
+    def across(i, which_core):
+        return pltpu.make_async_remote_copy(
+            src_ref=outs[i].at[rows(which_core), :],
+            dst_ref=outs[i].at[rows(which_core), :],
+            send_sem=send_sem.at[i, 1],
+            recv_sem=recv_sem.at[i, 1],
+            device_id={"dp": partner},
+            device_id_type=MESH,
+        )
+
+    def begin(i):
+        @pl.when(jnp.logical_not(stays))
+        def _():
+            away(i).start()
+
+        @pl.when(stays)
+        def _():
+            first = pltpu.make_async_copy(blocks[i], stage.at[i], local_sem.at[i, 0])
+            first.start()
+            first.wait()
+            second = pltpu.make_async_copy(stage.at[i], outs[i].at[rows(core), :], local_sem.at[i, 1])
+            second.start()
+            second.wait()
+            across(i, core).start()
+
+    def relay(i):
+        @pl.when(jnp.logical_not(stays))
+        def _():
+            away(i).wait_recv()
+            across(i, core).start()
+
+    def finish(i):
+        across(i, 1 - core).wait_recv()
+        across(i, core).wait_send()
+
+        @pl.when(jnp.logical_not(stays))
+        def _():
+            away(i).wait_send()
+
+    return begin, relay, finish
+
+
+def gather_kernel(pieces, n_src, *refs):
+    it = iter(refs)
+    srcs = [next(it) for _ in range(n_src)]
+    blocks = [next(it) for _ in range(2)]
+    notes = next(it)
+    outs = [next(it) for _ in range(n_src)]
+    tokens = [next(it) for _ in range(2)]
+    notes_out = next(it)
+    stages = [next(it) for _ in range(n_src)]
+    weight_sems = [next(it) for _ in range(5)]
+    token_stage = next(it)
+    token_sems = [next(it) for _ in range(3)]
+    note_sem = next(it)
+    tower, dp, z, core, line, other, partner = spots()
+    stays = z == 3 * core
+
+    @pl.when(z > 0)
+    def _():
+        greet({"mp": z - 1})
+
+    @pl.when(z < 3)
+    def _():
+        greet({"mp": z + 1})
+
+    greet({"dp": other})
+    greet({"tower": 1 - tower})
+    greet({"dp": partner})
+
+    @pl.when(jnp.logical_not(stays))
+    def _():
+        greet({"dp": 2 * line + lax.rem(z, 2), "mp": 2 * core + z // 2})
+        greet({"dp": 2 * line + z // 2, "mp": 2 * lax.rem(z, 2) + core})
+
+    at_end = jnp.logical_or(z == 0, z == 3)
+
+    @pl.when(stays)
+    def _():
+        pl.semaphore_wait(pltpu.get_barrier_semaphore(), 4)
+
+    @pl.when(jnp.logical_and(at_end, jnp.logical_not(stays)))
+    def _():
+        pl.semaphore_wait(pltpu.get_barrier_semaphore(), 6)
+
+    @pl.when(jnp.logical_not(at_end))
+    def _():
+        pl.semaphore_wait(pltpu.get_barrier_semaphore(), 7)
+
+    begin, begin_local, pass_on, arrived, sent, end_local = weight_steps(pieces, srcs, outs, stages, weight_sems)
+    token_begin, token_relay, token_finish = token_steps(blocks, tokens, token_stage, token_sems)
+    note_copy = pltpu.make_async_remote_copy(
+        src_ref=notes,
+        dst_ref=notes_out,
+        send_sem=note_sem.at[0],
+        recv_sem=note_sem.at[1],
+        device_id={"dp": partner},
+        device_id_type=MESH,
+    )
+    note_copy.start()
+    token_begin(0)
+    begin()
+    token_begin(1)
+    begin_local()
+    token_relay(0)
     for k in range(len(pieces)):
         pass_on(k)
-
-    def finish(k):
-        piece = pieces[k]
-
-        @pl.when(gate(piece, place <= 2))
-        def _():
-            move(k, spot(piece, slot_of[0], line), slot_of[0], line, 0, 0, {"mp": z}).wait_send()
-
-        @pl.when(gate(piece, jnp.logical_and(place >= 1, place <= 2)))
-        def _():
-            move(k, spot(piece, slot_of[1], line), slot_of[1], line, 1, 1, {"mp": z}).wait_send()
-
-        @pl.when(gate(piece, place == 1))
-        def _():
-            move(k, spot(piece, slot_of[1], line), slot_of[1], line, 2, 1, {"mp": z}).wait_send()
-
-        @pl.when(gate(piece, place >= 1))
-        def _():
-            made = move(k, spot(piece, slot_of[0], 1 - line), slot_of[0], 1 - line, 3, 2, {"dp": dp})
-            made.wait_send()
-            made.wait_recv()
-
-        @pl.when(gate(piece, place != 1))
-        def _():
-            made = move(k, spot(piece, slot_of[1], 1 - line), slot_of[1], 1 - line, 4, 3, {"dp": dp})
-            made.wait_send()
-            made.wait_recv()
-
+        if k == 1:
+            token_relay(1)
     for k in range(len(pieces)):
-        finish(k)
-
-    @pl.when(holder)
+        arrived(k)
+        sent(k)
+    end_local()
+    token_finish(0)
+    token_finish(1)
+    note_copy.wait()
+
+
+def later_kernel(pieces, n_src, only, *refs):
+    srcs = refs[:n_src]
+    outs = refs[2 * n_src : 3 * n_src]
+    stages = refs[3 * n_src : 4 * n_src]
+    weight_sems = refs[4 * n_src :]
+
+    @pl.when(lax.axis_index("tower") == only)
     def _():
-        for i in range(n_src):
-            local_out(i).wait()
-
-    @pl.when(jnp.logical_and(holder, tower == 0))
-    def _():
-        twin_copy().wait_send()
-
-
-def gather_weights(shards):
+        tower, dp, z, core, line, other, partner = spots()
+
+        @pl.when(z > 0)
+        def _():
+            greet({"mp": z - 1})
+
+        @pl.when(z < 3)
+        def _():
+            greet({"mp": z + 1})
+
+        greet({"dp": other})
+
+        @pl.when(jnp.logical_or(z == 0, z == 3))
+        def _():
+            pl.semaphore_wait(pltpu.get_barrier_semaphore(), 2)
+
+        @pl.when(jnp.logical_and(z > 0, z < 3))
+        def _():
+            pl.semaphore_wait(pltpu.get_barrier_semaphore(), 3)
+
+        begin, begin_local, pass_on, arrived, sent, end_local = weight_steps(
+            pieces, srcs, outs, stages, weight_sems
+        )
+        begin()
+        begin_local()
+        for k in range(len(pieces)):
+            pass_on(k)
+        for k in range(len(pieces)):
+            arrived(k)
+            sent(k)
+        end_local()
+
+
+def weight_scratch(n, shards):
+    return [pltpu.VMEM(s.shape, BF16) for s in shards] + [
+        pltpu.SemaphoreType.DMA((n, 5)),
+        pltpu.SemaphoreType.DMA((n, 4)),
+        pltpu.SemaphoreType.DMA((len(shards), 2)),
+        pltpu.SemaphoreType.DMA,
+        pltpu.SemaphoreType.DMA,
+    ]
+
+
+def row_cuts(i, shard, flag):
+    rows = shard.shape[1]
+    cut = rows if rows <= 192 else rows // 2
+    return [(i, 0, at, cut, flag, False) for at in range(0, rows, cut)]
+
+
+def gather_weights(shards, blocks, notes):
+    qkv, out, cross, ffn_in, ffn_out = shards
     n_src = len(shards)
+    pieces = row_cuts(0, qkv, None) + row_cuts(1, out, None)
+    pieces += [(2, cross.shape[0], 0, cross.shape[1], 1, False), (2, 0, 0, cross.shape[1], 1, True)]
+    pieces += row_cuts(3, ffn_in, 0) + row_cuts(4, ffn_out, 0)
     outs = [
-        jax.ShapeDtypeStruct(((2 if i == n_src - 1 else 1) * s.shape[0], 2) + s.shape[1:], BF16)
-        for i, s in enumerate(shards)
+        jax.ShapeDtypeStruct(((2 if i == 2 else 1) * s.shape[0], 2) + s.shape[1:], BF16) for i, s in enumerate(shards)
     ]
-    pieces = []
-    for i, s in enumerate(shards):
-        rows = s.shape[1]
-        if i == n_src - 1:
-            pieces.append((i, s.shape[0], 0, rows, False))
-            pieces.insert(2, (i, 0, 0, rows, True))
-        else:
-            cut = rows if rows <= 192 else rows // 2
-            pieces += [(i, 0, at, cut, False) for at in range(0, rows, cut)]
-    n = len(pieces)
-    any_spec = pl.BlockSpec(memory_space=pl.ANY)
+    outs += [jax.ShapeDtypeStruct((2 * b.shape[0], b.shape[1]), b.dtype) for b in blocks]
+    outs += [jax.ShapeDtypeStruct(notes.shape, notes.dtype)]
+    any_spec = pl.BlockSpec(memory_space=pltpu.HBM)
     return pl.pallas_call(
         functools.partial(gather_kernel, tuple(pieces), n_src),
-        in_specs=[any_spec] * n_src,
-        out_specs=[any_spec] * n_src,
+        in_specs=[any_spec] * (n_src + 3),
+        out_specs=[any_spec] * (n_src + 3),
         out_shape=outs,
-        scratch_shapes=[pltpu.VMEM(s.shape, BF16) for s in shards]
+        scratch_shapes=weight_scratch(len(pieces), shards)
         + [
-            pltpu.SemaphoreType.DMA((n, 5)),
-            pltpu.SemaphoreType.DMA((n, 4)),
-            pltpu.SemaphoreType.DMA((n_src, 2)),
-            pltpu.SemaphoreType.DMA,
-            pltpu.SemaphoreType.DMA,
+            pltpu.VMEM((2,) + blocks[0].shape, BF16),
+            pltpu.SemaphoreType.DMA((2, 2)),
+            pltpu.SemaphoreType.DMA((2, 2)),
+            pltpu.SemaphoreType.DMA((2, 2)),
+            pltpu.SemaphoreType.DMA((2,)),
         ],
         compiler_params=pltpu.CompilerParams(
             collective_id=0, has_side_effects=True, vmem_limit_bytes=VMEM_LIMIT
         ),
         name="gather_weights",
-    )(*shards)
+    )(*shards, *blocks, notes)
+
+
+def gather_later(shards, filled):
+    n_src = len(shards)
+    pieces = []
+    for i, s in enumerate(shards):
+        pieces += row_cuts(i, s, None)
+    any_spec = pl.BlockSpec(memory_space=pltpu.HBM)
+    return pl.pallas_call(
+        functools.partial(later_kernel, tuple(pieces), n_src, 1),
+        in_specs=[any_spec] * (2 * n_src),
+        out_specs=[any_spec] * n_src,
+        out_shape=[jax.ShapeDtypeStruct(f.shape, f.dtype) for f in filled],
+        input_output_aliases={n_src + i: i for i in range(n_src)},
+        scratch_shapes=weight_scratch(len(pieces), shards),
+        compiler_params=pltpu.CompilerParams(
+            collective_id=3, has_side_effects=True, vmem_limit_bytes=VMEM_LIMIT
+        ),
+        name="gather_later",
+    )(*shards, *filled)
 
 
 TILE = 32
-
-
-def reduce_kernel(pieces, flags, n_src, with_smalls, *refs):
+WINDOW = 2
+
+
+def reduce_kernel(pieces, flags, n_src, with_smalls, only, *refs):
+    if only is None:
+        reduce_steps(pieces, flags, n_src, with_smalls, refs)
+    else:
+
+        @pl.when(lax.axis_index("tower") == only)
+        def _():
+            reduce_steps(pieces, flags, n_src, with_smalls, refs)
+
+
+def reduce_steps(pieces, flags, n_src, with_smalls, refs):
     it = iter(refs)
     srcs = [next(it) for _ in range(n_src)]
     small_in = next(it) if with_smalls else None
@@ -560,28 +785,26 @@
         pl.semaphore_signal(barrier, inc=1, device_id={"mp": lax.rem(z + away, 4)}, device_id_type=MESH)
     pl.semaphore_wait(barrier, 5)
 
-    def gate(piece, cond=None):
-        flag = flags[piece[0]]
-        if flag is None:
-            return cond
-        here = tower == flag
-        return here if cond is None else jnp.logical_and(cond, here)
-
-    def guarded(cond, run):
+    def guarded(k, run, cond=None):
+        flag = flags[pieces[k][0]]
+        if flag is not None:
+            here = tower == flag
+            cond = here if cond is None else jnp.logical_and(cond, here)
         if cond is None:
             run()
         else:
             pl.when(cond)(run)
 
-    def rows_of(piece):
-        return pl.ds(piece[1], piece[2])
+    def cut(k):
+        _, first, count, start, size = pieces[k]
+        return (pl.ds(first, count), pl.ds(start, size))
 
     def to_line(k):
         which = pieces[k][0]
-        rows = rows_of(pieces[k])
+        span, rows = cut(k)
         return pltpu.make_async_remote_copy(
-            src_ref=srcs[which].at[:, :, rows, pl.ds(pl.multiple_of((1 - line) * half, LANES), half)],
-            dst_ref=near[which].at[:, :, rows, :],
+            src_ref=srcs[which].at[span, :, rows, pl.ds(pl.multiple_of((1 - line) * half, LANES), half)],
+            dst_ref=near[which].at[span, :, rows, :],
             send_sem=y_send.at[k],
             recv_sem=y_recv.at[k],
             device_id={"dp": other},
@@ -590,32 +813,31 @@
 
     def to_mine(k):
         which = pieces[k][0]
-        rows = rows_of(pieces[k])
+        span, rows = cut(k)
         return pltpu.make_async_copy(
-            srcs[which].at[:, :, rows, pl.ds(pl.multiple_of(line * half, LANES), half)],
-            mine[which].at[:, :, rows, :],
+            srcs[which].at[span, :, rows, pl.ds(pl.multiple_of(line * half, LANES), half)],
+            mine[which].at[span, :, rows, :],
             local_sem.at[k],
         )
 
     def to_chip(k, shard, seat):
         which = pieces[k][0]
-        rows = rows_of(pieces[k])
-        target = 2 * core + shard
+        span, rows = cut(k)
         return pltpu.make_async_remote_copy(
-            src_ref=mine[which].at[:, shard, rows, :],
-            dst_ref=far[which].at[seat, :, rows, :],
+            src_ref=mine[which].at[span, shard, rows, :],
+            dst_ref=far[which].at[seat, span, rows, :],
             send_sem=z_send.at[k, shard],
             recv_sem=z_recv.at[k, seat],
-            device_id={"mp": target},
+            device_id={"mp": 2 * core + shard},
             device_id_type=MESH,
         )
 
     def to_core(k):
         which = pieces[k][0]
-        rows = rows_of(pieces[k])
+        span, rows = cut(k)
         return pltpu.make_async_remote_copy(
-            src_ref=outs[which].at[:, rows, :],
-            dst_ref=outs[which].at[:, rows, :],
+            src_ref=outs[which].at[span, rows, :],
+            dst_ref=outs[which].at[span, rows, :],
             send_sem=c_send.at[k],
             recv_sem=c_recv.at[k],
             device_id={"dp": partner},
@@ -625,13 +847,30 @@
     def seat_of(shard):
         return lax.rem(z - (2 * core + shard) + 4, 4) - 1
 
-    for k, piece in enumerate(pieces):
-
-        def begin(k=k):
+    towers = [0, 1] if any(f is not None for f in flags) else [None]
+    lists = []
+    for t in towers:
+        lists.append([k for k in range(len(pieces)) if t is None or flags[pieces[k][0]] in (None, t)])
+
+    def start_line(t, place):
+        chosen = lists[towers.index(t)]
+        if place >= len(chosen):
+            return
+        k = chosen[place]
+
+        def run():
             to_line(k).start()
-            to_mine(k).start()
-
-        guarded(gate(piece), begin)
+
+        if t is None:
+            run()
+        else:
+            pl.when(tower == t)(run)
+
+    for t in towers:
+        for place in range(WINDOW):
+            start_line(t, place)
+    for k in range(len(pieces)):
+        guarded(k, lambda k=k: to_mine(k).start())
 
     if with_smalls:
         small_line = pltpu.make_async_remote_copy(
@@ -644,18 +883,7 @@
         )
         small_line.start()
 
-        def small_move(away):
-            return pltpu.make_async_remote_copy(
-                src_ref=small_all.at[z],
-                dst_ref=small_all.at[z],
-                send_sem=small_sem.at[1 + away],
-                recv_sem=small_sem.at[4 + away],
-                device_id={"mp": lax.rem(z + away, 4)},
-                device_id_type=MESH,
-            )
-
-        def small_got(away):
-            sender = lax.rem(z + 4 - away, 4)
+        def small_pair(sender, away):
             return pltpu.make_async_remote_copy(
                 src_ref=small_all.at[sender],
                 dst_ref=small_all.at[sender],
@@ -664,6 +892,12 @@
                 device_id={"mp": lax.rem(z + away, 4)},
                 device_id_type=MESH,
             )
+
+        def small_move(away):
+            return small_pair(z, away)
+
+        def small_got(away):
+            return small_pair(lax.rem(z + 4 - away, 4), away)
 
         def small_core(which):
             return pltpu.make_async_remote_copy(
@@ -679,17 +913,20 @@
         small_all[z] = small_in[...] + small_near[...]
 
     for k, piece in enumerate(pieces):
-        which, start, size = piece
-        count = srcs[which].shape[0]
-
-        def add_near(k=k, which=which, start=start, size=size, count=count):
+        which, first, count, start, size = piece
+
+        def add_near(k=k, which=which, first=first, count=count, start=start, size=size):
             to_mine(k).wait()
             to_line(k).wait_recv()
+            to_line(k).wait_send()
+            for t, chosen in zip(towers, lists):
+                if k in chosen:
+                    start_line(t, chosen.index(k) + WINDOW)
 
             @pl.loop(0, size // TILE)
             def _(i):
                 rows = pl.ds(pl.multiple_of(start + i * TILE, TILE), TILE)
-                for a in range(count):
+                for a in range(first, first + count):
                     for b in range(2):
                         total = mine[which][a, b, rows, :].astype(F32) + near[which][a, b, rows, :].astype(F32)
                         mine[which][a, b, rows, :] = total.astype(BF16)
@@ -700,23 +937,22 @@
                 def _(shard=shard):
                     to_chip(k, shard, seat_of(shard)).start()
 
-        guarded(gate(piece), add_near)
+        guarded(k, add_near)
         if with_smalls and k == 0:
             for away in range(1, 4):
                 small_move(away).start()
 
     for k, piece in enumerate(pieces):
-        which, start, size = piece
-        count = srcs[which].shape[0]
-
-        def add_far(k=k, which=which, start=start, size=size, count=count):
+        which, first, count, start, size = piece
+
+        def add_far(k=k, which=which, first=first, count=count, start=start, size=size):
             for seat in range(3):
                 to_chip(k, 0, seat).wait_recv()
 
             @pl.loop(0, size // TILE)
             def _(i):
                 rows = pl.ds(pl.multiple_of(start + i * TILE, TILE), TILE)
-                for a in range(count):
+                for a in range(first, first + count):
                     total = mine[which][a, slot, rows, :].astype(F32)
                     for seat in range(3):
                         total = total + far[which][seat, a, rows, :].astype(F32)
@@ -724,7 +960,7 @@
 
             to_core(k).start()
 
-        guarded(gate(piece, holder), add_far)
+        guarded(k, add_far, holder)
 
     if with_smalls:
         for away in range(1, 4):
@@ -735,7 +971,6 @@
     for k, piece in enumerate(pieces):
 
         def ended(k=k):
-            to_line(k).wait_send()
             for shard in range(2):
 
                 @pl.when(z != 2 * core + shard)
@@ -750,7 +985,7 @@
             def _():
                 to_core(k).wait_recv()
 
-        guarded(gate(piece), ended)
+        guarded(k, ended)
 
     if with_smalls:
         for away in range(1, 4):
@@ -759,13 +994,15 @@
         small_core(1 - core).wait_recv()
 
 
-def reduce_grads(grads, flags, smalls, collective_id):
+def reduce_grads(grads, flags, smalls, only, collective_id):
     n_src = len(grads)
     pieces = []
     for i, g in enumerate(grads):
         rows = g.shape[2]
-        cut = rows if rows <= 192 else rows // 2
-        pieces += [(i, at, cut) for at in range(0, rows, cut)]
+        cut = rows if rows <= 192 else rows // 4
+        pieces += [
+            (i, first, 1, at, cut) for first in range(g.shape[0]) for at in range(0, rows, cut)
+        ]
     n = len(pieces)
     half = grads[0].shape[3] // 2
     any_spec = pl.BlockSpec(memory_space=pl.ANY)
@@ -799,7 +1036,7 @@
         pltpu.SemaphoreType.DMA((n,)),
     ]
     return pl.pallas_call(
-        functools.partial(reduce_kernel, tuple(pieces), tuple(flags), n_src, with_smalls),
+        functools.partial(reduce_kernel, tuple(pieces), tuple(flags), n_src, with_smalls, only),
         in_specs=in_specs,
         out_specs=out_specs,
         out_shape=out_shape,
@@ -815,7 +1052,7 @@
     core = lax.rem(lax.axis_index("dp"), 2)
     outs = []
     for i, s in enumerate(shards):
-        if i == len(shards) - 1:
+        if i == 2:
             s = jnp.concatenate([lax.ppermute(s, "tower", [(0, 1)]), s], axis=0)
         full = lax.all_gather(s, "mp", axis=1, tiled=False)
         outs.append(lax.dynamic_slice_in_dim(full, 2 * core, 2, 1))
@@ -894,38 +1131,50 @@
     def own_rows(full):
         return lax.dynamic_slice_in_dim(full, core * quarter, quarter, full.ndim - 2)
 
+    def lowered(part):
+        return lax.reduce_precision(part, 8, 7).astype(BF16)
+
+    def add_lowered(low):
+        return low.astype(F32) + swap_cores(low).astype(F32)
+
     def add_cores(part):
-        low = lax.reduce_precision(part, 8, 7).astype(BF16)
-        return low.astype(F32) + swap_cores(low).astype(F32)
+        return add_lowered(lowered(part))
+
+    def only_image(run, *operands):
+        def idle(*inputs):
+            return jax.tree.map(lambda x: jnp.zeros(x.shape, x.dtype), jax.eval_shape(run, *inputs))
+
+        return lax.cond(is_enc, run, idle, *operands)
 
     shards = [
         jnp.swapaxes(attn_qkv[0], 1, 2),
         attn_out,
+        jnp.swapaxes(cross_proj[0], 1, 2),
         mlp_in,
         mlp_out,
-        jnp.swapaxes(cross_proj[0], 1, 2),
     ]
-    gathered = gather_weights(shards) if direct else gather_plain(shards)
+    notes = jnp.concatenate([segment_ids, row_image[:, None]], axis=1)
+    if direct:
+        *gathered, stream_low, cot_low, other_notes = gather_weights(shards, [tower_in[0], out_cot[0]], notes)
+    else:
+        gathered = gather_plain(shards)
+        stream_low = both_cores(lax.ppermute(tower_in[0], ("dp", "mp"), out_moves))
+        cot_low = both_cores(lax.ppermute(out_cot[0], ("dp", "mp"), out_moves))
+        other_notes = swap_cores(notes)
     w_qkv = gathered[0].reshape(3 * head_cols, width)
     w_out = gathered[1].reshape(head_cols, width)
-    w_in = gathered[2][0]
-    w_mlp = gathered[3].reshape(hidden, width)
-    w_cross = gathered[4].reshape(4, head_cols, width)
+    w_cross = gathered[2].reshape(4, head_cols, width)
     bias_qv = lax.dynamic_slice_in_dim(qv_bias[0], core * head_cols, head_cols, 1)
     bias_packed = jnp.concatenate([bias_qv[0], jnp.zeros_like(bias_qv[0]), bias_qv[1]])
     bias_in = lax.dynamic_slice_in_dim(mlp_bias_in[0], core * hidden, hidden, 0)
     gains = norm_gain[0]
     shifts = norm_bias[0]
-
-    stream_low = both_cores(lax.ppermute(tower_in[0], ("dp", "mp"), out_moves))
-    cot_low = both_cores(lax.ppermute(out_cot[0], ("dp", "mp"), out_moves))
     stream = stream_low.astype(F32)
-    rows_dev = segment_ids.shape[0]
-    rows = rows_dev // 2
-    segs = jnp.where(core == group, segment_ids, swap_cores(segment_ids))
-    segs = lax.dynamic_slice_in_dim(segs, rows * side, rows, 0)
-    picks = jnp.where(core == group, row_image, swap_cores(row_image))
-    picks = lax.dynamic_slice_in_dim(picks, rows * side, rows, 0)
+    rows = segment_ids.shape[0] // 2
+    chosen = jnp.where(core == group, notes, other_notes)
+    chosen = lax.dynamic_slice_in_dim(chosen, rows * side, rows, 0)
+    segs = chosen[:, :LTXT]
+    picks = chosen[:, LTXT]
     seg_row = jnp.pad(jnp.concatenate([segs, segs], axis=1), ((0, 16 - rows), (0, 0)))
     seg_col = jnp.broadcast_to(segs.reshape(rows * LTXT, 1), (rows * LTXT, LANES))
 
@@ -939,16 +1188,21 @@
     )
     stream_one = stream + add_cores(dot_plain(mixed, w_out)) + out_bias[0]
 
-    def feed_in(values):
+    filled = gathered[3:]
+    if direct:
+        *filled, stream_one = lax.optimization_barrier((*filled, stream_one))
+        filled = gather_later(shards[3:], filled)
+    w_in = filled[0][0]
+    w_mlp = filled[1].reshape(hidden, width)
+
+    def feed_forward(values):
         act = norm_rows(values, gains[1], shifts[1]).astype(BF16)
         pre = jnp.concatenate([dot_plain(act, w_in[0]), dot_plain(act, w_in[1])], axis=1) + bias_in
-        return (act, pre, gelu_tanh(pre).astype(BF16))
-
-    def feed_out(hid):
-        return add_cores(dot_plain(hid, w_mlp)) + mlp_bias_out[0]
-
-    act_enc, pre_enc, hid_enc = feed_in(stream_one)
-    out_enc = stream_one + feed_out(hid_enc)
+        hid = gelu_tanh(pre).astype(BF16)
+        return (act, pre, hid, lowered(dot_plain(hid, w_mlp)))
+
+    act_enc, pre_enc, hid_enc, part_enc = only_image(feed_forward, stream_one)
+    out_enc = stream_one + add_lowered(part_enc) + mlp_bias_out[0]
     base_three = jnp.where(is_enc, out_enc, stream_one)
     act_three = norm_rows(base_three, gains[2], shifts[2]).astype(BF16)
 
@@ -964,8 +1218,8 @@
     cross_mix, cross_tops = cross_attend(cross_q, cross_k, cross_v, picks, scale_qk)
     stream_two = stream_one + add_cores(dot_plain(cross_mix, w_cross[3]))
 
-    act_dec, pre_dec, hid_dec = feed_in(stream_two)
-    out_dec = stream_two + feed_out(hid_dec)
+    act_dec, pre_dec, hid_dec, part_dec = feed_forward(stream_two)
+    out_dec = stream_two + add_lowered(part_dec) + mlp_bias_out[0]
     tower_out = own_rows(jnp.where(is_enc, out_enc, out_dec).astype(BF16))
     tower_out = lax.ppermute(tower_out, ("dp", "mp"), back_moves)
 
@@ -975,7 +1229,7 @@
         grad_pre = pullback(grad_hid)[0].astype(BF16)
         cols = hidden // 2
         part = dot_rows(grad_pre[:, :cols], w_in[0]) + dot_rows(grad_pre[:, cols:], w_in[1])
-        return (grad_pre, add_cores(part))
+        return (grad_pre, lowered(part))
 
     def feed_grads(grad_low, act, grad_pre, hid):
         g_in = dot_first(grad_pre, act).astype(BF16)
@@ -987,7 +1241,7 @@
 
     cot = cot_low.astype(F32)
     grad_pre_dec, back_in = feed_back(cot_low, pre_dec)
-    back_a, gain_a, shift_a = norm_back(stream_two, gains[1], back_in)
+    back_a, gain_a, shift_a = norm_back(stream_two, gains[1], add_lowered(back_in))
     grad_two = cot + back_a
     grad_two_low = grad_two.astype(BF16)
 
@@ -1006,37 +1260,47 @@
     keep = lax.dynamic_index_in_dim(pair_sum, side, 0, keepdims=False)
     got = lax.ppermute(give, "mp", [(i, i ^ 1) for i in range(depth)])
     image_sum = (keep.astype(F32) + got.astype(F32)).astype(BF16)
-    image_back = both_cores(lax.ppermute(image_sum, "tower", [(1, 0)])).astype(F32)
-    query_back = add_cores(dot_plain(grad_q, w_cross[2]))
-
+    image_half = lax.ppermute(image_sum, "tower", [(1, 0)])
+    later = lax.optimization_barrier(
+        (cot_low, act_dec, grad_pre_dec, hid_dec, flat_k, flat_v, grad_q, cross_mix, image_sum)
+    )
+    g_in_dec, g_mlp_dec = feed_grads(later[0], later[1], later[2], later[3])
     g_cross = jnp.concatenate(
         [
-            dot_first(flat_k, flat_images).astype(BF16),
-            dot_first(flat_v, flat_images).astype(BF16),
-            dot_first(grad_q, act_three).astype(BF16),
-            dot_first(cross_mix, grad_two_low).astype(BF16),
+            dot_first(later[4], flat_images).astype(BF16),
+            dot_first(later[5], flat_images).astype(BF16),
+            dot_first(later[6], act_three).astype(BF16),
+            dot_first(later[7], grad_two_low).astype(BF16),
         ],
         axis=0,
     ).reshape(4, 2, head_cols // 2, width)
+    text_grads = [g_in_dec, g_mlp_dec, g_cross]
+    if direct:
+        *text_grads, image_half = lax.optimization_barrier((*text_grads, image_half))
+        text_sums = reduce_grads(text_grads, [None] * 3, None, 1, 1)
+        image_half, *text_sums = lax.optimization_barrier((image_half, *text_sums))
+    else:
+        text_sums = reduce_plain(text_grads, None)
+    image_back = both_cores(image_half).astype(F32)
+    query_back = add_cores(dot_plain(grad_q, w_cross[2]))
 
     back_three, gain_three, shift_three = norm_back(
         base_three, gains[2], jnp.where(is_enc, image_back, query_back)
     )
     grad_enc = cot + back_three
     grad_enc_low = grad_enc.astype(BF16)
-    grad_pre_enc, back_in = feed_back(grad_enc_low, pre_enc)
-    back_b, gain_b, shift_b = norm_back(stream_one, gains[1], back_in)
+
+    def image_back_run(grad_low, pre, act, hid):
+        grad_pre, part = feed_back(grad_low, pre)
+        return (grad_pre, part) + feed_grads(grad_low, act, grad_pre, hid)
+
+    grad_pre_enc, back_in, g_in, g_mlp = only_image(image_back_run, grad_enc_low, pre_enc, act_enc, hid_enc)
+    back_b, gain_b, shift_b = norm_back(stream_one, gains[1], add_lowered(back_in))
     grad_one = jnp.where(is_enc, grad_enc + back_b, grad_two + back_three)
     grad_one_low = grad_one.astype(BF16)
 
     feed_low = jnp.where(is_enc, grad_enc_low, cot_low)
     feed_pre = jnp.where(is_enc, grad_pre_enc, grad_pre_dec)
-    g_in, g_mlp = feed_grads(
-        feed_low,
-        jnp.where(is_enc, act_enc, act_dec),
-        feed_pre,
-        jnp.where(is_enc, hid_enc, hid_dec),
-    )
 
     g_out = dot_first(mixed, grad_one_low).astype(BF16).reshape(1, 2, head_cols // 2, width)
     grad_mixed = dot_rows(grad_one_low, w_out).astype(BF16)
@@ -1075,20 +1339,23 @@
     lines_of = -(-used // (8 * LANES)) * 8
     smalls = jnp.pad(smalls, (0, lines_of * LANES - used)).reshape(lines_of, LANES)
 
-    grads = [g_qkv, g_out, g_in, g_mlp, g_cross]
-    flags = [None, None, None, None, 1]
+    grads = [g_in, g_mlp, g_out, g_qkv]
     if direct:
-        sums = reduce_grads(grads, flags, smalls, 1)
+        *sums, total = reduce_grads(grads, [0, 0, None, None], smalls, None, 2)
 
         def own_cols(x):
             cut = x.shape[2] // 2
             return jnp.where(core == 0, x[:, :, :cut], x[:, :, cut:])
 
-        *sums, total = sums
-        sums = [own_cols(s) for s in sums]
+        sums = [own_cols(x) for x in sums]
+        text_sums = [own_cols(x) for x in text_sums]
     else:
         *sums, total = reduce_plain(grads, smalls)
-    s_qkv, s_out, s_in, s_mlp, s_cross = sums
+    s_in, s_mlp, s_out, s_qkv = sums
+    s_in = jnp.where(is_enc, s_in, text_sums[0])
+    s_mlp = jnp.where(is_enc, s_mlp, text_sums[1])
+    s_cross = text_sums[2]
+    s_cross, s_qkv = lax.optimization_barrier((s_cross, s_qkv))
     from_text = lax.ppermute(s_cross[:2], "tower", [(1, 0)])
     s_cross = jnp.where(is_enc, from_text, s_cross[2:])
 

time: 613 us -> 571 us (0.931)
  Pallas kernels: 371 us -> 328 us
  waiting for transfers between devices: 66.5 us -> 43 us
  other arithmetic: 38.6 us -> 61.2 us
  local copies, waits for them, and re-layouts: 36 us -> 54 us
  matrix products: 61.8 us -> 51.8 us
  starting transfers between devices: 26.8 us -> 19.8 us
    pallas_call x1 -> x2, Pallas kernels: 217 us -> 148 us  [reduce_grads(): pl.pallas_call(functools.partial(reduce_kernel, tuple(pieces), tuple(flag...]
    pallas_call x0 -> x1, Pallas kernels: none -> 52.2 us  [gather_later(): pl.pallas_call(functools.partial(later_kernel, tuple(pieces), n_src, 1),...]
    pallas_call x1, Pallas kernels: 102 us -> 69.2 us  [gather_weights(): pl.pallas_call(functools.partial(gather_kernel, tuple(pieces), n_src), in...]
    ppermute x3 -> x1, waiting for transfers between devices: 23 us -> 0.01 us  [body(): image_half = lax.ppermute(image_sum, 'tower', [(1, 0)])]
    another operation x0 -> x10, local copies, waits for them, and re-layouts: none -> 13.8 us
    pallas_call x1, Pallas kernels: 19.4 us -> 27.9 us  [cross_attend_back(): pl.pallas_call(functools.partial(attend_back_kernel, 'cross', tokens // L...]
    ppermute x15 -> x11, starting transfers between devices: 11.6 us -> 3.38 us  [swap_cores(): return lax.ppermute(x, 'dp', [(i, i ^ 1) for i in range(devices)])]
    ppermute x15 -> x11, waiting for transfers between devices: 5.76 us -> 12.1 us  [swap_cores(): return lax.ppermute(x, 'dp', [(i, i ^ 1) for i in range(devices)])]
  transfers between devices with their start and end apart: 24 -> 18, of which waited for: 11 -> 9; matrix products, arithmetic and copies ran while one was open for 7% -> 11% of each run, Pallas kernels for 17% -> 17%
where the time goes in v2:
time: 571 us; the launch traced here: 560 us
  Pallas kernels  328 us (57%)
  other arithmetic  61.2 us (11%)
  local copies, waits for them, and re-layouts  54 us (9%)
  matrix products  51.8 us (9%)
  waiting for transfers between devices  43 us (8%)
  starting transfers between devices  19.8 us (3%)
    pallas_call x2, Pallas kernels, reduce_grads(): pl.pallas_call(functools.partial(reduce_kernel, tuple(pieces), tuple(flag...  148 us
    pallas_call x1, Pallas kernels, gather_weights(): pl.pallas_call(functools.partial(gather_kernel, tuple(pieces), n_src), in...  69.2 us
    pallas_call x1, Pallas kernels, gather_later(): pl.pallas_call(functools.partial(later_kernel, tuple(pieces), n_src, 1),...  52.2 us
    unnamed x179, local copies, waits for them, and re-layouts  30.8 us
    pallas_call x1, Pallas kernels, cross_attend_back(): pl.pallas_call(functools.partial(attend_back_kernel, 'cross', tokens // L...  27.9 us
    dot_general x9, matrix products, dot_rows(): lax.dot_general(left, right, (((1,), (1,)), ((), ())), preferred_element_...  18.2 us
    dot_general x9, matrix products, dot_plain(): lax.dot_general(left, right, (((1,), (0,)), ((), ())), preferred_element_...  17.7 us
    dot_general x8, matrix products, dot_first(): lax.dot_general(left, right, (((0,), (0,)), ((), ())), preferred_element_...  16 us
  transfers between devices with their start and end apart: 18, of which 9 were waited for; matrix products, arithmetic and copies ran while one was open for 11% of the time, Pallas kernels for 17%

profile of v2, /device:TPU:11, one launch (start us, length us, event | category | flops | bytes accessed | tf_op | source)
XLA Modules:
  0.0 560.2 jit_solution(773360413199529919)
XLA Ops:
  2.8 69.2 %gather_weights.1 = (bf16[3,2,192,768]{3,2,1,0:T(8,128)(2,1)}, bf16[1,2,192,768]{3,2,1,0:T(8,128)(2,1)}, bf16[4,2,192,768]{3,2,1,0:T(8,128)(2,1)}, bf16[1,2,768,...) custom-call(bf16[3,192,768]{2,1,0:T(8,128)(2,1)} %bitcast.222, ...), custom_call_target="tpu_custom_call" | custom-call | tf_op jit(solution)/shard_map/gather_weights/pallas_call | solution.py:703
  76.3 3.0 fusion.36
  79.5 9.0 %conditional.4 = ((bf16[576,384]{1,0:T(8,128)(2,1)}, f32[3,16,128]{2,1,0:T(8,128)S(1)})) conditional(s32[]{:T(128)} %convert_element_type.257, (bf16[576,1152]{1,0:T(8,128)(2,1)S(1)}, s32[576,128]{1,0:T(8,128)S(1)}, s32[16,128]{1,0:T(8,128)S(1)}) %tuple.53, bf16[576,1152]{1,0:T(8,128)(2,1)S(1)} %fusion.36), branch_computations={%region_2.3_spmd, %region_3.4_spmd} | conditional | flops 1019215872 | bytes 1769480 | solution.py:1183
  79.5 9.0 %attend_text.1 = (bf16[576,384]{1,0:T(8,128)(2,1)}, f32[3,16,128]{2,1,0:T(8,128)S(1)}) custom-call(bf16[576,1152]{1,0:T(8,128)(2,1)S(1)} %get-tuple-element.61.refs_0_.refs_1_.refs_2_, bf16[576,1152]{1,0:T(8,128)(2,1)S(1)} %get-tuple-element.61.refs_0_.refs_1_.refs_2_, bf16[576,1152]{1,0:T(8,128)(2,1)S(1)} %get-tuple-element.61.refs_0_.refs_1_.refs_2_, ...), custom_call_target="tpu_custom_call" | custom-call | flops 113246208 | bytes 1769472 | tf_op jit(solution)/shard_map/cond/branch_0_fun/attend_text/pallas_call | solution.py:208
  88.5 1.6 reduce-precision_convert_fusion.7
  91.1 1.7 collective-permute-done
  92.8 2.0 fusion.40
  94.8 52.2 %gather_later.1 = (bf16[1,2,768,768]{3,2,1,0:T(8,128)(2,1)}, bf16[1,2,768,768]{3,2,1,0:T(8,128)(2,1)}) custom-call(bf16[1,768,768]{2,1,0:T(8,128)(2,1)} %refs_0_.2, bf16[1,768,768]{2,1,0:T(8,128)(2,1)} %refs_1_.4, bf16[1,2,768,768]{3,2,1,0:T(8,128)(2,1)} %get-tuple-element.164.refs_2_, ...), custom_call_target="tpu_custom_call", output_to_operand_aliasing={{0}: (2, {}), {1}: (3, {})} | custom-call | tf_op jit(solution)/shard_map/gather_later/pallas_call | solution.py:729
  147.1 7.1 %conditional.5 = (bf16[576,768]{1,0:T(8,128)(2,1)}, f32[576,1536]{1,0:T(8,128)}, bf16[576,1536]{1,0:T(8,128)(2,1)}, bf16[576,768]{1,0:T(8,128)(2,1)}, f32[576,768]{1,0:T(8,128)}) conditional(s32[]{:T(128)} %convert_element_type.257, () %tuple.55, (f32[576,768]{1,0:T(8,128)S(1)}, f32[1,3,768]{2,0,1:T(1,128)S(1)}, f32[1,3,768]{2,0,1:T(1,128)S(1)}, ...), branch_computations={%region_4.5_spmd, %region_5.8_spmd} | conditional | flops 2732950016 | bytes 48447844 | solution.py:1147
  151.8 2.2 broadcast.208
  154.3 2.7 collective-permute-done.1
  157.0 3.1 fusion.82
  163.6 12.3 %collective-permute-done.2 = bf16[288,768]{1,0:T(8,128)(2,1)} collective-permute-done((bf16[288,768]{1,0:T(8,128)(2,1)S(1)}, bf16[288,768]{1,0:T(8,128)(2,1)}, u32[]{:S(2)}, u32[]{:S(2)}) %collective-permute-start.2) | collective-permute-done | bytes 442400 | tf_op jit(solution)/shard_map/ppermute | solution.py:1209
  175.9 5.7 %collective-permute-start.3 = (bf16[288,768]{1,0:T(8,128)(2,1)}, bf16[288,768]{1,0:T(8,128)(2,1)}, u32[]{:S(2)}, u32[]{:S(2)}) collective-permute-start(bf16[288,768]{1,0:T(8,128)(2,1)} %collective-permute-done.2), channel_id=1, source_target_pairs={{0,1},{1,0},{2,3},{3,2},{4,5},{5,4},{6,7},{7,6},{8,9},{9,8},{10,11... | collective-permute-start | bytes 1327112 | tf_op jit(solution)/shard_map/ppermute | solution.py:1210
  181.6 9.9 %collective-permute-done.3 = bf16[288,768]{1,0:T(8,128)(2,1)} collective-permute-done((bf16[288,768]{1,0:T(8,128)(2,1)}, bf16[288,768]{1,0:T(8,128)(2,1)}, u32[]{:S(2)}, u32[]{:S(2)}) %collective-permute-start.3) | collective-permute-done | bytes 442400 | tf_op jit(solution)/shard_map/ppermute | solution.py:1210
  191.5 2.5 maximum_select_fusion.1
  196.2 2.6 fusion.87
  200.3 2.4 maximum_select_fusion
  202.7 2.0 convolution_convert_fusion.5
  204.8 2.0 convolution_convert_fusion.6
  206.8 9.5 %attend_cross.1 = (bf16[576,384]{1,0:T(8,128)(2,1)}, f32[3,16,128]{2,1,0:T(8,128)}) custom-call(s32[9]{0:T(128)} %slice_reduce_fusion.2.refs_0_, bf16[576,384]{1,0:T(8,128)(2,1)} %convolution_convert_fusion.14.refs_1_, bf16[2,576,384]{2,1,0:T(8,128)(2,1)} %bitcast.244, bf16[2,576,384]{2,1,0:T(8,128)(2,1)} %bitcast.242), custom_call_target="tpu_custom_call" | custom-call | flops 1019215872 | bytes 1769472 | tf_op jit(solution)/shard_map/attend_cross/pallas_call | solution.py:259
  216.3 1.8 reduce-precision_convert_fusion.6
  218.2 2.4 collective-permute-done.5
  226.5 5.0 fusion.34
  232.7 1.8 reduce-precision_convert_fusion.4
  234.6 2.6 collective-permute-done.8
  237.3 3.6 multiply_reduce_fusion.2
  240.8 2.2 convert_add_fusion.2
  245.7 27.9 %attend_back_cross.1 = (bf16[576,384]{1,0:T(8,128)(2,1)}, bf16[2,576,384]{2,1,0:T(8,128)(2,1)}, bf16[2,576,384]{2,1,0:T(8,128)(2,1)}) custom-call(s32[9]{0:T(128)} %slice_reduce_fusion.2.refs_0_, bf16[576,384]{1,0:T(8,128)(2,1)} %convolution_convert_fusion.14.refs_1_, bf16[2,576,384]{2,1,0:T(8,128)(2,1)} %bitcast.245, bf16[2,576,384]{2,1,0:T(8,128)(2,1)} %bitcast.243, ...), custom_call_target="tpu_custom_call" | custom-call | flops 2548039680 | bytes 1769472 | tf_op jit(solution)/shard_map/attend_back_cross/pallas_call | solution.py:289
  273.7 2.5 fusion.88
  279.6 2.6 collective-permute-done.9
  282.2 1.6 fusion.41
  285.5 4.0 reduce-precision_convert_fusion.5
  291.6 4.1 collective-permute-done.10
  302.2 3.5 convolution_convert_fusion.4
  305.7 1.6 pad_maximum_fusion
  308.3 3.4 convolution_convert_fusion.3
  311.8 95.6 %reduce_grads_1.1 = (bf16[1,768,384]{2,1,0:T(8,128)(2,1)}, bf16[1,768,384]{2,1,0:T(8,128)(2,1)}, bf16[4,192,384]{2,1,0:T(8,128)(2,1)}) custom-call(bf16[1,2,768,768]{3,2,1,0:T(8,128)(2,1)} %bitcast.216, bf16[1,2,768,768]{3,2,1,0:T(8,128)(2,1)} %bitcast.217, bf16[4,2,192,768]{3,2,1,0:T(8,128)(2,1)} %bitcast.199), custom_call_target="tpu_custom_call" | custom-call | tf_op jit(solution)/shard_map/reduce_grads_1/pallas_call | solution.py:1038
  407.6 2.6 fusion.64
  410.2 2.0 collective-permute-start.7
  412.3 3.2 multiply_reduce_fusion.1
  418.6 7.1 %conditional.6 = (bf16[576,1536]{1,0:T(8,128)(2,1)}, bf16[576,768]{1,0:T(8,128)(2,1)}, bf16[1,2,768,768]{3,2,1,0:T(8,128)(2,1)}, bf16[1,2,768,768]{3,2,1,0:T(8,128)(2,1)}, f32[576,768]{1,0:T(8,128)}) conditional(s32[]{:T(128)} %convert_element_type.257, () %tuple.60, (bf16[576,768]{1,0:T(8,128)(2,1)S(1)}, bf16[1536,768]{1,0:T(8,128)(2,1)S(1)}, ...), branch_computations={%region_16.17_spmd, %region_17.18_spmd} | conditional | flops 5457641472 | bytes 28901416 | solution.py:1147
  426.7 2.0 slice_select_fusion
  428.8 2.7 convert_reduce_fusion.2
  431.5 3.4 multiply_reduce_fusion.3
  434.9 3.0 convert_reduce_fusion.5
  439.2 13.3 %conditional.7 = (bf16[576,1152]{1,0:T(8,128)(2,1)}, f32[384]{0:T(512)S(1)}, f32[384]{0:T(512)S(1)}) conditional(s32[]{:T(128)} %convert_element_type.257, (bf16[576,1152]{1,0:T(8,128)(2,1)S(1)}, bf16[576,384]{1,0:T(8,128)(2,1)S(1)}, f32[3,16,128]{2,1,0:T(8,128)S(1)}, s32[576,128]{1,0:T(8,128)S(1)}, s32[16,128]{1,0:T(8,128)S(1)}) %tuple.62, ...), branch_computations={%region_22.24_spmd, %region_24.26_spmd} | conditional | flops 2549365760 | bytes 3107352 | solution.py:1307
  439.2 11.7 %attend_back_text.2 = bf16[576,1152]{1,0:T(8,128)(2,1)} custom-call(bf16[576,1152]{1,0:T(8,128)(2,1)S(1)} %get-tuple-element.76.refs_0_.refs_1_.refs_2_, bf16[576,1152]{1,0:T(8,128)(2,1)S(1)} %get-tuple-element.76.refs_0_.refs_1_.refs_2_, bf16[576,1152]{1,0:T(8,128)(2,1)S(1)} %get-tuple-element.76.refs_0_.refs_1_.refs_2_, ...), custom_call_target="tpu_custom_call" | custom-call | flops 283115520 | bytes 1769472 | tf_op jit(solution)/shard_map/cond/branch_0_fun/attend_back_text/pallas_call | solution.py:232
  452.5 3.3 reduce-precision_convert_fusion.2
  460.3 4.3 convolution_convert_fusion.2
  464.6 2.7 fusion.44
  468.2 52.5 %reduce_grads_2.1 = (bf16[1,768,384]{2,1,0:T(8,128)(2,1)}, bf16[1,768,384]{2,1,0:T(8,128)(2,1)}, bf16[1,192,384]{2,1,0:T(8,128)(2,1)}, bf16[3,192,384]{2,1,0:T(8,128)(2,1)}, f32[2,72,128]{2,1,0:T(8,128)}) custom-call(bf16[1,2,768,768]{3,2,1,0:T(8,128)(2,1)} %get-tuple-element.201.refs_0_, bf16[1,2,768,768]{3,2,1,0:T(8,128)(2,1)} %get-tuple-element.202.refs_1_, ...), custom_call_target="tpu_custom_call" | custom-call | tf_op jit(solution)/shard_map/reduce_grads_2/pallas_call | solution.py:1038
  520.8 2.0 slice_select_fusion.1
  528.4 1.7 select_convert_fusion.1
  530.2 2.8 convert_bitcast_fusion
  533.0 2.2 copy.42
  535.2 2.0 collective-permute-start.17
  537.2 1.8 convert_bitcast_fusion.1
  539.0 2.1 copy.41
  541.1 2.2 fusion.59
  543.4 2.6 collective-permute-start.16
  547.9 2.2 copy.43
  552.7 4.5 collective-permute-done.16
  557.2 1.8 copy.115
  (284 shorter events, 73.5 us)
Async XLA Ops:
  0.6 89.6 %copy-start = (f32[1,3072]{1,0:T(1,128)S(1)}, f32[1,3072]{1,0:T(1,128)}, u32[]{:S(2)}) copy-start(f32[1,3072]{1,0:T(1,128)} %param.34) | copy-start | bytes 36868
  2.8 69.2 %copy-start.57 = (s32[18,64]{1,0:T(8,128)S(1)}, s32[18,64]{1,0:T(8,128)}, u32[]{:S(2)}) copy-start(s32[18,64]{1,0:T(8,128)} %param.25) | copy-start | bytes 13828
  2.8 70.3 %copy-start.60 = (f32[1,3,768]{2,0,1:T(1,128)S(1)}, f32[1,3,768]{2,0,1:T(1,128)}, u32[]{:S(2)}) copy-start(f32[1,3,768]{2,0,1:T(1,128)} %param.36) | copy-start | bytes 27652
  2.8 70.3 %copy-start.59 = (f32[1,3,768]{2,0,1:T(1,128)S(1)}, f32[1,3,768]{2,0,1:T(1,128)}, u32[]{:S(2)}) copy-start(f32[1,3,768]{2,0,1:T(1,128)} %param.37) | copy-start | bytes 27652
  72.0 4.1 copy-start.77
  72.0 4.2 copy-start.16
  73.1 387.1 %copy-start.70 = (f32[768]{0:T(1024)}, f32[768]{0:T(1024)S(1)}, u32[]{:S(2)}) copy-start(f32[768]{0:T(1024)S(1)} %get-tuple-element.270) | copy-start | bytes 9220
  76.1 384.1 %copy-start.62 = (f32[576]{0:T(1024)}, f32[576]{0:T(1024)S(1)}, u32[]{:S(2)}) copy-start(f32[576]{0:T(1024)S(1)} %add_rsqrt_fusion.4) | copy-start | bytes 6916
  79.5 9.0 %copy-start.52 = (bf16[1,2,192,768]{3,2,1,0:T(8,128)(2,1)S(1)}, bf16[1,2,192,768]{3,2,1,0:T(8,128)(2,1)}, u32[]{:S(2)}) copy-start(bf16[1,2,192,768]{3,2,1,0:T(8,128)(2,1)} %get-tuple-element.162) | copy-start | bytes 1769476
  90.1 2.6 collective-permute-start
  147.0 7.3 %copy-start.76 = (f32[1,768]{1,0:T(1,128)S(1)}, f32[1,768]{1,0:T(1,128)}, u32[]{:S(2)}) copy-start(f32[1,768]{1,0:T(1,128)} %param.35) | copy-start | bytes 9220
  154.2 2.8 collective-permute-start.1
  162.3 13.6 %collective-permute-start.2 = (bf16[288,768]{1,0:T(8,128)(2,1)S(1)}, bf16[288,768]{1,0:T(8,128)(2,1)}, u32[]{:S(2)}, u32[]{:S(2)}) collective-permute-start(bf16[288,768]{1,0:T(8,128)(2,1)S(1)} %constant_dynamic-slice_fusion.1), channel_id=1, source_target_pairs={{0,16},{1,17},{2,18},{3,19},{4,20},{5,21},{6,22},{7,23},{8,24},{9,... | collective-permute-start | bytes 1327112 | tf_op jit(solution)/shard_map/ppermute | solution.py:1209
  175.9 15.6 %collective-permute-start.3 = (bf16[288,768]{1,0:T(8,128)(2,1)}, bf16[288,768]{1,0:T(8,128)(2,1)}, u32[]{:S(2)}, u32[]{:S(2)}) collective-permute-start(bf16[288,768]{1,0:T(8,128)(2,1)} %collective-permute-done.2), channel_id=1, source_target_pairs={{0,1},{1,0},{2,3},{3,2},{4,5},{5,4},{6,7},{7,6},{8,9},{9,8},{10,11... | collective-permute-start | bytes 1327112 | tf_op jit(solution)/shard_map/ppermute | solution.py:1210
  194.0 6.3 %collective-permute-start.4 = (bf16[2,288,768]{2,1,0:T(8,128)(2,1)}, bf16[2,288,768]{2,1,0:T(8,128)(2,1)}, u32[]{:S(2)}, u32[]{:S(2)}) collective-permute-start(bf16[2,288,768]{2,1,0:T(8,128)(2,1)} %maximum_select_fusion.1), channel_id=1, source_target_pairs={{0,4},{4,0},{8,12},{12,8},{1,5},{5,1},{9,13},{13,9},{2,6},{6,2},{1... | collective-permute-start | bytes 2654216 | tf_op jit(solution)/shard_map/ppermute | solution.py:1125
  198.9 3.8 copy-start.30
  198.9 5.9 %copy-start.32 = (bf16[1,2,192,768]{3,2,1,0:T(8,128)(2,1)}, bf16[1,2,192,768]{3,2,1,0:T(8,128)(2,1)S(1)}, u32[]{:S(2)}) copy-start(bf16[1,2,192,768]{3,2,1,0:T(8,128)(2,1)S(1)} %get-tuple-element.307) | copy-start | bytes 1769476
  218.1 2.5 collective-permute-start.5
  234.5 2.8 collective-permute-start.8
  234.6 6.2 %copy-start.6 = (f32[576,768]{1,0:T(8,128)S(1)}, f32[576,768]{1,0:T(8,128)}, u32[]{:S(2)}) copy-start(f32[576,768]{1,0:T(8,128)} %copy-done.5) | copy-start | bytes 5308420
  234.6 6.2 %copy-start.19 = (bf16[576,768]{1,0:T(8,128)(2,1)S(1)}, bf16[576,768]{1,0:T(8,128)(2,1)}, u32[]{:S(2)}) copy-start(bf16[576,768]{1,0:T(8,128)(2,1)} %get-tuple-element.180) | copy-start | bytes 2654212
  240.8 3.5 copy-start.37
  279.5 2.8 collective-permute-start.9
  279.6 5.9 %copy-start.34 = (bf16[1,2,768,768]{3,2,1,0:T(8,128)(2,1)S(1)}, bf16[1,2,768,768]{3,2,1,0:T(8,128)(2,1)}, u32[]{:S(2)}) copy-start(bf16[1,2,768,768]{3,2,1,0:T(8,128)(2,1)} %get-tuple-element.167) | copy-start | bytes 7077892
  283.9 11.7 %collective-permute-start.10 = (bf16[288,768]{1,0:T(8,128)(2,1)S(1)}, bf16[288,768]{1,0:T(8,128)(2,1)S(1)}, u32[]{:S(2)}, u32[]{:S(2)}) collective-permute-start(bf16[288,768]{1,0:T(8,128)(2,1)S(1)} %dynamic-slice_bitcast_fusion.1), channel_id=1, source_target_pairs={{0,1},{1,0},{2,3},{3,2},{4,5},{5,4},{6,7},{7,6},{8,9},{9,8},{10,11... | collective-permute-start | bytes 1327112 | tf_op jit(solution)/shard_map/ppermute | solution.py:1261
  285.5 4.5 copy-start.51
  285.5 4.5 copy-start.78
  289.5 7.6 %copy-start.40 = (bf16[576,768]{1,0:T(8,128)(2,1)S(1)}, bf16[576,768]{1,0:T(8,128)(2,1)}, u32[]{:S(2)}) copy-start(bf16[576,768]{1,0:T(8,128)(2,1)} %copy-done.38) | copy-start | bytes 2654212
  289.5 118.0 %collective-permute-start.6 = (bf16[576,768]{1,0:T(8,128)(2,1)}, bf16[576,768]{1,0:T(8,128)(2,1)}, u32[]{:S(2)}, u32[]{:S(2)}) collective-permute-start(bf16[576,768]{1,0:T(8,128)(2,1)} %reduce-precision_convert_fusion.5), channel_id=1, source_target_pairs={{0,4},{4,0},{8,12},{12,8},{1,5},{5,1},{9,13},{13,9},{2,6},{6,2},{1... | collective-permute-start | bytes 2654216 | tf_op jit(solution)/shard_map/ppermute | solution.py:1125
  291.5 6.3 %copy-start.13 = (bf16[2,576,768]{2,1,0:T(8,128)(2,1)S(1)}, bf16[2,576,768]{2,1,0:T(8,128)(2,1)}, u32[]{:S(2)}) copy-start(bf16[2,576,768]{2,1,0:T(8,128)(2,1)} %copy-done.12) | copy-start | bytes 5308420
  291.5 6.3 %copy-start.24 = (bf16[2,576,384]{2,1,0:T(8,128)(2,1)S(1)}, bf16[2,576,384]{2,1,0:T(8,128)(2,1)}, u32[]{:S(2)}) copy-start(bf16[2,576,384]{2,1,0:T(8,128)(2,1)} %get-tuple-element.174) | copy-start | bytes 2654212
  291.5 120.8 %collective-permute-start.13 = (bf16[576,768]{1,0:T(8,128)(2,1)}, bf16[576,768]{1,0:T(8,128)(2,1)}, u32[]{:S(2)}, u32[]{:S(2)}) collective-permute-start(bf16[576,768]{1,0:T(8,128)(2,1)} %reduce-precision_convert_fusion.3), channel_id=1, source_target_pairs={{0,4},{4,0},{8,12},{12,8},{1,5},{5,1},{9,13},{13,9},{2,6},{6,2},{1... | collective-permute-start | bytes 2654216 | tf_op jit(solution)/shard_map/ppermute | solution.py:1125
  295.8 16.0 %collective-permute-start.11 = (bf16[288,768]{1,0:T(8,128)(2,1)S(1)}, bf16[288,768]{1,0:T(8,128)(2,1)S(1)}, u32[]{:S(2)}, u32[]{:S(2)}) collective-permute-start(bf16[288,768]{1,0:T(8,128)(2,1)S(1)} %fusion.66), channel_id=1, source_target_pairs={{16,0},{17,1},{18,2},{19,3},{20,4},{21,5},{22,6},{23,7},{24,8},{25... | collective-permute-start | bytes 1327112 | tf_op jit(solution)/shard_map/ppermute | solution.py:1263
  407.3 4.9 copy-start.3
  407.3 4.9 collective-permute-start.12
  410.2 5.3 copy-start.21
  410.2 16.5 %collective-permute-start.7 = (bf16[288,768]{1,0:T(8,128)(2,1)}, bf16[288,768]{1,0:T(8,128)(2,1)}, u32[]{:S(2)}, u32[]{:S(2)}) collective-permute-start(bf16[288,768]{1,0:T(8,128)(2,1)} %fusion.64), channel_id=1, source_target_pairs={{0,0},{4,1},{1,2},{5,3},{2,4},{6,5},{3,6},{7,7},{8,8},{12,9},{9,10... | collective-permute-start | bytes 1327112 | tf_op jit(solution)/shard_map/ppermute | solution.py:1224
  415.5 3.0 copy-start.35
  425.7 5.8 %collective-permute-start.14 = (bf16[576,768]{1,0:T(8,128)(2,1)}, bf16[576,768]{1,0:T(8,128)(2,1)}, u32[]{:S(2)}, u32[]{:S(2)}) collective-permute-start(bf16[576,768]{1,0:T(8,128)(2,1)} %get-tuple-element.197), channel_id=1, source_target_pairs={{0,4},{4,0},{8,12},{12,8},{1,5},{5,1},{9,13},{13,9},{2,6},{6,2},{1... | collective-permute-start | bytes 2654216 | tf_op jit(solution)/shard_map/ppermute | solution.py:1125
  428.8 6.1 %copy-start.15 = (f32[576,768]{1,0:T(8,128)S(1)}, f32[576,768]{1,0:T(8,128)}, u32[]{:S(2)}) copy-start(f32[576,768]{1,0:T(8,128)} %copy-done.14) | copy-start | bytes 5308420
  431.5 3.4 copy-start.4
  431.5 3.4 copy-start.9
  431.5 3.4 copy-start.22
  434.9 3.1 copy-start.53
  452.5 3.4 copy-start.71
  452.5 3.4 copy-start.73
  452.5 6.3 %copy-start.11 = (f32[576,768]{1,0:T(8,128)S(1)}, f32[576,768]{1,0:T(8,128)}, u32[]{:S(2)}) copy-start(f32[576,768]{1,0:T(8,128)} %copy-done.10) | copy-start | bytes 5308420
  452.5 6.3 %copy-start.55 = (bf16[576,384]{1,0:T(8,128)(2,1)S(1)}, bf16[576,384]{1,0:T(8,128)(2,1)}, u32[]{:S(2)}) copy-start(bf16[576,384]{1,0:T(8,128)(2,1)} %get-tuple-element.161) | copy-start | bytes 1327108
  455.9 4.4 copy-start.17
  455.9 8.8 %collective-permute-start.15 = (bf16[576,768]{1,0:T(8,128)(2,1)S(1)}, bf16[576,768]{1,0:T(8,128)(2,1)S(1)}, u32[]{:S(2)}, u32[]{:S(2)}) collective-permute-start(bf16[576,768]{1,0:T(8,128)(2,1)S(1)} %reduce-precision_convert_fusion.2), channel_id=1, source_target_pairs={{0,4},{4,0},{8,12},{12,8},{1,5},{5,1},{9,13},{13,9},{2,6},{6,2},{1... | collective-permute-start | bytes 2654216 | tf_op jit(solution)/shard_map/ppermute | solution.py:1125
  464.6 2.9 copy-start.63
  464.6 2.9 copy-start.68
  464.6 2.9 copy-start.74
  464.6 2.9 copy-start.72
  464.6 2.9 copy-start.61
  468.2 59.5 %copy-start.43 = (bf16[4,192,192]{2,1,0:T(8,128)(2,1)S(1)}, bf16[4,192,192]{2,1,0:T(8,128)(2,1)}, u32[]{:S(2)}) copy-start(bf16[4,192,192]{2,1,0:T(8,128)(2,1)} %slice_select_fusion) | copy-start | bytes 884740
  520.7 9.4 %copy-start.44 = (bf16[1,768,384]{2,1,0:T(8,128)(2,1)S(1)}, bf16[1,768,384]{2,1,0:T(8,128)(2,1)}, u32[]{:S(2)}) copy-start(bf16[1,768,384]{2,1,0:T(8,128)(2,1)} %get-tuple-element.210) | copy-start | bytes 1769476
  520.7 9.4 %copy-start.45 = (bf16[1,768,384]{2,1,0:T(8,128)(2,1)S(1)}, bf16[1,768,384]{2,1,0:T(8,128)(2,1)}, u32[]{:S(2)}) copy-start(bf16[1,768,384]{2,1,0:T(8,128)(2,1)} %get-tuple-element.212) | copy-start | bytes 1769476
  520.7 9.4 %copy-start.46 = (bf16[1,768,384]{2,1,0:T(8,128)(2,1)S(1)}, bf16[1,768,384]{2,1,0:T(8,128)(2,1)}, u32[]{:S(2)}) copy-start(bf16[1,768,384]{2,1,0:T(8,128)(2,1)} %get-tuple-element.209) | copy-start | bytes 1769476
  527.7 5.3 copy-start.56
  535.2 15.5 %collective-permute-start.17 = (bf16[2,192,192]{2,1,0:T(8,128)(2,1)}, bf16[2,192,192]{2,1,0:T(8,128)(2,1)}, u32[]{:S(2)}, u32[]{:S(2)}) collective-permute-start(bf16[2,192,192]{2,1,0:T(8,128)(2,1)} %slice.263), channel_id=1, source_target_pairs={{16,0},{17,1},{18,2},{19,3},{20,4},{21,5},{22,6},{23,7},{24,8},{25... | collective-permute-start | bytes 442376 | tf_op jit(solution)/shard_map/ppermute | solution.py:1359
  541.1 4.9 copy-start.65
  543.4 13.9 %collective-permute-start.16 = (bf16[288,768]{1,0:T(8,128)(2,1)}, bf16[288,768]{1,0:T(8,128)(2,1)S(1)}, u32[]{:S(2)}, u32[]{:S(2)}) collective-permute-start(bf16[288,768]{1,0:T(8,128)(2,1)} %fusion.59), channel_id=1, source_target_pairs={{0,0},{4,1},{1,2},{5,3},{2,4},{6,5},{3,6},{7,7},{8,8},{12,9},{9,10... | collective-permute-start | bytes 1327112 | tf_op jit(solution)/shard_map/ppermute | solution.py:1319
  550.7 9.1 %copy-start.1 = (f32[1,3072]{1,0:T(1,128)S(1)}, f32[1,3072]{1,0:T(1,128)}, u32[]{:S(2)}) copy-start(f32[1,3072]{1,0:T(1,128)} %param.34) | copy-start | bytes 36868
  (32 other events, 57.5 us)
